TPU v7x, 256 devices: a whole 4x4x8 slice. The times are simulated.
256 devices in a mesh: kpt: 8 (over y, x_hi), row: 4 (over x_lo, core), col: 8 (over z).
Axes of the slice: x: 4 (x_hi: 2, x_lo: 2; x = x_hi * 2 + x_lo), y: 4, z: 8, core: 2. Of those that a mesh axis runs over, the one named last changes fastest.
Arguments:
- left_blocks: bfloat16 [32, 64, 2, 2, 128, 128], P(('kpt', 'row'), 'col'), parts along dimension 0, may hold values from -0.5 to 0.5
- left_rows: int32 [32, 64, 2], P(('kpt', 'row'), 'col'), parts along dimension 0, may hold values from 0 to 7, as said below
- left_count: int32 [32, 64], P(('kpt', 'row'), 'col'), parts along dimension 0, may hold values from 1 to 2, as said below
- left_level: int32 [32, 64, 2], P(('kpt', 'row'), 'col'), parts along dimension 0, may hold values from 0 to 7
- right_blocks: bfloat16 [16, 32, 8, 2, 2, 128, 128], P('kpt', 'row', 'col'), parts along dimension 0, may hold values from -6 to 6
- right_cols: int32 [16, 32, 8, 2], P('kpt', 'row', 'col'), parts along dimension 0, may hold values from 0 to 7, as said below
- right_count: int32 [16, 32, 8], P('kpt', 'row', 'col'), parts along dimension 0, may hold values from 1 to 2, as said below
- right_level: int32 [16, 32, 8, 2], P('kpt', 'row', 'col'), parts along dimension 0, may hold values from 0 to 7
Outputs:
- product_blocks: bfloat16 [256, 64, 2, 128, 128], P(('kpt', 'row'), 'col'), parts along dimension 0
There are 8 independent parts, one for each index of `kpt`. A program takes and returns all parts, laid end to end along the dimension named above; each array names one. Nothing has to cross between parts.
Inputs may be any that keep to these rules, and one draw needn't show every extreme that they name: `left_rows`: the 2 slots of one row group and block column name distinct block rows. `left_count`: in every row group some block column has all 2 slots live. `right_cols`: the 2 slots of one block row and column group name distinct block columns. `right_count`: in every column group some block row has all 2 slots live.
All inputs are finite; a program needn't handle non-finite values.
Results may differ from a plain program's by a relative error of at most 0.001.
Values may be sent and summed in bfloat16 or wider, within the bound.
No kernel may reach another device: no remote copies, remote signals or barrier semaphores. Data moves between devices by JAX's collectives and lax.ppermute only.
A program may use at most 192 MiB of HBM per device.

v0:
```python
import jax
import jax.numpy as jnp
from jax import lax
from jax.sharding import PartitionSpec as P

GR = 8
LEVEL_CUT = 7


def shortened(value):

    def short(part):
        return part.astype(jnp.bfloat16) if part.dtype == jnp.float32 else part

    return jax.tree.map(short, value)


def passed_along(value, axis, steps):
    count = lax.axis_size(axis)
    pairs = [(source, (source + steps) % count) for source in range(count)]
    return lax.ppermute(value, axis, pairs)


def pair_products(left_pack, right_pack, total):
    left_blocks, left_rows, left_count, left_level = left_pack
    right_blocks, right_cols, right_count, right_level = right_pack
    slots_left = left_rows.shape[1]
    slots_right = right_cols.shape[1]
    live_left = jnp.arange(slots_left, dtype=jnp.int32)[None, :] < left_count[:, None]
    live_right = jnp.arange(slots_right, dtype=jnp.int32)[None, :] < right_count[:, None]
    kept = live_left[:, :, None] & live_right[:, None, :]
    kept = kept & (left_level[:, :, None] + right_level[:, None, :] >= LEVEL_CUT)
    terms = jnp.einsum(
        "kmcij,kndjl->kmncdil", left_blocks, right_blocks, preferred_element_type=jnp.float32
    )
    real_part = terms[:, :, :, 0, 0] - terms[:, :, :, 1, 1]
    imag_part = terms[:, :, :, 0, 1] + terms[:, :, :, 1, 0]
    product = jnp.stack([real_part, imag_part], axis=3) * kept[:, :, :, None, None, None].astype(
        jnp.float32
    )
    row_index = jnp.broadcast_to(left_rows[:, :, None], kept.shape).reshape(-1)
    col_index = jnp.broadcast_to(right_cols[:, None, :], kept.shape).reshape(-1)
    width = left_blocks.shape[-1]
    return total.at[row_index, col_index].add(product.reshape(-1, 2, width, width))


def choose(flag, fresh, stale):
    return jax.tree.map(lambda newer, older: jnp.where(flag, newer, older), fresh, stale)


def pick_slot(pack, slot):
    return jax.tree.map(
        lambda member: lax.dynamic_index_in_dim(member, slot, 0, keepdims=False), pack
    )


def body(
    left_blocks,
    left_rows,
    left_count,
    left_level,
    right_blocks,
    right_cols,
    right_count,
    right_level,
):
    left_pack = (left_blocks[0], left_rows[0], left_count[0], left_level[0])
    right_pack = (
        right_blocks[:, :, 0],
        right_cols[:, :, 0],
        right_count[:, :, 0],
        right_level[:, :, 0],
    )
    grid_rows = lax.axis_size("row")
    grid_cols = lax.axis_size("col")
    own_row = lax.axis_index("row")
    own_col = lax.axis_index("col")
    width = left_blocks.shape[-1]
    panel_rows = left_blocks.shape[1]
    total = jnp.zeros((GR, panel_rows, 2, width, width), jnp.float32)
    offset = own_col % grid_rows
    for power in range((grid_rows - 1).bit_length()):
        moved = jax.tree.map(
            lambda part, own: part.astype(own.dtype),
            passed_along(shortened(left_pack), "col", -(1 << power)),
            left_pack,
        )
        left_pack = choose((own_row >> power) % 2 == 1, moved, left_pack)
        arrived = jax.tree.map(
            lambda part, own: part.astype(own.dtype),
            passed_along(shortened(right_pack), "row", -(1 << power)),
            right_pack,
        )
        right_pack = choose((offset >> power) % 2 == 1, arrived, right_pack)

    def turn(step, carry):
        left_now, right_now, running = carry
        panel = (own_row + own_col + step) % grid_cols
        running = pair_products(left_now, pick_slot(right_now, panel // grid_rows), running)
        left_now = jax.tree.map(
            lambda part, own: part.astype(own.dtype),
            passed_along(shortened(left_now), "col", -1),
            left_now,
        )
        right_now = jax.tree.map(
            lambda part, own: part.astype(own.dtype),
            passed_along(shortened(right_now), "row", -1),
            right_now,
        )
        return (left_now, right_now, running)

    left_pack, right_pack, total = lax.fori_loop(
        0, grid_cols - 1, turn, (left_pack, right_pack, total)
    )
    panel = (own_row + own_col + grid_cols - 1) % grid_cols
    total = pair_products(left_pack, pick_slot(right_pack, panel // grid_rows), total)
    return total.astype(jnp.bfloat16)


def solution(mesh):
    in_specs = (
        P(("kpt", "row"), "col", None, None, None, None),
        P(("kpt", "row"), "col", None),
        P(("kpt", "row"), "col"),
        P(("kpt", "row"), "col", None),
        P("kpt", "row", "col", None, None, None, None),
        P("kpt", "row", "col", None),
        P("kpt", "row", "col"),
        P("kpt", "row", "col", None),
    )
    out_specs = P(("kpt", "row"), "col", None, None, None)
    return jax.shard_map(body, mesh=mesh, in_specs=in_specs, out_specs=out_specs, check_vma=False)
```

profile of v0, /device:TPU:1, one launch (start us, length us, event | category | flops | bytes accessed | tf_op | source)
XLA Modules:
  0.0 408.7 jit_solution(11240274125978105502)
XLA Ops:
  0.1 3.1 copy.33
  3.2 3.3 collective-permute-start.16
  6.7 5.3 %collective-permute-start.10 = (s32[8,2]{0,1:T(2,128)S(1)}, s32[8,2]{0,1:T(2,128)S(1)}, u32[]{:S(2)}, u32[]{:S(2)}) collective-permute-start(s32[8,2]{0,1:T(2,128)S(1)} %bitcast.87), channel_id=1, source_target_pairs={{0,7},{1,0},{2,1},{3,2},{4,3},{5,4},{6,5},{7,6},{8,15},{9,8},{10,9... | collective-permute-start | bytes 200 | tf_op jit(solution)/shard_map/ppermute | solution.py:21
  20.0 10.0 %collective-permute-done.20 = s32[2,8]{1,0:T(2,128)S(1)} collective-permute-done((s32[2,8]{1,0:T(2,128)S(1)}, s32[2,8]{1,0:T(2,128)S(1)}, u32[]{:S(2)}, u32[]{:S(2)}) %collective-permute-start.20) | collective-permute-done | bytes 96 | tf_op jit(solution)/shard_map/ppermute | solution.py:21
  30.0 6.0 %collective-permute-start.13 = (s32[8]{0:T(128)S(1)}, s32[8]{0:T(128)S(1)}, u32[]{:S(2)}, u32[]{:S(2)}) collective-permute-start(s32[8]{0:T(128)S(1)} %broadcast_select_fusion.10), channel_id=1, source_target_pairs={{0,6},{1,7},{2,0},{3,1},{4,2},{5,3},{6,4},{7,5},{8,14},{9,15},{10,... | collective-permute-start | bytes 104 | tf_op jit(solution)/shard_map/ppermute | solution.py:21
  36.0 4.9 %collective-permute-done.13 = s32[8]{0:T(128)S(1)} collective-permute-done((s32[8]{0:T(128)S(1)}, s32[8]{0:T(128)S(1)}, u32[]{:S(2)}, u32[]{:S(2)}) %collective-permute-start.13) | collective-permute-done | bytes 64 | tf_op jit(solution)/shard_map/ppermute | solution.py:21
  40.9 3.0 collective-permute-start.11
  52.1 36.9 %collective-permute-done.21 = s32[2,8]{1,0:T(2,128)S(1)} collective-permute-done((s32[2,8]{1,0:T(2,128)S(1)}, s32[2,8]{1,0:T(2,128)S(1)}, u32[]{:S(2)}, u32[]{:S(2)}) %collective-permute-start.21) | collective-permute-done | bytes 96 | tf_op jit(solution)/shard_map/ppermute | solution.py:21
  91.9 4.3 %broadcast_in_dim.104 = f32[8,8,2,128,128]{4,3,2,1,0:T(8,128)} broadcast(f32[]{:T(128)} %constant.184.clone.1), dimensions={} | broadcast | bytes 8388612 | tf_op jit(solution)/shard_map/broadcast_in_dim | solution.py:80
  96.2 280.3 %while.31 = (s32[]{:T(128)}, bf16[8,2,2,128,128]{4,3,2,1,0:T(8,128)(2,1)}, s32[8,2]{1,0:T(8,128)S(1)}, s32[8]{0:T(128)S(1)}, s32[8,2]{1,0:T(8,128)S(1)}, /*index...) while((s32[]{:T(128)}, ...), condition=%wide.region_2.3_spmd, body=%wide.region_0.2_spmd.sunk | while | flops 541065856 | bytes 79698328 | solution.py:112
  96.2 3.2 copy.71
  99.4 5.0 %collective-permute-start.4 = (bf16[2,8,2,2,128,128]{4,5,3,2,1,0:T(8,128)(2,1)}, bf16[2,8,2,2,128,128]{4,5,3,2,1,0:T(8,128)(2,1)}, u32[]{:S(2)}, u32[]{:S(2)}) collective-permute-start(bf16[2,8,2,2,128,128]{4,5,3,2,1,0:T(8,128)(2,1)} %copy.71), channel_id=1, source_target_pairs={{0,24},{8,0},{16,8},{24,16},{1,25},{9,1},{17,9},{25,17},{2,26},{10... | collective-permute-start | bytes 6291464 | tf_op jit(solution)/shard_map/while/body/eval_jaxpr/ppermute | solution.py:21
  105.6 7.5 %collective-permute-start = (bf16[8,2,2,128,128]{4,3,2,1,0:T(8,128)(2,1)S(1)}, bf16[8,2,2,128,128]{4,3,2,1,0:T(8,128)(2,1)}, u32[]{:S(2)}, u32[]{:S(2)}) collective-permute-start(bf16[8,2,2,128,128]{4,3,2,1,0:T(8,128)(2,1)S(1)} %copy.67), channel_id=1, source_target_pairs={{0,7},{1,0},{2,1},{3,2},{4,3},{5,4},{6,5},{7,6},{8,15},{9,8},{10,9... | collective-permute-start | bytes 3145736 | tf_op jit(solution)/shard_map/while/body/eval_jaxpr/ppermute | solution.py:21
  115.9 2.8 slice_subtract_fusion.3
  120.7 2.9 copy.52
  128.6 10.2 %scatter_fusion = f32[8,8,2,128,128]{4,3,2,1,0:T(8,128)} fusion(f32[8,8,2,128,128]{4,3,2,1,0:T(8,128)} %get-tuple-element.477, s32[32]{0:T(128)S(1)} %fusion.20, f32[32,2,128,128]{3,2,1,0:T(8,128)} %copy.54), kind=kCustom, calls=%fused_computation.clone.1 | custom fusion | flops 1048576 | bytes 12583168 | tf_op jit(solution)/shard_map/while/body/eval_jaxpr/scatter-add | solution.py:44
  143.9 3.2 copy.71
  148.3 4.3 %collective-permute-start = (bf16[8,2,2,128,128]{4,3,2,1,0:T(8,128)(2,1)S(1)}, bf16[8,2,2,128,128]{4,3,2,1,0:T(8,128)(2,1)}, u32[]{:S(2)}, u32[]{:S(2)}) collective-permute-start(bf16[8,2,2,128,128]{4,3,2,1,0:T(8,128)(2,1)S(1)} %copy.67), channel_id=1, source_target_pairs={{0,7},{1,0},{2,1},{3,2},{4,3},{5,4},{6,5},{7,6},{8,15},{9,8},{10,9... | collective-permute-start | bytes 3145736 | tf_op jit(solution)/shard_map/while/body/eval_jaxpr/ppermute | solution.py:21
  155.5 2.8 slice_subtract_fusion.3
  160.2 2.9 copy.52
  168.1 10.2 %scatter_fusion = f32[8,8,2,128,128]{4,3,2,1,0:T(8,128)} fusion(f32[8,8,2,128,128]{4,3,2,1,0:T(8,128)} %get-tuple-element.477, s32[32]{0:T(128)S(1)} %fusion.20, f32[32,2,128,128]{3,2,1,0:T(8,128)} %copy.54), kind=kCustom, calls=%fused_computation.clone.1 | custom fusion | flops 1048576 | bytes 12583168 | tf_op jit(solution)/shard_map/while/body/eval_jaxpr/scatter-add | solution.py:44
  182.9 3.2 copy.71
  187.5 3.2 collective-permute-start
  193.4 2.8 slice_subtract_fusion.3
  198.1 2.9 copy.52
  206.1 10.2 %scatter_fusion = f32[8,8,2,128,128]{4,3,2,1,0:T(8,128)} fusion(f32[8,8,2,128,128]{4,3,2,1,0:T(8,128)} %get-tuple-element.477, s32[32]{0:T(128)S(1)} %fusion.20, f32[32,2,128,128]{3,2,1,0:T(8,128)} %copy.54), kind=kCustom, calls=%fused_computation.clone.1 | custom fusion | flops 1048576 | bytes 12583168 | tf_op jit(solution)/shard_map/while/body/eval_jaxpr/scatter-add | solution.py:44
  221.4 3.2 copy.71
  225.8 4.2 %collective-permute-start = (bf16[8,2,2,128,128]{4,3,2,1,0:T(8,128)(2,1)S(1)}, bf16[8,2,2,128,128]{4,3,2,1,0:T(8,128)(2,1)}, u32[]{:S(2)}, u32[]{:S(2)}) collective-permute-start(bf16[8,2,2,128,128]{4,3,2,1,0:T(8,128)(2,1)S(1)} %copy.67), channel_id=1, source_target_pairs={{0,7},{1,0},{2,1},{3,2},{4,3},{5,4},{6,5},{7,6},{8,15},{9,8},{10,9... | collective-permute-start | bytes 3145736 | tf_op jit(solution)/shard_map/while/body/eval_jaxpr/ppermute | solution.py:21
  237.7 2.9 copy.52
  245.7 10.1 %scatter_fusion = f32[8,8,2,128,128]{4,3,2,1,0:T(8,128)} fusion(f32[8,8,2,128,128]{4,3,2,1,0:T(8,128)} %get-tuple-element.477, s32[32]{0:T(128)S(1)} %fusion.20, f32[32,2,128,128]{3,2,1,0:T(8,128)} %copy.54), kind=kCustom, calls=%fused_computation.clone.1 | custom fusion | flops 1048576 | bytes 12583168 | tf_op jit(solution)/shard_map/while/body/eval_jaxpr/scatter-add | solution.py:44
  260.8 3.2 copy.71
  265.2 3.1 collective-permute-start
  271.0 2.8 slice_subtract_fusion.3
  275.7 2.9 copy.52
  283.7 10.3 %scatter_fusion = f32[8,8,2,128,128]{4,3,2,1,0:T(8,128)} fusion(f32[8,8,2,128,128]{4,3,2,1,0:T(8,128)} %get-tuple-element.477, s32[32]{0:T(128)S(1)} %fusion.20, f32[32,2,128,128]{3,2,1,0:T(8,128)} %copy.54), kind=kCustom, calls=%fused_computation.clone.1 | custom fusion | flops 1048576 | bytes 12583168 | tf_op jit(solution)/shard_map/while/body/eval_jaxpr/scatter-add | solution.py:44
  298.8 3.2 copy.71
  303.2 4.4 %collective-permute-start = (bf16[8,2,2,128,128]{4,3,2,1,0:T(8,128)(2,1)S(1)}, bf16[8,2,2,128,128]{4,3,2,1,0:T(8,128)(2,1)}, u32[]{:S(2)}, u32[]{:S(2)}) collective-permute-start(bf16[8,2,2,128,128]{4,3,2,1,0:T(8,128)(2,1)S(1)} %copy.67), channel_id=1, source_target_pairs={{0,7},{1,0},{2,1},{3,2},{4,3},{5,4},{6,5},{7,6},{8,15},{9,8},{10,9... | collective-permute-start | bytes 3145736 | tf_op jit(solution)/shard_map/while/body/eval_jaxpr/ppermute | solution.py:21
  315.3 2.9 copy.52
  323.3 10.2 %scatter_fusion = f32[8,8,2,128,128]{4,3,2,1,0:T(8,128)} fusion(f32[8,8,2,128,128]{4,3,2,1,0:T(8,128)} %get-tuple-element.477, s32[32]{0:T(128)S(1)} %fusion.20, f32[32,2,128,128]{3,2,1,0:T(8,128)} %copy.54), kind=kCustom, calls=%fused_computation.clone.1 | custom fusion | flops 1048576 | bytes 12583168 | tf_op jit(solution)/shard_map/while/body/eval_jaxpr/scatter-add | solution.py:44
  338.3 3.2 copy.71
  342.7 2.9 collective-permute-start
  353.2 2.9 copy.52
  361.2 10.3 %scatter_fusion = f32[8,8,2,128,128]{4,3,2,1,0:T(8,128)} fusion(f32[8,8,2,128,128]{4,3,2,1,0:T(8,128)} %get-tuple-element.477, s32[32]{0:T(128)S(1)} %fusion.20, f32[32,2,128,128]{3,2,1,0:T(8,128)} %copy.54), kind=kCustom, calls=%fused_computation.clone.1 | custom fusion | flops 1048576 | bytes 12583168 | tf_op jit(solution)/shard_map/while/body/eval_jaxpr/scatter-add | solution.py:44
  376.9 2.8 convolution_bitcast_fusion.1
  379.7 2.8 slice_subtract_fusion.1
  384.5 2.9 copy.38
  392.1 10.3 %scatter_fusion.1 = f32[8,8,2,128,128]{4,3,2,1,0:T(8,128)} fusion(f32[8,8,2,128,128]{4,3,2,1,0:T(8,128)} %get-tuple-element.301, s32[32]{0:T(128)S(1)} %fusion.13, f32[32,2,128,128]{3,2,1,0:T(8,128)} %copy.40), kind=kCustom, calls=%fused_computation.1 | custom fusion | flops 1048576 | bytes 12583168 | tf_op jit(solution)/shard_map/scatter-add | solution.py:44
  402.4 6.4 %convert_element_type.34 = bf16[8,8,2,128,128]{4,3,2,1,0:T(8,128)(2,1)} convert(f32[8,8,2,128,128]{4,3,2,1,0:T(8,128)} %scatter_fusion.1) | non-fusion elementwise | flops 2097152 | bytes 12582912 | tf_op jit(solution)/shard_map/convert_element_type | solution.py:117
  (351 shorter events, 146.1 us)
Async XLA Ops:
  3.2 40.7 %collective-permute-start.16 = (bf16[2,8,2,2,128,128]{4,5,3,2,1,0:T(8,128)(2,1)S(1)}, bf16[2,8,2,2,128,128]{4,5,3,2,1,0:T(8,128)(2,1)}, u32[]{:S(2)}, u32[]{:S(2)}) collective-permute-start(bf16[2,8,2,2,128,128]{4,5,3,2,1,0:T(8,128)(2,1)S(1)} %bitcast.81), channel_id=1, source_target_pairs={{0,24},{8,0},{16,8},{24,16},{1,25},{9,1},{17,9},{25,17},{2,26},{10... | collective-permute-start | bytes 6291464 | tf_op jit(solution)/shard_map/ppermute | solution.py:21
  6.5 40.8 %collective-permute-start.22 = (s32[2,8,2]{1,2,0:T(2,128)S(1)}, s32[2,8,2]{1,2,0:T(2,128)S(1)}, u32[]{:S(2)}, u32[]{:S(2)}) collective-permute-start(s32[2,8,2]{1,2,0:T(2,128)S(1)} %bitcast.85), channel_id=1, source_target_pairs={{0,24},{8,0},{16,8},{24,16},{1,25},{9,1},{17,9},{25,17},{2,26},{10... | collective-permute-start | bytes 392 | tf_op jit(solution)/shard_map/ppermute | solution.py:21
  6.6 44.1 %collective-permute-start.18 = (s32[2,8,2]{1,2,0:T(2,128)S(1)}, s32[2,8,2]{1,2,0:T(2,128)S(1)}, u32[]{:S(2)}, u32[]{:S(2)}) collective-permute-start(s32[2,8,2]{1,2,0:T(2,128)S(1)} %bitcast.86), channel_id=1, source_target_pairs={{0,24},{8,0},{16,8},{24,16},{1,25},{9,1},{17,9},{25,17},{2,26},{10... | collective-permute-start | bytes 392 | tf_op jit(solution)/shard_map/ppermute | solution.py:21
  6.7 9.7 %collective-permute-start.10 = (s32[8,2]{0,1:T(2,128)S(1)}, s32[8,2]{0,1:T(2,128)S(1)}, u32[]{:S(2)}, u32[]{:S(2)}) collective-permute-start(s32[8,2]{0,1:T(2,128)S(1)} %bitcast.87), channel_id=1, source_target_pairs={{0,7},{1,0},{2,1},{3,2},{4,3},{5,4},{6,5},{7,6},{8,15},{9,8},{10,9... | collective-permute-start | bytes 200 | tf_op jit(solution)/shard_map/ppermute | solution.py:21
  16.4 13.6 %collective-permute-start.20 = (s32[2,8]{1,0:T(2,128)S(1)}, s32[2,8]{1,0:T(2,128)S(1)}, u32[]{:S(2)}, u32[]{:S(2)}) collective-permute-start(s32[2,8]{1,0:T(2,128)S(1)} %bitcast.89), channel_id=1, source_target_pairs={{0,24},{8,0},{16,8},{24,16},{1,25},{9,1},{17,9},{25,17},{2,26},{10... | collective-permute-start | bytes 200 | tf_op jit(solution)/shard_map/ppermute | solution.py:21
  18.3 30.2 %collective-permute-start.8 = (bf16[8,2,2,128,128]{4,3,2,1,0:T(8,128)(2,1)S(1)}, bf16[8,2,2,128,128]{4,3,2,1,0:T(8,128)(2,1)S(1)}, u32[]{:S(2)}, u32[]{:S(2)}) collective-permute-start(bf16[8,2,2,128,128]{4,3,2,1,0:T(8,128)(2,1)S(1)} %bitcast.84), channel_id=1, source_target_pairs={{0,7},{1,0},{2,1},{3,2},{4,3},{5,4},{6,5},{7,6},{8,15},{9,8},{10,9... | collective-permute-start | bytes 3145736 | tf_op jit(solution)/shard_map/ppermute | solution.py:21
  30.0 10.9 %collective-permute-start.13 = (s32[8]{0:T(128)S(1)}, s32[8]{0:T(128)S(1)}, u32[]{:S(2)}, u32[]{:S(2)}) collective-permute-start(s32[8]{0:T(128)S(1)} %broadcast_select_fusion.10), channel_id=1, source_target_pairs={{0,6},{1,7},{2,0},{3,1},{4,2},{5,3},{6,4},{7,5},{8,14},{9,15},{10,... | collective-permute-start | bytes 104 | tf_op jit(solution)/shard_map/ppermute | solution.py:21
  45.7 44.6 %collective-permute-start.17 = (bf16[2,8,2,2,128,128]{4,5,3,2,1,0:T(8,128)(2,1)S(1)}, bf16[2,8,2,2,128,128]{4,5,3,2,1,0:T(8,128)(2,1)}, u32[]{:S(2)}, u32[]{:S(2)}) collective-permute-start(bf16[2,8,2,2,128,128]{4,5,3,2,1,0:T(8,128)(2,1)S(1)} %broadcast_select_fusion), channel_id=1, source_target_pairs={{0,16},{8,24},{16,0},{24,8},{1,17},{9,25},{17,1},{25,9},{2,18},{10... | collective-permute-start | bytes 6291464 | tf_op jit(solution)/shard_map/ppermute | solution.py:21
  45.8 43.2 %collective-permute-start.21 = (s32[2,8]{1,0:T(2,128)S(1)}, s32[2,8]{1,0:T(2,128)S(1)}, u32[]{:S(2)}, u32[]{:S(2)}) collective-permute-start(s32[2,8]{1,0:T(2,128)S(1)} %broadcast_select_fusion.8), channel_id=1, source_target_pairs={{0,16},{8,24},{16,0},{24,8},{1,17},{9,25},{17,1},{25,9},{2,18},{10... | collective-permute-start | bytes 200 | tf_op jit(solution)/shard_map/ppermute | solution.py:21
  48.6 40.5 %collective-permute-start.9 = (bf16[8,2,2,128,128]{4,3,2,1,0:T(8,128)(2,1)S(1)}, bf16[8,2,2,128,128]{4,3,2,1,0:T(8,128)(2,1)}, u32[]{:S(2)}, u32[]{:S(2)}) collective-permute-start(bf16[8,2,2,128,128]{4,3,2,1,0:T(8,128)(2,1)S(1)} %broadcast_select_fusion.2), channel_id=1, source_target_pairs={{0,6},{1,7},{2,0},{3,1},{4,2},{5,3},{6,4},{7,5},{8,14},{9,15},{10,... | collective-permute-start | bytes 3145736 | tf_op jit(solution)/shard_map/ppermute | solution.py:21
  50.6 38.6 %collective-permute-start.23 = (s32[2,8,2]{1,2,0:T(2,128)S(1)}, s32[2,8,2]{1,2,0:T(2,128)S(1)}, u32[]{:S(2)}, u32[]{:S(2)}) collective-permute-start(s32[2,8,2]{1,2,0:T(2,128)S(1)} %broadcast_select_fusion.4), channel_id=1, source_target_pairs={{0,16},{8,24},{16,0},{24,8},{1,17},{9,25},{17,1},{25,9},{2,18},{10... | collective-permute-start | bytes 392 | tf_op jit(solution)/shard_map/ppermute | solution.py:21
  50.7 38.4 %collective-permute-start.19 = (s32[2,8,2]{1,2,0:T(2,128)S(1)}, s32[2,8,2]{1,2,0:T(2,128)S(1)}, u32[]{:S(2)}, u32[]{:S(2)}) collective-permute-start(s32[2,8,2]{1,2,0:T(2,128)S(1)} %broadcast_select_fusion.5), channel_id=1, source_target_pairs={{0,16},{8,24},{16,0},{24,8},{1,17},{9,25},{17,1},{25,9},{2,18},{10... | collective-permute-start | bytes 392 | tf_op jit(solution)/shard_map/ppermute | solution.py:21
  99.4 44.4 %collective-permute-start.4 = (bf16[2,8,2,2,128,128]{4,5,3,2,1,0:T(8,128)(2,1)}, bf16[2,8,2,2,128,128]{4,5,3,2,1,0:T(8,128)(2,1)}, u32[]{:S(2)}, u32[]{:S(2)}) collective-permute-start(bf16[2,8,2,2,128,128]{4,5,3,2,1,0:T(8,128)(2,1)} %copy.71), channel_id=1, source_target_pairs={{0,24},{8,0},{16,8},{24,16},{1,25},{9,1},{17,9},{25,17},{2,26},{10... | collective-permute-start | bytes 6291464 | tf_op jit(solution)/shard_map/while/body/eval_jaxpr/ppermute | solution.py:21
  105.6 38.2 %collective-permute-start = (bf16[8,2,2,128,128]{4,3,2,1,0:T(8,128)(2,1)S(1)}, bf16[8,2,2,128,128]{4,3,2,1,0:T(8,128)(2,1)}, u32[]{:S(2)}, u32[]{:S(2)}) collective-permute-start(bf16[8,2,2,128,128]{4,3,2,1,0:T(8,128)(2,1)S(1)} %copy.67), channel_id=1, source_target_pairs={{0,7},{1,0},{2,1},{3,2},{4,3},{5,4},{6,5},{7,6},{8,15},{9,8},{10,9... | collective-permute-start | bytes 3145736 | tf_op jit(solution)/shard_map/while/body/eval_jaxpr/ppermute | solution.py:21
  113.2 26.6 %collective-permute-start.1 = (s32[8,2]{1,0:T(8,128)S(1)}, s32[8,2]{1,0:T(8,128)S(1)}, u32[]{:S(2)}, u32[]{:S(2)}) collective-permute-start(s32[8,2]{1,0:T(8,128)S(1)} %copy.68), channel_id=1, source_target_pairs={{0,7},{1,0},{2,1},{3,2},{4,3},{5,4},{6,5},{7,6},{8,15},{9,8},{10,9... | collective-permute-start | bytes 200 | tf_op jit(solution)/shard_map/while/body/eval_jaxpr/ppermute | solution.py:21
  113.2 27.6 %collective-permute-start.3 = (s32[8,2]{1,0:T(8,128)S(1)}, s32[8,2]{1,0:T(8,128)S(1)}, u32[]{:S(2)}, u32[]{:S(2)}) collective-permute-start(s32[8,2]{1,0:T(8,128)S(1)} %copy.70), channel_id=1, source_target_pairs={{0,7},{1,0},{2,1},{3,2},{4,3},{5,4},{6,5},{7,6},{8,15},{9,8},{10,9... | collective-permute-start | bytes 200 | tf_op jit(solution)/shard_map/while/body/eval_jaxpr/ppermute | solution.py:21
  113.3 25.6 %collective-permute-start.2 = (s32[8]{0:T(128)S(1)}, s32[8]{0:T(128)S(1)}, u32[]{:S(2)}, u32[]{:S(2)}) collective-permute-start(s32[8]{0:T(128)S(1)} %copy.69), channel_id=1, source_target_pairs={{0,7},{1,0},{2,1},{3,2},{4,3},{5,4},{6,5},{7,6},{8,15},{9,8},{10,9... | collective-permute-start | bytes 104 | tf_op jit(solution)/shard_map/while/body/eval_jaxpr/ppermute | solution.py:21
  147.1 35.8 %collective-permute-start.4 = (bf16[2,8,2,2,128,128]{4,5,3,2,1,0:T(8,128)(2,1)}, bf16[2,8,2,2,128,128]{4,5,3,2,1,0:T(8,128)(2,1)}, u32[]{:S(2)}, u32[]{:S(2)}) collective-permute-start(bf16[2,8,2,2,128,128]{4,5,3,2,1,0:T(8,128)(2,1)} %copy.71), channel_id=1, source_target_pairs={{0,24},{8,0},{16,8},{24,16},{1,25},{9,1},{17,9},{25,17},{2,26},{10... | collective-permute-start | bytes 6291464 | tf_op jit(solution)/shard_map/while/body/eval_jaxpr/ppermute | solution.py:21
  148.3 34.6 %collective-permute-start = (bf16[8,2,2,128,128]{4,3,2,1,0:T(8,128)(2,1)S(1)}, bf16[8,2,2,128,128]{4,3,2,1,0:T(8,128)(2,1)}, u32[]{:S(2)}, u32[]{:S(2)}) collective-permute-start(bf16[8,2,2,128,128]{4,3,2,1,0:T(8,128)(2,1)S(1)} %copy.67), channel_id=1, source_target_pairs={{0,7},{1,0},{2,1},{3,2},{4,3},{5,4},{6,5},{7,6},{8,15},{9,8},{10,9... | collective-permute-start | bytes 3145736 | tf_op jit(solution)/shard_map/while/body/eval_jaxpr/ppermute | solution.py:21
  152.6 27.2 %collective-permute-start.1 = (s32[8,2]{1,0:T(8,128)S(1)}, s32[8,2]{1,0:T(8,128)S(1)}, u32[]{:S(2)}, u32[]{:S(2)}) collective-permute-start(s32[8,2]{1,0:T(8,128)S(1)} %copy.68), channel_id=1, source_target_pairs={{0,7},{1,0},{2,1},{3,2},{4,3},{5,4},{6,5},{7,6},{8,15},{9,8},{10,9... | collective-permute-start | bytes 200 | tf_op jit(solution)/shard_map/while/body/eval_jaxpr/ppermute | solution.py:21
  152.7 27.1 %collective-permute-start.3 = (s32[8,2]{1,0:T(8,128)S(1)}, s32[8,2]{1,0:T(8,128)S(1)}, u32[]{:S(2)}, u32[]{:S(2)}) collective-permute-start(s32[8,2]{1,0:T(8,128)S(1)} %copy.70), channel_id=1, source_target_pairs={{0,7},{1,0},{2,1},{3,2},{4,3},{5,4},{6,5},{7,6},{8,15},{9,8},{10,9... | collective-permute-start | bytes 200 | tf_op jit(solution)/shard_map/while/body/eval_jaxpr/ppermute | solution.py:21
  152.8 25.5 %collective-permute-start.2 = (s32[8]{0:T(128)S(1)}, s32[8]{0:T(128)S(1)}, u32[]{:S(2)}, u32[]{:S(2)}) collective-permute-start(s32[8]{0:T(128)S(1)} %copy.69), channel_id=1, source_target_pairs={{0,7},{1,0},{2,1},{3,2},{4,3},{5,4},{6,5},{7,6},{8,15},{9,8},{10,9... | collective-permute-start | bytes 104 | tf_op jit(solution)/shard_map/while/body/eval_jaxpr/ppermute | solution.py:21
  186.1 35.3 %collective-permute-start.4 = (bf16[2,8,2,2,128,128]{4,5,3,2,1,0:T(8,128)(2,1)}, bf16[2,8,2,2,128,128]{4,5,3,2,1,0:T(8,128)(2,1)}, u32[]{:S(2)}, u32[]{:S(2)}) collective-permute-start(bf16[2,8,2,2,128,128]{4,5,3,2,1,0:T(8,128)(2,1)} %copy.71), channel_id=1, source_target_pairs={{0,24},{8,0},{16,8},{24,16},{1,25},{9,1},{17,9},{25,17},{2,26},{10... | collective-permute-start | bytes 6291464 | tf_op jit(solution)/shard_map/while/body/eval_jaxpr/ppermute | solution.py:21
  187.5 33.9 %collective-permute-start = (bf16[8,2,2,128,128]{4,3,2,1,0:T(8,128)(2,1)S(1)}, bf16[8,2,2,128,128]{4,3,2,1,0:T(8,128)(2,1)}, u32[]{:S(2)}, u32[]{:S(2)}) collective-permute-start(bf16[8,2,2,128,128]{4,3,2,1,0:T(8,128)(2,1)S(1)} %copy.67), channel_id=1, source_target_pairs={{0,7},{1,0},{2,1},{3,2},{4,3},{5,4},{6,5},{7,6},{8,15},{9,8},{10,9... | collective-permute-start | bytes 3145736 | tf_op jit(solution)/shard_map/while/body/eval_jaxpr/ppermute | solution.py:21
  190.7 27.6 %collective-permute-start.1 = (s32[8,2]{1,0:T(8,128)S(1)}, s32[8,2]{1,0:T(8,128)S(1)}, u32[]{:S(2)}, u32[]{:S(2)}) collective-permute-start(s32[8,2]{1,0:T(8,128)S(1)} %copy.68), channel_id=1, source_target_pairs={{0,7},{1,0},{2,1},{3,2},{4,3},{5,4},{6,5},{7,6},{8,15},{9,8},{10,9... | collective-permute-start | bytes 200 | tf_op jit(solution)/shard_map/while/body/eval_jaxpr/ppermute | solution.py:21
  190.7 27.7 %collective-permute-start.3 = (s32[8,2]{1,0:T(8,128)S(1)}, s32[8,2]{1,0:T(8,128)S(1)}, u32[]{:S(2)}, u32[]{:S(2)}) collective-permute-start(s32[8,2]{1,0:T(8,128)S(1)} %copy.70), channel_id=1, source_target_pairs={{0,7},{1,0},{2,1},{3,2},{4,3},{5,4},{6,5},{7,6},{8,15},{9,8},{10,9... | collective-permute-start | bytes 200 | tf_op jit(solution)/shard_map/while/body/eval_jaxpr/ppermute | solution.py:21
  190.8 25.5 %collective-permute-start.2 = (s32[8]{0:T(128)S(1)}, s32[8]{0:T(128)S(1)}, u32[]{:S(2)}, u32[]{:S(2)}) collective-permute-start(s32[8]{0:T(128)S(1)} %copy.69), channel_id=1, source_target_pairs={{0,7},{1,0},{2,1},{3,2},{4,3},{5,4},{6,5},{7,6},{8,15},{9,8},{10,9... | collective-permute-start | bytes 104 | tf_op jit(solution)/shard_map/while/body/eval_jaxpr/ppermute | solution.py:21
  216.3 5.0 %collective-permute-start.5 = (s32[2,8,2]{1,2,0:T(2,128)S(1)}, s32[2,8,2]{1,2,0:T(2,128)S(1)}, u32[]{:S(2)}, u32[]{:S(2)}) collective-permute-start(s32[2,8,2]{1,2,0:T(2,128)S(1)} %copy.72), channel_id=1, source_target_pairs={{0,24},{8,0},{16,8},{24,16},{1,25},{9,1},{17,9},{25,17},{2,26},{10... | collective-permute-start | bytes 392 | tf_op jit(solution)/shard_map/while/body/eval_jaxpr/ppermute | solution.py:21
  224.6 36.2 %collective-permute-start.4 = (bf16[2,8,2,2,128,128]{4,5,3,2,1,0:T(8,128)(2,1)}, bf16[2,8,2,2,128,128]{4,5,3,2,1,0:T(8,128)(2,1)}, u32[]{:S(2)}, u32[]{:S(2)}) collective-permute-start(bf16[2,8,2,2,128,128]{4,5,3,2,1,0:T(8,128)(2,1)} %copy.71), channel_id=1, source_target_pairs={{0,24},{8,0},{16,8},{24,16},{1,25},{9,1},{17,9},{25,17},{2,26},{10... | collective-permute-start | bytes 6291464 | tf_op jit(solution)/shard_map/while/body/eval_jaxpr/ppermute | solution.py:21
  225.8 34.9 %collective-permute-start = (bf16[8,2,2,128,128]{4,3,2,1,0:T(8,128)(2,1)S(1)}, bf16[8,2,2,128,128]{4,3,2,1,0:T(8,128)(2,1)}, u32[]{:S(2)}, u32[]{:S(2)}) collective-permute-start(bf16[8,2,2,128,128]{4,3,2,1,0:T(8,128)(2,1)S(1)} %copy.67), channel_id=1, source_target_pairs={{0,7},{1,0},{2,1},{3,2},{4,3},{5,4},{6,5},{7,6},{8,15},{9,8},{10,9... | collective-permute-start | bytes 3145736 | tf_op jit(solution)/shard_map/while/body/eval_jaxpr/ppermute | solution.py:21
  230.0 27.6 %collective-permute-start.1 = (s32[8,2]{1,0:T(8,128)S(1)}, s32[8,2]{1,0:T(8,128)S(1)}, u32[]{:S(2)}, u32[]{:S(2)}) collective-permute-start(s32[8,2]{1,0:T(8,128)S(1)} %copy.68), channel_id=1, source_target_pairs={{0,7},{1,0},{2,1},{3,2},{4,3},{5,4},{6,5},{7,6},{8,15},{9,8},{10,9... | collective-permute-start | bytes 200 | tf_op jit(solution)/shard_map/while/body/eval_jaxpr/ppermute | solution.py:21
  230.3 27.4 %collective-permute-start.3 = (s32[8,2]{1,0:T(8,128)S(1)}, s32[8,2]{1,0:T(8,128)S(1)}, u32[]{:S(2)}, u32[]{:S(2)}) collective-permute-start(s32[8,2]{1,0:T(8,128)S(1)} %copy.70), channel_id=1, source_target_pairs={{0,7},{1,0},{2,1},{3,2},{4,3},{5,4},{6,5},{7,6},{8,15},{9,8},{10,9... | collective-permute-start | bytes 200 | tf_op jit(solution)/shard_map/while/body/eval_jaxpr/ppermute | solution.py:21
  230.3 25.4 %collective-permute-start.2 = (s32[8]{0:T(128)S(1)}, s32[8]{0:T(128)S(1)}, u32[]{:S(2)}, u32[]{:S(2)}) collective-permute-start(s32[8]{0:T(128)S(1)} %copy.69), channel_id=1, source_target_pairs={{0,7},{1,0},{2,1},{3,2},{4,3},{5,4},{6,5},{7,6},{8,15},{9,8},{10,9... | collective-permute-start | bytes 104 | tf_op jit(solution)/shard_map/while/body/eval_jaxpr/ppermute | solution.py:21
  264.0 34.8 %collective-permute-start.4 = (bf16[2,8,2,2,128,128]{4,5,3,2,1,0:T(8,128)(2,1)}, bf16[2,8,2,2,128,128]{4,5,3,2,1,0:T(8,128)(2,1)}, u32[]{:S(2)}, u32[]{:S(2)}) collective-permute-start(bf16[2,8,2,2,128,128]{4,5,3,2,1,0:T(8,128)(2,1)} %copy.71), channel_id=1, source_target_pairs={{0,24},{8,0},{16,8},{24,16},{1,25},{9,1},{17,9},{25,17},{2,26},{10... | collective-permute-start | bytes 6291464 | tf_op jit(solution)/shard_map/while/body/eval_jaxpr/ppermute | solution.py:21
  265.2 33.6 %collective-permute-start = (bf16[8,2,2,128,128]{4,3,2,1,0:T(8,128)(2,1)S(1)}, bf16[8,2,2,128,128]{4,3,2,1,0:T(8,128)(2,1)}, u32[]{:S(2)}, u32[]{:S(2)}) collective-permute-start(bf16[8,2,2,128,128]{4,3,2,1,0:T(8,128)(2,1)S(1)} %copy.67), channel_id=1, source_target_pairs={{0,7},{1,0},{2,1},{3,2},{4,3},{5,4},{6,5},{7,6},{8,15},{9,8},{10,9... | collective-permute-start | bytes 3145736 | tf_op jit(solution)/shard_map/while/body/eval_jaxpr/ppermute | solution.py:21
  268.3 27.4 %collective-permute-start.1 = (s32[8,2]{1,0:T(8,128)S(1)}, s32[8,2]{1,0:T(8,128)S(1)}, u32[]{:S(2)}, u32[]{:S(2)}) collective-permute-start(s32[8,2]{1,0:T(8,128)S(1)} %copy.68), channel_id=1, source_target_pairs={{0,7},{1,0},{2,1},{3,2},{4,3},{5,4},{6,5},{7,6},{8,15},{9,8},{10,9... | collective-permute-start | bytes 200 | tf_op jit(solution)/shard_map/while/body/eval_jaxpr/ppermute | solution.py:21
  268.3 27.5 %collective-permute-start.3 = (s32[8,2]{1,0:T(8,128)S(1)}, s32[8,2]{1,0:T(8,128)S(1)}, u32[]{:S(2)}, u32[]{:S(2)}) collective-permute-start(s32[8,2]{1,0:T(8,128)S(1)} %copy.70), channel_id=1, source_target_pairs={{0,7},{1,0},{2,1},{3,2},{4,3},{5,4},{6,5},{7,6},{8,15},{9,8},{10,9... | collective-permute-start | bytes 200 | tf_op jit(solution)/shard_map/while/body/eval_jaxpr/ppermute | solution.py:21
  268.4 25.6 %collective-permute-start.2 = (s32[8]{0:T(128)S(1)}, s32[8]{0:T(128)S(1)}, u32[]{:S(2)}, u32[]{:S(2)}) collective-permute-start(s32[8]{0:T(128)S(1)} %copy.69), channel_id=1, source_target_pairs={{0,7},{1,0},{2,1},{3,2},{4,3},{5,4},{6,5},{7,6},{8,15},{9,8},{10,9... | collective-permute-start | bytes 104 | tf_op jit(solution)/shard_map/while/body/eval_jaxpr/ppermute | solution.py:21
  302.0 36.3 %collective-permute-start.4 = (bf16[2,8,2,2,128,128]{4,5,3,2,1,0:T(8,128)(2,1)}, bf16[2,8,2,2,128,128]{4,5,3,2,1,0:T(8,128)(2,1)}, u32[]{:S(2)}, u32[]{:S(2)}) collective-permute-start(bf16[2,8,2,2,128,128]{4,5,3,2,1,0:T(8,128)(2,1)} %copy.71), channel_id=1, source_target_pairs={{0,24},{8,0},{16,8},{24,16},{1,25},{9,1},{17,9},{25,17},{2,26},{10... | collective-permute-start | bytes 6291464 | tf_op jit(solution)/shard_map/while/body/eval_jaxpr/ppermute | solution.py:21
  303.2 35.0 %collective-permute-start = (bf16[8,2,2,128,128]{4,3,2,1,0:T(8,128)(2,1)S(1)}, bf16[8,2,2,128,128]{4,3,2,1,0:T(8,128)(2,1)}, u32[]{:S(2)}, u32[]{:S(2)}) collective-permute-start(bf16[8,2,2,128,128]{4,3,2,1,0:T(8,128)(2,1)S(1)} %copy.67), channel_id=1, source_target_pairs={{0,7},{1,0},{2,1},{3,2},{4,3},{5,4},{6,5},{7,6},{8,15},{9,8},{10,9... | collective-permute-start | bytes 3145736 | tf_op jit(solution)/shard_map/while/body/eval_jaxpr/ppermute | solution.py:21
  307.6 27.5 %collective-permute-start.1 = (s32[8,2]{1,0:T(8,128)S(1)}, s32[8,2]{1,0:T(8,128)S(1)}, u32[]{:S(2)}, u32[]{:S(2)}) collective-permute-start(s32[8,2]{1,0:T(8,128)S(1)} %copy.68), channel_id=1, source_target_pairs={{0,7},{1,0},{2,1},{3,2},{4,3},{5,4},{6,5},{7,6},{8,15},{9,8},{10,9... | collective-permute-start | bytes 200 | tf_op jit(solution)/shard_map/while/body/eval_jaxpr/ppermute | solution.py:21
  308.0 27.3 %collective-permute-start.3 = (s32[8,2]{1,0:T(8,128)S(1)}, s32[8,2]{1,0:T(8,128)S(1)}, u32[]{:S(2)}, u32[]{:S(2)}) collective-permute-start(s32[8,2]{1,0:T(8,128)S(1)} %copy.70), channel_id=1, source_target_pairs={{0,7},{1,0},{2,1},{3,2},{4,3},{5,4},{6,5},{7,6},{8,15},{9,8},{10,9... | collective-permute-start | bytes 200 | tf_op jit(solution)/shard_map/while/body/eval_jaxpr/ppermute | solution.py:21
  308.0 25.5 %collective-permute-start.2 = (s32[8]{0:T(128)S(1)}, s32[8]{0:T(128)S(1)}, u32[]{:S(2)}, u32[]{:S(2)}) collective-permute-start(s32[8]{0:T(128)S(1)} %copy.69), channel_id=1, source_target_pairs={{0,7},{1,0},{2,1},{3,2},{4,3},{5,4},{6,5},{7,6},{8,15},{9,8},{10,9... | collective-permute-start | bytes 104 | tf_op jit(solution)/shard_map/while/body/eval_jaxpr/ppermute | solution.py:21
  341.5 34.9 %collective-permute-start.4 = (bf16[2,8,2,2,128,128]{4,5,3,2,1,0:T(8,128)(2,1)}, bf16[2,8,2,2,128,128]{4,5,3,2,1,0:T(8,128)(2,1)}, u32[]{:S(2)}, u32[]{:S(2)}) collective-permute-start(bf16[2,8,2,2,128,128]{4,5,3,2,1,0:T(8,128)(2,1)} %copy.71), channel_id=1, source_target_pairs={{0,24},{8,0},{16,8},{24,16},{1,25},{9,1},{17,9},{25,17},{2,26},{10... | collective-permute-start | bytes 6291464 | tf_op jit(solution)/shard_map/while/body/eval_jaxpr/ppermute | solution.py:21
  342.7 33.6 %collective-permute-start = (bf16[8,2,2,128,128]{4,3,2,1,0:T(8,128)(2,1)S(1)}, bf16[8,2,2,128,128]{4,3,2,1,0:T(8,128)(2,1)}, u32[]{:S(2)}, u32[]{:S(2)}) collective-permute-start(bf16[8,2,2,128,128]{4,3,2,1,0:T(8,128)(2,1)S(1)} %copy.67), channel_id=1, source_target_pairs={{0,7},{1,0},{2,1},{3,2},{4,3},{5,4},{6,5},{7,6},{8,15},{9,8},{10,9... | collective-permute-start | bytes 3145736 | tf_op jit(solution)/shard_map/while/body/eval_jaxpr/ppermute | solution.py:21
  345.7 27.6 %collective-permute-start.1 = (s32[8,2]{1,0:T(8,128)S(1)}, s32[8,2]{1,0:T(8,128)S(1)}, u32[]{:S(2)}, u32[]{:S(2)}) collective-permute-start(s32[8,2]{1,0:T(8,128)S(1)} %copy.68), channel_id=1, source_target_pairs={{0,7},{1,0},{2,1},{3,2},{4,3},{5,4},{6,5},{7,6},{8,15},{9,8},{10,9... | collective-permute-start | bytes 200 | tf_op jit(solution)/shard_map/while/body/eval_jaxpr/ppermute | solution.py:21
  345.8 27.6 %collective-permute-start.3 = (s32[8,2]{1,0:T(8,128)S(1)}, s32[8,2]{1,0:T(8,128)S(1)}, u32[]{:S(2)}, u32[]{:S(2)}) collective-permute-start(s32[8,2]{1,0:T(8,128)S(1)} %copy.70), channel_id=1, source_target_pairs={{0,7},{1,0},{2,1},{3,2},{4,3},{5,4},{6,5},{7,6},{8,15},{9,8},{10,9... | collective-permute-start | bytes 200 | tf_op jit(solution)/shard_map/while/body/eval_jaxpr/ppermute | solution.py:21
  345.8 25.6 %collective-permute-start.2 = (s32[8]{0:T(128)S(1)}, s32[8]{0:T(128)S(1)}, u32[]{:S(2)}, u32[]{:S(2)}) collective-permute-start(s32[8]{0:T(128)S(1)} %copy.69), channel_id=1, source_target_pairs={{0,7},{1,0},{2,1},{3,2},{4,3},{5,4},{6,5},{7,6},{8,15},{9,8},{10,9... | collective-permute-start | bytes 104 | tf_op jit(solution)/shard_map/while/body/eval_jaxpr/ppermute | solution.py:21
  (33 other events, 213.0 us)
where the time goes:
time: 411 us; the launch traced here: 409 us
  other arithmetic  133 us (32%)
  local copies, waits for them, and re-layouts  99.8 us (24%)
  starting transfers between devices  85.8 us (21%)
  waiting for transfers between devices  69 us (17%)
  matrix products  20.2 us (5%)
    ppermute x72, starting transfers between devices, passed_along(): return lax.ppermute(value, axis, pairs)  85.8 us
    scatter-add x8, other arithmetic, pair_products(): total.at[row_index, col_index].add(product.reshape(-1, 2, width, width))  81.7 us
    ppermute x72, waiting for transfers between devices, passed_along(): return lax.ppermute(value, axis, pairs)  69 us
    another operation x56, local copies, waits for them, and re-layouts  31 us
    sub x8, local copies, waits for them, and re-layouts, pair_products(): real_part = terms[:, :, :, 0, 0] - terms[:, :, :, 1, 1]  22.2 us
    sub x8, other arithmetic, pair_products(): real_part = terms[:, :, :, 0, 0] - terms[:, :, :, 1, 1]  22.2 us
    dot_general x8, matrix products, pair_products(): jnp.einsum('kmcij,kndjl->kmncdil', left_blocks, right_blocks, preferred_e...  20.2 us
    mul x8, local copies, waits for them, and re-layouts, pair_products(): jnp.stack([real_part, imag_part], axis=3)  18.3 us
  transfers between devices with their start and end apart: 72, of which 19 were waited for; matrix products, arithmetic and copies ran while one was open for 46% of the time, Pallas kernels for 0%

commit v1 on v0

v1 whole, which is shorter than its diff:
```python
import functools

import jax
import jax.numpy as jnp
from jax import lax
from jax.experimental import pallas as pl
from jax.experimental.pallas import tpu as pltpu
from jax.sharding import PartitionSpec as P

GR = 8
KB = 8
BS = 128
LEVEL_CUT = 7
HALF = 4
BLOCK_ROWS = 2 * 2 * BS
META = 16
CHUNK = HALF * BLOCK_ROWS
PANEL = KB * BLOCK_ROWS


def fill_table(table_ref, places, count, level, rows):
    lane = lax.broadcasted_iota(jnp.int32, (META, BS), 1)
    sub = lax.broadcasted_iota(jnp.int32, (META, BS), 0)
    table = jnp.zeros((META, BS), jnp.float32)
    for k in range(rows):
        for m in range(2):
            live = (m < count(k)).astype(jnp.int32)
            for at, value in ((m, places(k, m)), (2 + m, level(k, m)), (4 + m, live)):
                table = jnp.where((sub == k) & (lane == at), value.astype(jnp.float32), table)
    table_ref[...] = table.astype(jnp.bfloat16)


def pack_left_kernel(rows_ref, count_ref, level_ref, blocks_ref, first_ref, second_ref, sem):
    outs = (first_ref, second_ref)
    copies = [
        pltpu.make_async_copy(
            blocks_ref.at[pl.ds(h * CHUNK, CHUNK)], outs[h].at[pl.ds(0, CHUNK)], sem.at[h]
        )
        for h in range(2)
    ]
    for copy in copies:
        copy.start()
    for h in range(2):
        fill_table(
            outs[h].at[pl.ds(CHUNK, META)],
            lambda k, m: rows_ref[m, h * HALF + k],
            lambda k: count_ref[0, h * HALF + k],
            lambda k, m: level_ref[m, h * HALF + k],
            HALF,
        )
    for copy in copies:
        copy.wait()


def pack_left(blocks, rows, count, level):
    shape = pltpu.VMEM((CHUNK + META, BS), jnp.bfloat16)
    return pl.pallas_call(
        pack_left_kernel,
        out_shape=(shape, shape),
        in_specs=[pl.BlockSpec(memory_space=pltpu.SMEM)] * 3
        + [pl.BlockSpec(memory_space=pltpu.HBM)],
        out_specs=[pl.BlockSpec(memory_space=pltpu.VMEM)] * 2,
        scratch_shapes=[pltpu.SemaphoreType.DMA((2,))],
    )(jnp.swapaxes(rows[0], 0, 1), count, jnp.swapaxes(level[0], 0, 1), blocks.reshape(-1, BS))


def pack_right_kernel(which_ref, cols_ref, count_ref, level_ref, blocks_ref, out_ref, sem):
    which = which_ref[0]
    blocks = pltpu.make_async_copy(blocks_ref.at[which], out_ref.at[pl.ds(0, PANEL)], sem)
    blocks.start()
    fill_table(
        out_ref.at[pl.ds(PANEL, META)],
        lambda k, m: cols_ref[which, m, k],
        lambda k: count_ref[which, 0, k],
        lambda k, m: level_ref[which, m, k],
        KB,
    )
    blocks.wait()


def pack_right(which, blocks, cols, count, level):
    return pl.pallas_call(
        pack_right_kernel,
        out_shape=pltpu.VMEM((PANEL + META, BS), jnp.bfloat16),
        in_specs=[pl.BlockSpec(memory_space=pltpu.SMEM)] * 4
        + [pl.BlockSpec(memory_space=pltpu.HBM)],
        out_specs=pl.BlockSpec(memory_space=pltpu.VMEM),
        scratch_shapes=[pltpu.SemaphoreType.DMA],
    )(
        which,
        jnp.swapaxes(cols[:, :, 0], 1, 2),
        jnp.swapaxes(count, 1, 2),
        jnp.swapaxes(level[:, :, 0], 1, 2),
        blocks.reshape(-1, PANEL, BS),
    )


def shifted(value, axis, steps):
    count = lax.axis_size(axis)
    return lax.ppermute(value, axis, [(i, (i + steps) % count) for i in range(count)])


def crossed(value, axis, bit):
    count = lax.axis_size(axis)
    return lax.ppermute(value, axis, [(i, i ^ bit) for i in range(count)])


def multiply_kernel(offsets, halves, first, last, grid_rows, grid_cols, n_rights, *refs):
    n = len(offsets)
    where_ref = refs[0]
    lefts = refs[1 : 1 + n]
    rights = refs[1 + n : 1 + n + n_rights]
    rest = refs[1 + n + n_rights :]
    if not first:
        acc_ref = rest[0]
        rest = rest[1:]
    out_ref = rest[0]
    rest = rest[1:]
    if last:
        stage_ref = rest[0]
        rest = rest[1:]
    else:
        acc_ref = out_ref
    left_buf, right_buf, table_buf, whole_buf, table_smem, data_sem, table_sem, smem_sem, out_sem = rest
    own_row = where_ref[0]
    own_col = where_ref[1]

    def right_copies(i, act):
        panel = (own_col + offsets[i] + grid_cols) % grid_cols
        source = (panel % grid_rows) ^ own_row
        near = -1 <= offsets[i] <= grid_rows - 2
        for s in range(grid_rows):

            @pl.when(source == s)
            def _(s=s):
                act(rights[s if near else n_rights - grid_rows + s])

    for i in range(n):
        pltpu.make_async_copy(
            lefts[i].at[pl.ds(CHUNK, META)], table_buf.at[2 * i], table_sem
        ).start()
        right_copies(
            i,
            lambda src, i=i: pltpu.make_async_copy(
                src.at[pl.ds(PANEL, META)], table_buf.at[2 * i + 1], table_sem
            ).start(),
        )
    for i in range(n):
        pltpu.make_async_copy(lefts[i].at[pl.ds(0, CHUNK)], left_buf.at[i], data_sem.at[i]).start()
        right_copies(
            i,
            lambda src, i=i: pltpu.make_async_copy(
                src.at[pl.ds(halves[i] * CHUNK, CHUNK)], right_buf.at[i], data_sem.at[i]
            ).start(),
        )
    if first:
        acc_ref[...] = jnp.zeros_like(acc_ref)
    pltpu.make_async_copy(table_buf, table_buf, table_sem).wait()
    whole_buf[...] = table_buf[:, : whole_buf.shape[1]].astype(jnp.float32).astype(jnp.int32)
    to_smem = pltpu.make_async_copy(whole_buf, table_smem, smem_sem)
    to_smem.start()
    to_smem.wait()

    def one_item(i, half_kb):
        pltpu.make_async_copy(left_buf.at[i], left_buf.at[i], data_sem.at[i]).wait()
        pltpu.make_async_copy(right_buf.at[i], right_buf.at[i], data_sem.at[i]).wait()

        def one_kb(k, carry):
            kr = half_kb + k
            base = pl.multiple_of(k * BLOCK_ROWS, BLOCK_ROWS)

            def right_part(slot, part):
                return right_buf[i, pl.ds(base + (2 * slot + part) * BS, BS), :]

            right = jnp.concatenate(
                [
                    jnp.concatenate([right_part(0, 0), right_part(1, 0)], axis=1),
                    jnp.concatenate([right_part(0, 1), right_part(1, 1)], axis=1),
                ],
                axis=0,
            )
            for m in range(2):
                row = table_smem[2 * i, k, m]
                level = table_smem[2 * i, k, 2 + m]
                live = table_smem[2 * i, k, 4 + m] > 0
                kept = [
                    live
                    & (table_smem[2 * i + 1, kr, 4 + q] > 0)
                    & (level + table_smem[2 * i + 1, kr, 2 + q] >= LEVEL_CUT)
                    for q in range(2)
                ]

                @pl.when(kept[0] | kept[1])
                def _():
                    real = left_buf[i, pl.ds(base + 2 * m * BS, BS), :]
                    imag = left_buf[i, pl.ds(base + (2 * m + 1) * BS, BS), :]
                    left = jnp.concatenate(
                        [
                            jnp.concatenate([real, -imag], axis=1),
                            jnp.concatenate([imag, real], axis=1),
                        ],
                        axis=0,
                    )
                    product = jnp.dot(left, right, preferred_element_type=jnp.float32)
                    for q in range(2):

                        @pl.when(kept[q])
                        def _(q=q):
                            col = table_smem[2 * i + 1, kr, q]
                            for part in range(2):
                                acc_ref[row, col, part] += product[
                                    part * BS : (part + 1) * BS, q * BS : (q + 1) * BS
                                ]

            return carry

        lax.fori_loop(0, HALF, one_kb, 0)

    assert all(h == i % 2 for i, h in enumerate(halves))
    lax.fori_loop(0, n, lambda i, c: (one_item(i, (i % 2) * HALF), c)[1], 0)

    if last:
        for r in range(GR):
            stage_ref[r] = acc_ref[r].astype(jnp.bfloat16)
            pltpu.make_async_copy(stage_ref.at[r], out_ref.at[r], out_sem).start()
        pltpu.make_async_copy(stage_ref, out_ref, out_sem).wait()


def multiply(where, items, rights, total, last, local):
    grid_rows = lax.axis_size("row")
    grid_cols = lax.axis_size("col")
    lefts = [value for value, _, _ in items]
    offsets = tuple(offset for _, offset, _ in items)
    halves = tuple(half for _, _, half in items)
    n = len(items)
    first = total is None
    shape = (GR, KB, 2, BS, BS)
    operands = [where, *lefts, *rights]
    in_specs = [pl.BlockSpec(memory_space=pltpu.SMEM)]
    in_specs += [
        pl.BlockSpec(memory_space=pltpu.VMEM if any(v is own for own in local) else pltpu.HBM)
        for v in operands[1:]
    ]
    scratch = []
    aliases = {}
    if not first:
        operands.append(total)
        in_specs.append(pl.BlockSpec(memory_space=pltpu.VMEM))
    if last:
        out_shape = jax.ShapeDtypeStruct(shape, jnp.bfloat16)
        out_specs = pl.BlockSpec(memory_space=pltpu.HBM)
        scratch = [pltpu.VMEM(shape, jnp.bfloat16)]
    else:
        out_shape = pltpu.VMEM(shape, jnp.float32)
        out_specs = pl.BlockSpec(memory_space=pltpu.VMEM)
        if not first:
            aliases = {len(operands) - 1: 0}
    scratch += [
        pltpu.VMEM((n, CHUNK, BS), jnp.bfloat16),
        pltpu.VMEM((n, CHUNK, BS), jnp.bfloat16),
        pltpu.VMEM((2 * n, META, BS), jnp.bfloat16),
        pltpu.VMEM((2 * n, KB, BS), jnp.int32),
        pltpu.SMEM((2 * n, KB, BS), jnp.int32),
        pltpu.SemaphoreType.DMA((n,)),
        pltpu.SemaphoreType.DMA,
        pltpu.SemaphoreType.DMA,
        pltpu.SemaphoreType.DMA,
    ]
    kernel = functools.partial(
        multiply_kernel, offsets, halves, first, last, grid_rows, grid_cols, len(rights)
    )
    return pl.pallas_call(
        kernel,
        out_shape=out_shape,
        in_specs=in_specs,
        out_specs=out_specs,
        scratch_shapes=scratch,
        input_output_aliases=aliases,
        compiler_params=pltpu.CompilerParams(vmem_limit_bytes=32 * 1024 * 1024),
    )(*operands)


def body(
    left_blocks,
    left_rows,
    left_count,
    left_level,
    right_blocks,
    right_cols,
    right_count,
    right_level,
):
    row, col = lax.axis_index("row"), lax.axis_index("col")
    grid_rows, grid_cols = lax.axis_size("row"), lax.axis_size("col")
    start = col + grid_cols - 1
    near = (((start + (row - start) % grid_rows) % grid_cols) // grid_rows).astype(jnp.int32)
    where = jnp.stack([row, col]).astype(jnp.int32)
    own = list(pack_left(left_blocks, left_rows, left_count, left_level))
    right = (right_blocks, right_cols, right_count, right_level)
    held = [pack_right(which.reshape(1), *right) for which in (near, 1 - near)]

    hops = []
    up, down = list(own), list(own)
    for step in range(1, 4):
        for h in range(2):
            up[h] = shifted(up[h], "col", 1)
            down[h] = shifted(down[h], "col", -1)
        hops.append(
            [(up[0], -step, 0), (up[1], -step, 1), (down[0], step, 0), (down[1], step, 1)]
        )
    hops.append([(shifted(up[0], "col", 1), -4, 0), (shifted(down[1], "col", -1), 4, 1)])
    rights = []
    for s in range(2):
        partner = crossed(held[s], "row", 1)
        other = crossed(held[s], "row", 2)
        corner = crossed(other, "row", 1)
        rights += [held[s], partner, other, corner]

    local = own + held
    own_items = [(own[0], 0, 0), (own[1], 0, 1)]
    total = multiply(where, own_items + hops[0], rights[:4], None, False, local)
    total = multiply(where, hops[1], rights, total, False, local)
    total = multiply(where, hops[2], rights[4:], total, False, local)
    return multiply(where, hops[3], rights[4:], total, True, local)


def solution(mesh):
    in_specs = (
        P(("kpt", "row"), "col", None, None, None, None),
        P(("kpt", "row"), "col", None),
        P(("kpt", "row"), "col"),
        P(("kpt", "row"), "col", None),
        P("kpt", "row", "col", None, None, None, None),
        P("kpt", "row", "col", None),
        P("kpt", "row", "col"),
        P("kpt", "row", "col", None),
    )
    out_specs = P(("kpt", "row"), "col", None, None, None)

    return jax.shard_map(body, mesh=mesh, in_specs=in_specs, out_specs=out_specs, check_vma=False)
```

time: 411 us -> 118 us (0.29)
  other arithmetic: 133 us -> 0.07 us
  local copies, waits for them, and re-layouts: 99.8 us -> 0 us
  starting transfers between devices: 85.8 us -> 30.8 us
  Pallas kernels: 0 us -> 36.1 us
  matrix products: 20.2 us -> 0 us
  waiting for transfers between devices: 69 us -> 50 us
    scatter-add x8 -> x0, other arithmetic: 81.7 us -> none  [pair_products(): total.at[row_index, col_index].add(product.reshape(-1, 2, width, width))]
    ppermute x72 -> x20, starting transfers between devices: 85.8 us -> 30.8 us  [the longest x14 17.9 us: shifted(): lax.ppermute(value, axis, [(i, (i + steps) % count) for i in range(count)])]
    pallas_call x0 -> x7, Pallas kernels: none -> 36.1 us  [the longest x4 29.2 us: multiply(): pl.pallas_call(kernel, out_shape=out_shape, in_specs=in_specs, out_specs=...]
    another operation x56 -> x0, local copies, waits for them, and re-layouts: 31 us -> none
    sub x8 -> x0, local copies, waits for them, and re-layouts: 22.2 us -> none  [pair_products(): real_part = terms[:, :, :, 0, 0] - terms[:, :, :, 1, 1]]
    sub x8 -> x0, other arithmetic: 22.2 us -> none  [pair_products(): real_part = terms[:, :, :, 0, 0] - terms[:, :, :, 1, 1]]
    dot_general x8 -> x0, matrix products: 20.2 us -> none  [pair_products(): jnp.einsum('kmcij,kndjl->kmncdil', left_blocks, right_blocks, preferred_e...]
    ppermute x72 -> x20, waiting for transfers between devices: 69 us -> 50 us  [the longest x14 39.9 us: shifted(): lax.ppermute(value, axis, [(i, (i + steps) % count) for i in range(count)])]
  transfers between devices with their start and end apart: 72 -> 20, of which waited for: 19 -> 7; matrix products, arithmetic and copies ran while one was open for 46% -> 0% of each run, Pallas kernels for 0% -> 23%
where the time goes in v1:
time: 118 us; the launch traced here: 117 us
  waiting for transfers between devices  50 us (42%)
  Pallas kernels  36.1 us (31%)
  starting transfers between devices  30.8 us (26%)
    ppermute x14, waiting for transfers between devices, shifted(): lax.ppermute(value, axis, [(i, (i + steps) % count) for i in range(count)])  39.9 us
    pallas_call x4, Pallas kernels, multiply(): pl.pallas_call(kernel, out_shape=out_shape, in_specs=in_specs, out_specs=...  29.2 us
    ppermute x14, starting transfers between devices, shifted(): lax.ppermute(value, axis, [(i, (i + steps) % count) for i in range(count)])  17.9 us
    ppermute x6, starting transfers between devices, crossed(): return lax.ppermute(value, axis, [(i, i ^ bit) for i in range(count)])  12.9 us
    ppermute x6, waiting for transfers between devices, crossed(): return lax.ppermute(value, axis, [(i, i ^ bit) for i in range(count)])  10.1 us
    pallas_call x2, Pallas kernels, pack_right(): pl.pallas_call(pack_right_kernel, out_shape=pltpu.VMEM((PANEL + META, BS)...  3.95 us
    pallas_call x1, Pallas kernels, pack_left(): pl.pallas_call(pack_left_kernel, out_shape=(shape, shape), in_specs=[pl.B...  2.9 us
  transfers between devices with their start and end apart: 20, of which 7 were waited for; matrix products, arithmetic and copies ran while one was open for 0% of the time, Pallas kernels for 23%

profile of v1, /device:TPU:1, one launch (start us, length us, event | category | flops | bytes accessed | tf_op | source)
XLA Modules:
  0.0 117.2 jit_solution(11229169806438575794)
XLA Ops:
  0.0 2.9 %shard_map.82 = (bf16[2064,128]{1,0:T(8,128)(2,1)}, bf16[2064,128]{1,0:T(8,128)(2,1)}) custom-call(s32[2,8]{1,0:T(2,128)} %bitcast.30, s32[1,8]{1,0:T(1,128)} %count_ref.1, s32[2,8]{1,0:T(2,128)} %bitcast.31, bf16[4096,128]{1,0:T(8,128)(2,1)} %bitcast.23), custom_call_target="tpu_custom_call" | custom-call | tf_op jit(solution)/shard_map/pallas_call | solution.py:57
  2.9 2.5 %collective-permute-start = (bf16[2064,128]{1,0:T(8,128)(2,1)}, bf16[2064,128]{1,0:T(8,128)(2,1)}, u32[]{:S(2)}, u32[]{:S(2)}) collective-permute-start(bf16[2064,128]{1,0:T(8,128)(2,1)} %get-tuple-element.7.refs_1_), channel_id=1, source_target_pairs={{0,1},{1,2},{2,3},{3,4},{4,5},{5,6},{6,7},{7,0},{8,9},{9,10},{10,1... | collective-permute-start | bytes 1585160 | tf_op jit(solution)/shard_map/ppermute | solution.py:100
  5.4 1.6 %collective-permute-start.11 = (bf16[2064,128]{1,0:T(8,128)(2,1)}, bf16[2064,128]{1,0:T(8,128)(2,1)}, u32[]{:S(2)}, u32[]{:S(2)}) collective-permute-start(bf16[2064,128]{1,0:T(8,128)(2,1)} %get-tuple-element.8.refs_2_), channel_id=1, source_target_pairs={{0,1},{1,2},{2,3},{3,4},{4,5},{5,6},{6,7},{7,0},{8,9},{9,10},{10,1... | collective-permute-start | bytes 1585160 | tf_op jit(solution)/shard_map/ppermute | solution.py:100
  7.1 2.5 %collective-permute-start.14 = (bf16[2064,128]{1,0:T(8,128)(2,1)}, bf16[2064,128]{1,0:T(8,128)(2,1)}, u32[]{:S(2)}, u32[]{:S(2)}) collective-permute-start(bf16[2064,128]{1,0:T(8,128)(2,1)} %get-tuple-element.7.refs_1_), channel_id=1, source_target_pairs={{0,7},{1,0},{2,1},{3,2},{4,3},{5,4},{6,5},{7,6},{8,15},{9,8},{10,9... | collective-permute-start | bytes 1585160 | tf_op jit(solution)/shard_map/ppermute | solution.py:100
  9.6 2.0 %shard_map.84.refs_7_.refs_5_ = bf16[4112,128]{1,0:T(8,128)(2,1)S(1)} custom-call(s32[1]{0:T(128)} %bitcast.15.which_ref, s32[2,2,8]{2,1,0:T(2,128)} %bitcast.24, s32[2,1,8]{2,1,0:T(1,128)} %bitcast.28, s32[2,2,8]{2,1,0:T(2,128)} %bitcast.26, bf16[2,4096,128]{2,1,0:T(8,128)(2,1)} %bitcast.21), custom_call_target="tpu_custom_call" | custom-call | tf_op jit(solution)/shard_map/pallas_call | solution.py:82
  11.5 1.3 %collective-permute-start.18 = (bf16[4112,128]{1,0:T(8,128)(2,1)S(1)}, bf16[4112,128]{1,0:T(8,128)(2,1)S(1)}, u32[]{:S(2)}, u32[]{:S(2)}) collective-permute-start(bf16[4112,128]{1,0:T(8,128)(2,1)S(1)} %shard_map.84.refs_7_.refs_5_), channel_id=1, source_target_pairs={{0,16},{8,24},{16,0},{24,8},{1,17},{9,25},{17,1},{25,9},{2,18},{10... | collective-permute-start | bytes 3158024 | tf_op jit(solution)/shard_map/ppermute | solution.py:105
  12.8 1.2 %collective-permute-start.17 = (bf16[4112,128]{1,0:T(8,128)(2,1)S(1)}, bf16[4112,128]{1,0:T(8,128)(2,1)}, u32[]{:S(2)}, u32[]{:S(2)}) collective-permute-start(bf16[4112,128]{1,0:T(8,128)(2,1)S(1)} %shard_map.84.refs_7_.refs_5_), channel_id=1, source_target_pairs={{0,8},{8,0},{16,24},{24,16},{1,9},{9,1},{17,25},{25,17},{2,10},{10... | collective-permute-start | bytes 3158024 | tf_op jit(solution)/shard_map/ppermute | solution.py:105
  14.1 2.0 %shard_map.83.refs_9_.refs_5_.refs_3_ = bf16[4112,128]{1,0:T(8,128)(2,1)S(1)} custom-call(s32[1]{0:T(128)} %bitcast.7.which_ref, s32[2,2,8]{2,1,0:T(2,128)} %bitcast.25, s32[2,1,8]{2,1,0:T(1,128)} %bitcast.29, s32[2,2,8]{2,1,0:T(2,128)} %bitcast.27, bf16[2,4096,128]{2,1,0:T(8,128)(2,1)} %bitcast.22), custom_call_target="tpu_custom_call" | custom-call | tf_op jit(solution)/shard_map/pallas_call | solution.py:82
  16.1 5.4 %collective-permute-done.refs_3_ = bf16[2064,128]{1,0:T(8,128)(2,1)} collective-permute-done((bf16[2064,128]{1,0:T(8,128)(2,1)}, bf16[2064,128]{1,0:T(8,128)(2,1)}, u32[]{:S(2)}, u32[]{:S(2)}) %collective-permute-start) | collective-permute-done | bytes 528416 | tf_op jit(solution)/shard_map/ppermute | solution.py:100
  21.4 1.2 %collective-permute-start.9 = (bf16[4112,128]{1,0:T(8,128)(2,1)S(1)}, bf16[4112,128]{1,0:T(8,128)(2,1)S(1)}, u32[]{:S(2)}, u32[]{:S(2)}) collective-permute-start(bf16[4112,128]{1,0:T(8,128)(2,1)S(1)} %shard_map.83.refs_9_.refs_5_.refs_3_), channel_id=1, source_target_pairs={{0,16},{8,24},{16,0},{24,8},{1,17},{9,25},{17,1},{25,9},{2,18},{10... | collective-permute-start | bytes 3158024 | tf_op jit(solution)/shard_map/ppermute | solution.py:105
  22.6 10.1 %collective-permute-done.11.refs_4_ = bf16[2064,128]{1,0:T(8,128)(2,1)} collective-permute-done((bf16[2064,128]{1,0:T(8,128)(2,1)}, bf16[2064,128]{1,0:T(8,128)(2,1)}, u32[]{:S(2)}, u32[]{:S(2)}) %collective-permute-start.11) | collective-permute-done | bytes 528416 | tf_op jit(solution)/shard_map/ppermute | solution.py:100
  32.7 1.2 %collective-permute-start.4 = (bf16[2064,128]{1,0:T(8,128)(2,1)}, bf16[2064,128]{1,0:T(8,128)(2,1)S(1)}, u32[]{:S(2)}, u32[]{:S(2)}) collective-permute-start(bf16[2064,128]{1,0:T(8,128)(2,1)} %get-tuple-element.8.refs_2_), channel_id=1, source_target_pairs={{0,7},{1,0},{2,1},{3,2},{4,3},{5,4},{6,5},{7,6},{8,15},{9,8},{10,9... | collective-permute-start | bytes 1585160 | tf_op jit(solution)/shard_map/ppermute | solution.py:100
  33.9 0.0 collective-permute-done.14.refs_5_
  33.9 1.8 %collective-permute-start.8 = (bf16[4112,128]{1,0:T(8,128)(2,1)S(1)}, bf16[4112,128]{1,0:T(8,128)(2,1)S(1)}, u32[]{:S(2)}, u32[]{:S(2)}) collective-permute-start(bf16[4112,128]{1,0:T(8,128)(2,1)S(1)} %shard_map.83.refs_9_.refs_5_.refs_3_), channel_id=1, source_target_pairs={{0,8},{8,0},{16,24},{24,16},{1,9},{9,1},{17,25},{25,17},{2,10},{10... | collective-permute-start | bytes 3158024 | tf_op jit(solution)/shard_map/ppermute | solution.py:105
  35.7 9.5 %collective-permute-done.4.refs_6_ = bf16[2064,128]{1,0:T(8,128)(2,1)S(1)} collective-permute-done((bf16[2064,128]{1,0:T(8,128)(2,1)}, bf16[2064,128]{1,0:T(8,128)(2,1)S(1)}, u32[]{:S(2)}, u32[]{:S(2)}) %collective-permute-start.4) | collective-permute-done | bytes 528416 | tf_op jit(solution)/shard_map/ppermute | solution.py:100
  45.3 0.0 collective-permute-start.1
  45.3 0.0 collective-permute-done.18.refs_9_.refs_7_
  45.3 2.7 %collective-permute-start.5 = (bf16[2064,128]{1,0:T(8,128)(2,1)S(1)}, bf16[2064,128]{1,0:T(8,128)(2,1)S(1)}, u32[]{:S(2)}, u32[]{:S(2)}) collective-permute-start(bf16[2064,128]{1,0:T(8,128)(2,1)S(1)} %collective-permute-done.4.refs_6_), channel_id=1, source_target_pairs={{0,7},{1,0},{2,1},{3,2},{4,3},{5,4},{6,5},{7,6},{8,15},{9,8},{10,9... | collective-permute-start | bytes 1585160 | tf_op jit(solution)/shard_map/ppermute | solution.py:100
  48.0 0.0 collective-permute-done.17.refs_8_.refs_6_
  48.0 0.0 collective-permute-start.12
  48.0 10.1 %collective-permute-done.9.refs_11_.refs_7_.refs_5_ = bf16[4112,128]{1,0:T(8,128)(2,1)S(1)} collective-permute-done((bf16[4112,128]{1,0:T(8,128)(2,1)S(1)}, bf16[4112,128]{1,0:T(8,128)(2,1)S(1)}, u32[]{:S(2)}, u32[]{:S(2)}) %collective-permute-start.9) | collective-permute-done | bytes 1052704 | tf_op jit(solution)/shard_map/ppermute | solution.py:105
  58.0 1.8 %collective-permute-start.19 = (bf16[4112,128]{1,0:T(8,128)(2,1)S(1)}, bf16[4112,128]{1,0:T(8,128)(2,1)S(1)}, u32[]{:S(2)}, u32[]{:S(2)}) collective-permute-start(bf16[4112,128]{1,0:T(8,128)(2,1)S(1)} %collective-permute-done.18.refs_9_.refs_7_), channel_id=1, source_target_pairs={{0,8},{8,0},{16,24},{24,16},{1,9},{9,1},{17,25},{25,17},{2,10},{10... | collective-permute-start | bytes 3158024 | tf_op jit(solution)/shard_map/ppermute | solution.py:105
  59.9 0.0 collective-permute-done.8.refs_10_.refs_6_.refs_4_
  59.9 1.4 %collective-permute-start.15 = (bf16[2064,128]{1,0:T(8,128)(2,1)}, bf16[2064,128]{1,0:T(8,128)(2,1)S(1)}, u32[]{:S(2)}, u32[]{:S(2)}) collective-permute-start(bf16[2064,128]{1,0:T(8,128)(2,1)} %collective-permute-done.14.refs_5_), channel_id=1, source_target_pairs={{0,7},{1,0},{2,1},{3,2},{4,3},{5,4},{6,5},{7,6},{8,15},{9,8},{10,9... | collective-permute-start | bytes 1585160 | tf_op jit(solution)/shard_map/ppermute | solution.py:100
  61.2 0.0 collective-permute-done.1.refs_1_
  61.2 0.1 collective-permute-start.2
  61.3 0.0 collective-permute-done.5.refs_4_
  61.3 2.6 %collective-permute-start.6 = (bf16[2064,128]{1,0:T(8,128)(2,1)S(1)}, bf16[2064,128]{1,0:T(8,128)(2,1)S(1)}, u32[]{:S(2)}, u32[]{:S(2)}) collective-permute-start(bf16[2064,128]{1,0:T(8,128)(2,1)S(1)} %collective-permute-done.5.refs_4_), channel_id=1, source_target_pairs={{0,7},{1,0},{2,1},{3,2},{4,3},{5,4},{6,5},{7,6},{8,15},{9,8},{10,9... | collective-permute-start | bytes 1585160 | tf_op jit(solution)/shard_map/ppermute | solution.py:100
  63.9 5.6 %collective-permute-done.12.refs_2_ = bf16[2064,128]{1,0:T(8,128)(2,1)S(1)} collective-permute-done((bf16[2064,128]{1,0:T(8,128)(2,1)}, bf16[2064,128]{1,0:T(8,128)(2,1)S(1)}, u32[]{:S(2)}, u32[]{:S(2)}) %collective-permute-start.12) | collective-permute-done | bytes 528416 | tf_op jit(solution)/shard_map/ppermute | solution.py:100
  69.5 5.5 %collective-permute-start.10 = (bf16[4112,128]{1,0:T(8,128)(2,1)S(1)}, bf16[4112,128]{1,0:T(8,128)(2,1)S(1)}, u32[]{:S(2)}, u32[]{:S(2)}) collective-permute-start(bf16[4112,128]{1,0:T(8,128)(2,1)S(1)} %collective-permute-done.9.refs_11_.refs_7_.refs_5_), channel_id=1, source_target_pairs={{0,8},{8,0},{16,24},{24,16},{1,9},{9,1},{17,25},{25,17},{2,10},{10... | collective-permute-start | bytes 3158024 | tf_op jit(solution)/shard_map/ppermute | solution.py:105
  75.0 0.0 collective-permute-done.15.refs_3_
  75.0 0.0 collective-permute-start.13
  75.0 5.8 %collective-permute-done.2.refs_1_ = bf16[2064,128]{1,0:T(8,128)(2,1)S(1)} collective-permute-done((bf16[2064,128]{1,0:T(8,128)(2,1)S(1)}, bf16[2064,128]{1,0:T(8,128)(2,1)S(1)}, u32[]{:S(2)}, u32[]{:S(2)}) %collective-permute-start.2) | collective-permute-done | bytes 528416 | tf_op jit(solution)/shard_map/ppermute | solution.py:100
  80.8 0.6 collective-permute-start.16
  81.4 3.5 %collective-permute-done.6.refs_4_ = bf16[2064,128]{1,0:T(8,128)(2,1)S(1)} collective-permute-done((bf16[2064,128]{1,0:T(8,128)(2,1)S(1)}, bf16[2064,128]{1,0:T(8,128)(2,1)S(1)}, u32[]{:S(2)}, u32[]{:S(2)}) %collective-permute-start.6) | collective-permute-done | bytes 528416 | tf_op jit(solution)/shard_map/ppermute | solution.py:100
  85.0 0.8 collective-permute-start.3
  85.8 0.0 collective-permute-done.19.refs_10_.refs_8_
  85.8 1.9 %collective-permute-start.7 = (bf16[2064,128]{1,0:T(8,128)(2,1)S(1)}, bf16[2064,128]{1,0:T(8,128)(2,1)S(1)}, u32[]{:S(2)}, u32[]{:S(2)}) collective-permute-start(bf16[2064,128]{1,0:T(8,128)(2,1)S(1)} %collective-permute-done.6.refs_4_), channel_id=1, source_target_pairs={{0,7},{1,0},{2,1},{3,2},{4,3},{5,4},{6,5},{7,6},{8,15},{9,8},{10,9... | collective-permute-start | bytes 1585160 | tf_op jit(solution)/shard_map/ppermute | solution.py:100
  87.6 0.1 pad_add_fusion.refs_0_
  87.7 10.0 %shard_map.85.refs_13_ = f32[8,8,2,128,128]{4,3,2,1,0:T(8,128)S(1)} custom-call(s32[2]{0:T(128)S(1)} %pad_add_fusion.refs_0_, bf16[2064,128]{1,0:T(8,128)(2,1)} %get-tuple-element.7.refs_1_, bf16[2064,128]{1,0:T(8,128)(2,1)} %get-tuple-element.8.refs_2_, bf16[2064,128]{1,0:T(8,128)(2,1)} %collective-permute-done.refs_3_, ...), custom_call_target="tpu_custom_call" | custom-call | tf_op jit(solution)/shard_map/pallas_call | solution.py:272
  97.7 0.0 collective-permute-done.10.refs_12_.refs_8_.refs_6_
  97.7 7.0 %shard_map.86.refs_9_ = f32[8,8,2,128,128]{4,3,2,1,0:T(8,128)S(1)} custom-call(s32[2]{0:T(128)S(1)} %pad_add_fusion.refs_0_, bf16[2064,128]{1,0:T(8,128)(2,1)S(1)} %collective-permute-done.1.refs_1_, bf16[2064,128]{1,0:T(8,128)(2,1)S(1)} %collective-permute-done.12.refs_2_, ...), custom_call_target="tpu_custom_call", output_to_operand_aliasing={{}: (13, {})} | custom-call | tf_op jit(solution)/shard_map/pallas_call | solution.py:272
  104.7 0.0 collective-permute-done.13.refs_2_
  104.8 0.0 collective-permute-done.16.refs_3_
  104.8 6.6 %shard_map.87.refs_7_ = f32[8,8,2,128,128]{4,3,2,1,0:T(8,128)S(1)} custom-call(s32[2]{0:T(128)S(1)} %pad_add_fusion.refs_0_, bf16[2064,128]{1,0:T(8,128)(2,1)S(1)} %collective-permute-done.2.refs_1_, bf16[2064,128]{1,0:T(8,128)(2,1)S(1)} %collective-permute-done.13.refs_2_, ...), custom_call_target="tpu_custom_call", output_to_operand_aliasing={{}: (9, {})} | custom-call | tf_op jit(solution)/shard_map/pallas_call | solution.py:272
  111.4 0.0 collective-permute-done.3.refs_1_
  111.4 0.0 collective-permute-done.7.refs_2_
  111.4 5.6 %shard_map.88 = bf16[8,8,2,128,128]{4,3,2,1,0:T(8,128)(2,1)} custom-call(s32[2]{0:T(128)S(1)} %pad_add_fusion.refs_0_, bf16[2064,128]{1,0:T(8,128)(2,1)S(1)} %collective-permute-done.3.refs_1_, bf16[2064,128]{1,0:T(8,128)(2,1)S(1)} %collective-permute-done.7.refs_2_, bf16[4112,128]{1,0:T(8,128)(2,1)S(1)} %shard_map.83.refs_9_.refs_5_.refs_3_, ...), custom_call_target="tpu_custom_call" | custom-call | tf_op jit(solution)/shard_map/pallas_call | solution.py:272
Async XLA Ops:
  2.9 18.5 %collective-permute-start = (bf16[2064,128]{1,0:T(8,128)(2,1)}, bf16[2064,128]{1,0:T(8,128)(2,1)}, u32[]{:S(2)}, u32[]{:S(2)}) collective-permute-start(bf16[2064,128]{1,0:T(8,128)(2,1)} %get-tuple-element.7.refs_1_), channel_id=1, source_target_pairs={{0,1},{1,2},{2,3},{3,4},{4,5},{5,6},{6,7},{7,0},{8,9},{9,10},{10,1... | collective-permute-start | bytes 1585160 | tf_op jit(solution)/shard_map/ppermute | solution.py:100
  5.4 27.3 %collective-permute-start.11 = (bf16[2064,128]{1,0:T(8,128)(2,1)}, bf16[2064,128]{1,0:T(8,128)(2,1)}, u32[]{:S(2)}, u32[]{:S(2)}) collective-permute-start(bf16[2064,128]{1,0:T(8,128)(2,1)} %get-tuple-element.8.refs_2_), channel_id=1, source_target_pairs={{0,1},{1,2},{2,3},{3,4},{4,5},{5,6},{6,7},{7,0},{8,9},{9,10},{10,1... | collective-permute-start | bytes 1585160 | tf_op jit(solution)/shard_map/ppermute | solution.py:100
  7.1 26.8 %collective-permute-start.14 = (bf16[2064,128]{1,0:T(8,128)(2,1)}, bf16[2064,128]{1,0:T(8,128)(2,1)}, u32[]{:S(2)}, u32[]{:S(2)}) collective-permute-start(bf16[2064,128]{1,0:T(8,128)(2,1)} %get-tuple-element.7.refs_1_), channel_id=1, source_target_pairs={{0,7},{1,0},{2,1},{3,2},{4,3},{5,4},{6,5},{7,6},{8,15},{9,8},{10,9... | collective-permute-start | bytes 1585160 | tf_op jit(solution)/shard_map/ppermute | solution.py:100
  11.5 33.7 %collective-permute-start.18 = (bf16[4112,128]{1,0:T(8,128)(2,1)S(1)}, bf16[4112,128]{1,0:T(8,128)(2,1)S(1)}, u32[]{:S(2)}, u32[]{:S(2)}) collective-permute-start(bf16[4112,128]{1,0:T(8,128)(2,1)S(1)} %shard_map.84.refs_7_.refs_5_), channel_id=1, source_target_pairs={{0,16},{8,24},{16,0},{24,8},{1,17},{9,25},{17,1},{25,9},{2,18},{10... | collective-permute-start | bytes 3158024 | tf_op jit(solution)/shard_map/ppermute | solution.py:105
  12.8 35.1 %collective-permute-start.17 = (bf16[4112,128]{1,0:T(8,128)(2,1)S(1)}, bf16[4112,128]{1,0:T(8,128)(2,1)}, u32[]{:S(2)}, u32[]{:S(2)}) collective-permute-start(bf16[4112,128]{1,0:T(8,128)(2,1)S(1)} %shard_map.84.refs_7_.refs_5_), channel_id=1, source_target_pairs={{0,8},{8,0},{16,24},{24,16},{1,9},{9,1},{17,25},{25,17},{2,10},{10... | collective-permute-start | bytes 3158024 | tf_op jit(solution)/shard_map/ppermute | solution.py:105
  21.4 36.6 %collective-permute-start.9 = (bf16[4112,128]{1,0:T(8,128)(2,1)S(1)}, bf16[4112,128]{1,0:T(8,128)(2,1)S(1)}, u32[]{:S(2)}, u32[]{:S(2)}) collective-permute-start(bf16[4112,128]{1,0:T(8,128)(2,1)S(1)} %shard_map.83.refs_9_.refs_5_.refs_3_), channel_id=1, source_target_pairs={{0,16},{8,24},{16,0},{24,8},{1,17},{9,25},{17,1},{25,9},{2,18},{10... | collective-permute-start | bytes 3158024 | tf_op jit(solution)/shard_map/ppermute | solution.py:105
  32.7 12.5 %collective-permute-start.4 = (bf16[2064,128]{1,0:T(8,128)(2,1)}, bf16[2064,128]{1,0:T(8,128)(2,1)S(1)}, u32[]{:S(2)}, u32[]{:S(2)}) collective-permute-start(bf16[2064,128]{1,0:T(8,128)(2,1)} %get-tuple-element.8.refs_2_), channel_id=1, source_target_pairs={{0,7},{1,0},{2,1},{3,2},{4,3},{5,4},{6,5},{7,6},{8,15},{9,8},{10,9... | collective-permute-start | bytes 1585160 | tf_op jit(solution)/shard_map/ppermute | solution.py:100
  33.9 25.9 %collective-permute-start.8 = (bf16[4112,128]{1,0:T(8,128)(2,1)S(1)}, bf16[4112,128]{1,0:T(8,128)(2,1)S(1)}, u32[]{:S(2)}, u32[]{:S(2)}) collective-permute-start(bf16[4112,128]{1,0:T(8,128)(2,1)S(1)} %shard_map.83.refs_9_.refs_5_.refs_3_), channel_id=1, source_target_pairs={{0,8},{8,0},{16,24},{24,16},{1,9},{9,1},{17,25},{25,17},{2,10},{10... | collective-permute-start | bytes 3158024 | tf_op jit(solution)/shard_map/ppermute | solution.py:105
  45.3 16.0 %collective-permute-start.1 = (bf16[2064,128]{1,0:T(8,128)(2,1)}, bf16[2064,128]{1,0:T(8,128)(2,1)S(1)}, u32[]{:S(2)}, u32[]{:S(2)}) collective-permute-start(bf16[2064,128]{1,0:T(8,128)(2,1)} %collective-permute-done.refs_3_), channel_id=1, source_target_pairs={{0,1},{1,2},{2,3},{3,4},{4,5},{5,6},{6,7},{7,0},{8,9},{9,10},{10,1... | collective-permute-start | bytes 1585160 | tf_op jit(solution)/shard_map/ppermute | solution.py:100
  45.3 16.1 %collective-permute-start.5 = (bf16[2064,128]{1,0:T(8,128)(2,1)S(1)}, bf16[2064,128]{1,0:T(8,128)(2,1)S(1)}, u32[]{:S(2)}, u32[]{:S(2)}) collective-permute-start(bf16[2064,128]{1,0:T(8,128)(2,1)S(1)} %collective-permute-done.4.refs_6_), channel_id=1, source_target_pairs={{0,7},{1,0},{2,1},{3,2},{4,3},{5,4},{6,5},{7,6},{8,15},{9,8},{10,9... | collective-permute-start | bytes 1585160 | tf_op jit(solution)/shard_map/ppermute | solution.py:100
  48.0 21.5 %collective-permute-start.12 = (bf16[2064,128]{1,0:T(8,128)(2,1)}, bf16[2064,128]{1,0:T(8,128)(2,1)S(1)}, u32[]{:S(2)}, u32[]{:S(2)}) collective-permute-start(bf16[2064,128]{1,0:T(8,128)(2,1)} %collective-permute-done.11.refs_4_), channel_id=1, source_target_pairs={{0,1},{1,2},{2,3},{3,4},{4,5},{5,6},{6,7},{7,0},{8,9},{9,10},{10,1... | collective-permute-start | bytes 1585160 | tf_op jit(solution)/shard_map/ppermute | solution.py:100
  58.0 27.7 %collective-permute-start.19 = (bf16[4112,128]{1,0:T(8,128)(2,1)S(1)}, bf16[4112,128]{1,0:T(8,128)(2,1)S(1)}, u32[]{:S(2)}, u32[]{:S(2)}) collective-permute-start(bf16[4112,128]{1,0:T(8,128)(2,1)S(1)} %collective-permute-done.18.refs_9_.refs_7_), channel_id=1, source_target_pairs={{0,8},{8,0},{16,24},{24,16},{1,9},{9,1},{17,25},{25,17},{2,10},{10... | collective-permute-start | bytes 3158024 | tf_op jit(solution)/shard_map/ppermute | solution.py:105
  59.9 15.1 %collective-permute-start.15 = (bf16[2064,128]{1,0:T(8,128)(2,1)}, bf16[2064,128]{1,0:T(8,128)(2,1)S(1)}, u32[]{:S(2)}, u32[]{:S(2)}) collective-permute-start(bf16[2064,128]{1,0:T(8,128)(2,1)} %collective-permute-done.14.refs_5_), channel_id=1, source_target_pairs={{0,7},{1,0},{2,1},{3,2},{4,3},{5,4},{6,5},{7,6},{8,15},{9,8},{10,9... | collective-permute-start | bytes 1585160 | tf_op jit(solution)/shard_map/ppermute | solution.py:100
  61.2 19.6 %collective-permute-start.2 = (bf16[2064,128]{1,0:T(8,128)(2,1)S(1)}, bf16[2064,128]{1,0:T(8,128)(2,1)S(1)}, u32[]{:S(2)}, u32[]{:S(2)}) collective-permute-start(bf16[2064,128]{1,0:T(8,128)(2,1)S(1)} %collective-permute-done.1.refs_1_), channel_id=1, source_target_pairs={{0,1},{1,2},{2,3},{3,4},{4,5},{5,6},{6,7},{7,0},{8,9},{9,10},{10,1... | collective-permute-start | bytes 1585160 | tf_op jit(solution)/shard_map/ppermute | solution.py:100
  61.3 23.6 %collective-permute-start.6 = (bf16[2064,128]{1,0:T(8,128)(2,1)S(1)}, bf16[2064,128]{1,0:T(8,128)(2,1)S(1)}, u32[]{:S(2)}, u32[]{:S(2)}) collective-permute-start(bf16[2064,128]{1,0:T(8,128)(2,1)S(1)} %collective-permute-done.5.refs_4_), channel_id=1, source_target_pairs={{0,7},{1,0},{2,1},{3,2},{4,3},{5,4},{6,5},{7,6},{8,15},{9,8},{10,9... | collective-permute-start | bytes 1585160 | tf_op jit(solution)/shard_map/ppermute | solution.py:100
  69.5 28.3 %collective-permute-start.10 = (bf16[4112,128]{1,0:T(8,128)(2,1)S(1)}, bf16[4112,128]{1,0:T(8,128)(2,1)S(1)}, u32[]{:S(2)}, u32[]{:S(2)}) collective-permute-start(bf16[4112,128]{1,0:T(8,128)(2,1)S(1)} %collective-permute-done.9.refs_11_.refs_7_.refs_5_), channel_id=1, source_target_pairs={{0,8},{8,0},{16,24},{24,16},{1,9},{9,1},{17,25},{25,17},{2,10},{10... | collective-permute-start | bytes 3158024 | tf_op jit(solution)/shard_map/ppermute | solution.py:105
  75.0 29.7 %collective-permute-start.13 = (bf16[2064,128]{1,0:T(8,128)(2,1)S(1)}, bf16[2064,128]{1,0:T(8,128)(2,1)S(1)}, u32[]{:S(2)}, u32[]{:S(2)}) collective-permute-start(bf16[2064,128]{1,0:T(8,128)(2,1)S(1)} %collective-permute-done.12.refs_2_), channel_id=1, source_target_pairs={{0,1},{1,2},{2,3},{3,4},{4,5},{5,6},{6,7},{7,0},{8,9},{9,10},{10,1... | collective-permute-start | bytes 1585160 | tf_op jit(solution)/shard_map/ppermute | solution.py:100
  80.8 24.0 %collective-permute-start.16 = (bf16[2064,128]{1,0:T(8,128)(2,1)S(1)}, bf16[2064,128]{1,0:T(8,128)(2,1)S(1)}, u32[]{:S(2)}, u32[]{:S(2)}) collective-permute-start(bf16[2064,128]{1,0:T(8,128)(2,1)S(1)} %collective-permute-done.15.refs_3_), channel_id=1, source_target_pairs={{0,7},{1,0},{2,1},{3,2},{4,3},{5,4},{6,5},{7,6},{8,15},{9,8},{10,9... | collective-permute-start | bytes 1585160 | tf_op jit(solution)/shard_map/ppermute | solution.py:100
  85.0 26.4 %collective-permute-start.3 = (bf16[2064,128]{1,0:T(8,128)(2,1)S(1)}, bf16[2064,128]{1,0:T(8,128)(2,1)S(1)}, u32[]{:S(2)}, u32[]{:S(2)}) collective-permute-start(bf16[2064,128]{1,0:T(8,128)(2,1)S(1)} %collective-permute-done.2.refs_1_), channel_id=1, source_target_pairs={{0,1},{1,2},{2,3},{3,4},{4,5},{5,6},{6,7},{7,0},{8,9},{9,10},{10,1... | collective-permute-start | bytes 1585160 | tf_op jit(solution)/shard_map/ppermute | solution.py:100
  85.8 25.6 %collective-permute-start.7 = (bf16[2064,128]{1,0:T(8,128)(2,1)S(1)}, bf16[2064,128]{1,0:T(8,128)(2,1)S(1)}, u32[]{:S(2)}, u32[]{:S(2)}) collective-permute-start(bf16[2064,128]{1,0:T(8,128)(2,1)S(1)} %collective-permute-done.6.refs_4_), channel_id=1, source_target_pairs={{0,7},{1,0},{2,1},{3,2},{4,3},{5,4},{6,5},{7,6},{8,15},{9,8},{10,9... | collective-permute-start | bytes 1585160 | tf_op jit(solution)/shard_map/ppermute | solution.py:100

commit v2 on v1

v2 whole, which is shorter than its diff:
```python
import functools

import jax
import jax.numpy as jnp
from jax import lax
from jax.experimental import pallas as pl
from jax.experimental.pallas import tpu as pltpu
from jax.sharding import PartitionSpec as P

GR = 8
KB = 8
BS = 128
LEVEL_CUT = 7
HALF = 4
BLOCK_ROWS = 2 * 2 * BS
META = 16
UNROLL = 4
MIB = 1024 * 1024
PACK_LIMIT = (60, 2)
CHUNK = HALF * BLOCK_ROWS
PANEL = KB * BLOCK_ROWS


def fill_table(table_ref, places, count, level, rows):
    lane = lax.broadcasted_iota(jnp.int32, (META, BS), 1)
    sub = lax.broadcasted_iota(jnp.int32, (META, BS), 0)
    table = jnp.zeros((META, BS), jnp.float32)
    for k in range(rows):
        for m in range(2):
            live = (m < count(k)).astype(jnp.int32)
            for at, value in ((m, places(k, m)), (2 + m, level(k, m)), (4 + m, live)):
                table = jnp.where((sub == k) & (lane == at), value.astype(jnp.float32), table)
    table_ref[...] = table.astype(jnp.bfloat16)


def pack_left_kernel(
    half, rows_hbm, count_hbm, level_hbm, blocks_ref, out_ref, rows_ref, count_ref, level_ref, sem
):
    copies = [
        pltpu.make_async_copy(source, target, sem.at[i])
        for i, (source, target) in enumerate(
            (
                (rows_hbm, rows_ref),
                (count_hbm, count_ref),
                (level_hbm, level_ref),
                (blocks_ref.at[pl.ds(half * CHUNK, CHUNK)], out_ref.at[pl.ds(0, CHUNK)]),
            )
        )
    ]
    for copy in copies:
        copy.start()
    for copy in copies[:3]:
        copy.wait()
    fill_table(
        out_ref.at[pl.ds(CHUNK, META)],
        lambda k, m: rows_ref[m, half * HALF + k],
        lambda k: count_ref[0, half * HALF + k],
        lambda k, m: level_ref[m, half * HALF + k],
        HALF,
    )
    copies[3].wait()


def pack_left(half, blocks, rows, count, level):
    tables = (jnp.swapaxes(rows[0], 0, 1), count, jnp.swapaxes(level[0], 0, 1))
    return pl.pallas_call(
        functools.partial(pack_left_kernel, half),
        out_shape=pltpu.VMEM((CHUNK + META, BS), jnp.bfloat16),
        in_specs=[pl.BlockSpec(memory_space=pltpu.HBM)] * 4,
        out_specs=pl.BlockSpec(memory_space=pltpu.VMEM),
        scratch_shapes=[pltpu.SMEM(table.shape, jnp.int32) for table in tables]
        + [pltpu.SemaphoreType.DMA((4,))],
        compiler_params=pltpu.CompilerParams(vmem_limit_bytes=PACK_LIMIT[half] * MIB),
    )(*tables, blocks.reshape(-1, BS))


def pack_right_kernel(which_ref, cols_ref, count_ref, level_ref, blocks_ref, out_ref, sem):
    which = which_ref[0]
    blocks = pltpu.make_async_copy(blocks_ref.at[which], out_ref.at[pl.ds(0, PANEL)], sem)
    blocks.start()
    fill_table(
        out_ref.at[pl.ds(PANEL, META)],
        lambda k, m: cols_ref[which, m, k],
        lambda k: count_ref[which, 0, k],
        lambda k, m: level_ref[which, m, k],
        KB,
    )
    blocks.wait()


def pack_right(which, blocks, cols, count, level):
    return pl.pallas_call(
        pack_right_kernel,
        out_shape=pltpu.VMEM((PANEL + META, BS), jnp.bfloat16),
        in_specs=[pl.BlockSpec(memory_space=pltpu.SMEM)] * 4
        + [pl.BlockSpec(memory_space=pltpu.HBM)],
        out_specs=pl.BlockSpec(memory_space=pltpu.VMEM),
        scratch_shapes=[pltpu.SemaphoreType.DMA],
        compiler_params=pltpu.CompilerParams(vmem_limit_bytes=2 * MIB),
    )(
        which,
        jnp.swapaxes(cols[:, :, 0], 1, 2),
        jnp.swapaxes(count, 1, 2),
        jnp.swapaxes(level[:, :, 0], 1, 2),
        blocks.reshape(-1, PANEL, BS),
    )


def shifted(value, axis, steps):
    count = lax.axis_size(axis)
    return lax.ppermute(value, axis, [(i, (i + steps) % count) for i in range(count)])


def crossed(value, axis, bit):
    count = lax.axis_size(axis)
    return lax.ppermute(value, axis, [(i, i ^ bit) for i in range(count)])


def kept_pairs(table_smem, left_at, right_at, k, kr, m):
    level = table_smem[left_at, k, 2 + m]
    live = table_smem[left_at, k, 4 + m] > 0
    return [
        live
        & (table_smem[right_at, kr, 4 + q] > 0)
        & (level + table_smem[right_at, kr, 2 + q] >= LEVEL_CUT)
        for q in range(2)
    ]


def add_products(acc_ref, table_smem, left_at, right_at, k, kr, left_part, right_part, mark):
    right = jnp.concatenate(
        [
            jnp.concatenate([right_part(0, 0), right_part(1, 0)], axis=1),
            jnp.concatenate([right_part(0, 1), right_part(1, 1)], axis=1),
        ],
        axis=0,
    )
    for m in range(2):
        row = table_smem[left_at, k, m]
        kept = kept_pairs(table_smem, left_at, right_at, k, kr, m)
        real, imag = left_part(m, 0), left_part(m, 1)
        left = jnp.concatenate(
            [
                jnp.concatenate([real, -imag], axis=1),
                jnp.concatenate([imag, real], axis=1),
            ],
            axis=0,
        )
        product = jnp.dot(left, right, preferred_element_type=jnp.float32)
        for q in range(2):
            col = table_smem[right_at, kr, q]
            weight = kept[q].astype(jnp.float32)
            for part in range(2):
                acc_ref[row, col, part] += weight * product[
                    part * BS : (part + 1) * BS, q * BS : (q + 1) * BS
                ]
            mark(kept[q], row, col)


def tables_to_smem(table_buf, whole_buf, table_smem, sem):
    whole_buf[...] = table_buf[:, : whole_buf.shape[1]].astype(jnp.float32).astype(jnp.int32)
    to_smem = pltpu.make_async_copy(whole_buf, table_smem, sem)
    to_smem.start()
    to_smem.wait()


def right_source(where_ref, offset, grid_rows, grid_cols):
    panel = (where_ref[1] + offset + grid_cols) % grid_cols
    return (panel % grid_rows) ^ where_ref[0]


def multiply_kernel(offsets, halves, first, grid_rows, grid_cols, n_rights, *refs):
    n = len(offsets)
    where_ref = refs[0]
    lefts = refs[1 : 1 + n]
    rights = refs[1 + n : 1 + n + n_rights]
    acc_ref = refs[1 + n + n_rights + (not first)]
    left_buf, right_buf, table_buf, whole_buf, table_smem, data_sem, table_sem, smem_sem = refs[
        2 + n + n_rights + (not first) :
    ]

    def right_copies(i, act):
        source = right_source(where_ref, offsets[i], grid_rows, grid_cols)
        near = -1 <= offsets[i] <= grid_rows - 2
        for s in range(grid_rows):

            @pl.when(source == s)
            def _(s=s):
                act(rights[s if near else n_rights - grid_rows + s])

    for i in range(n):
        pltpu.make_async_copy(
            lefts[i].at[pl.ds(CHUNK, META)], table_buf.at[2 * i], table_sem
        ).start()
        right_copies(
            i,
            lambda src, i=i: pltpu.make_async_copy(
                src.at[pl.ds(PANEL, META)], table_buf.at[2 * i + 1], table_sem
            ).start(),
        )
    for i in range(n):
        pltpu.make_async_copy(lefts[i].at[pl.ds(0, CHUNK)], left_buf.at[i], data_sem.at[i]).start()
        right_copies(
            i,
            lambda src, i=i: pltpu.make_async_copy(
                src.at[pl.ds(halves[i] * CHUNK, CHUNK)], right_buf.at[i], data_sem.at[i]
            ).start(),
        )
    if first:
        acc_ref[...] = jnp.zeros_like(acc_ref)
    pltpu.make_async_copy(table_buf, table_buf, table_sem).wait()
    tables_to_smem(table_buf, whole_buf, table_smem, smem_sem)
    assert all(h == i % 2 for i, h in enumerate(halves))

    def one_item(i, carry):
        pltpu.make_async_copy(left_buf.at[i], left_buf.at[i], data_sem.at[i]).wait()
        pltpu.make_async_copy(right_buf.at[i], right_buf.at[i], data_sem.at[i]).wait()

        def one_kb(k, carry):
            base = pl.multiple_of(k * BLOCK_ROWS, BLOCK_ROWS)
            add_products(
                acc_ref,
                table_smem,
                2 * i,
                2 * i + 1,
                k,
                (i % 2) * HALF + k,
                lambda slot, part: left_buf[i, pl.ds(base + (2 * slot + part) * BS, BS), :],
                lambda slot, part: right_buf[i, pl.ds(base + (2 * slot + part) * BS, BS), :],
                lambda kept, row, col: None,
            )
            return carry

        return lax.fori_loop(0, HALF, one_kb, carry, unroll=UNROLL)

    lax.fori_loop(0, n, one_item, 0)


def fetch_kernel(offset, grid_rows, grid_cols, where_ref, *refs):
    *rights, out_ref, sem = refs
    source = right_source(where_ref, offset, grid_rows, grid_cols)
    for s in range(grid_rows):

        @pl.when(source == s)
        def _(s=s):
            pltpu.make_async_copy(rights[s], out_ref, sem).start()

    pltpu.make_async_copy(out_ref, out_ref, sem).wait()


def spaces(operands, local):
    return [
        pl.BlockSpec(memory_space=pltpu.VMEM if any(v is own for own in local) else pltpu.HBM)
        for v in operands
    ]


def fetch(where, offset, rights, local):
    kernel = functools.partial(
        fetch_kernel, offset, lax.axis_size("row"), lax.axis_size("col")
    )
    return pl.pallas_call(
        kernel,
        out_shape=pltpu.VMEM((PANEL + META, BS), jnp.bfloat16),
        in_specs=[pl.BlockSpec(memory_space=pltpu.SMEM)] + spaces(rights, local),
        out_specs=pl.BlockSpec(memory_space=pltpu.VMEM),
        scratch_shapes=[pltpu.SemaphoreType.DMA],
        compiler_params=pltpu.CompilerParams(vmem_limit_bytes=2 * MIB),
    )(where, *rights)


def flush_kernel(acc_ref, out_ref, stage_ref, sem):
    for r in range(GR):
        stage_ref[r] = acc_ref[r].astype(jnp.bfloat16)
        pltpu.make_async_copy(stage_ref.at[r], out_ref.at[r], sem).start()
    pltpu.make_async_copy(stage_ref, out_ref, sem).wait()


def flush(total):
    return pl.pallas_call(
        flush_kernel,
        out_shape=jax.ShapeDtypeStruct(total.shape, jnp.bfloat16),
        in_specs=[pl.BlockSpec(memory_space=pltpu.VMEM)],
        out_specs=pl.BlockSpec(memory_space=pltpu.HBM),
        scratch_shapes=[
            pltpu.VMEM(total.shape, jnp.bfloat16),
            pltpu.SemaphoreType.DMA,
        ],
        compiler_params=pltpu.CompilerParams(vmem_limit_bytes=6 * MIB),
    )(total)


def finish_kernel(
    up_ref, down_ref, right_ref, acc_ref, old_ref, out_ref,
    stage_ref, table_buf, whole_buf, table_smem, flag_smem, list_smem, out_sem, smem_sem,
):
    lefts = (up_ref, down_ref)
    for h in range(2):
        table_buf[h] = lefts[h][pl.ds(CHUNK, META), :]
    table_buf[2] = right_ref[pl.ds(PANEL, META), :]
    for at in range(GR * KB):
        flag_smem[at] = 0
    list_smem[GR * KB] = 0
    tables_to_smem(table_buf, whole_buf, table_smem, smem_sem)

    def mark(kept, row, col):
        at = row * KB + col

        @pl.when(kept & (flag_smem[at] == 0))
        def _():
            flag_smem[at] = 1
            count = list_smem[GR * KB]
            list_smem[count] = at
            list_smem[GR * KB] = count + 1

    for h in range(2):
        for k in range(HALF):
            for m in range(2):
                kept = kept_pairs(table_smem, h, 2, k, h * HALF + k, m)
                for q in range(2):
                    mark(kept[q], table_smem[h, k, m], table_smem[2, h * HALF + k, q])

    for h in range(2):

        def one_kb(k, carry, h=h):
            base = pl.multiple_of(k * BLOCK_ROWS, BLOCK_ROWS)
            add_products(
                acc_ref,
                table_smem,
                h,
                2,
                k,
                h * HALF + k,
                lambda slot, part: lefts[h][pl.ds(base + (2 * slot + part) * BS, BS), :],
                lambda slot, part: right_ref[
                    pl.ds(h * CHUNK + base + (2 * slot + part) * BS, BS), :
                ],
                lambda kept, row, col: None,
            )
            return carry

        lax.fori_loop(0, HALF, one_kb, 0, unroll=UNROLL)

    count = list_smem[GR * KB]

    def write_block(i, carry):
        at = list_smem[i]
        row, col = at // KB, at % KB
        stage_ref[i] = acc_ref[row, col].astype(jnp.bfloat16)
        pltpu.make_async_copy(stage_ref.at[i], out_ref.at[row, col], out_sem.at[i]).start()
        return carry

    def wait_block(i, carry):
        pltpu.make_async_copy(stage_ref.at[i], out_ref.at[0, 0], out_sem.at[i]).wait()
        return carry

    lax.fori_loop(0, count, write_block, 0)
    lax.fori_loop(0, count, wait_block, 0)


def finish(up, down, right, total, old):
    most = 2 * HALF * 4
    return pl.pallas_call(
        finish_kernel,
        out_shape=jax.ShapeDtypeStruct(old.shape, old.dtype),
        in_specs=[pl.BlockSpec(memory_space=pltpu.VMEM)] * 4
        + [pl.BlockSpec(memory_space=pltpu.HBM)],
        out_specs=pl.BlockSpec(memory_space=pltpu.HBM),
        input_output_aliases={4: 0},
        scratch_shapes=[
            pltpu.VMEM((most, 2, BS, BS), jnp.bfloat16),
            pltpu.VMEM((3, META, BS), jnp.bfloat16),
            pltpu.VMEM((3, KB, BS), jnp.int32),
            pltpu.SMEM((3, KB, BS), jnp.int32),
            pltpu.SMEM((GR * KB,), jnp.int32),
            pltpu.SMEM((GR * KB + 1,), jnp.int32),
            pltpu.SemaphoreType.DMA((most,)),
            pltpu.SemaphoreType.DMA,
        ],
        compiler_params=pltpu.CompilerParams(vmem_limit_bytes=5 * MIB),
    )(up, down, right, total, old)


def multiply(where, items, rights, total, local):
    grid_rows = lax.axis_size("row")
    grid_cols = lax.axis_size("col")
    lefts = [value for value, _, _ in items]
    offsets = tuple(offset for _, offset, _ in items)
    halves = tuple(half for _, _, half in items)
    n = len(items)
    first = total is None
    operands = [where, *lefts, *rights]
    in_specs = [pl.BlockSpec(memory_space=pltpu.SMEM)] + spaces(operands[1:], local)
    aliases = {}
    if not first:
        aliases = {len(operands): 0}
        operands.append(total)
        in_specs.append(pl.BlockSpec(memory_space=pltpu.VMEM))
    scratch = [
        pltpu.VMEM((n, CHUNK, BS), jnp.bfloat16),
        pltpu.VMEM((n, CHUNK, BS), jnp.bfloat16),
        pltpu.VMEM((2 * n, META, BS), jnp.bfloat16),
        pltpu.VMEM((2 * n, KB, BS), jnp.int32),
        pltpu.SMEM((2 * n, KB, BS), jnp.int32),
        pltpu.SemaphoreType.DMA((n,)),
        pltpu.SemaphoreType.DMA,
        pltpu.SemaphoreType.DMA,
    ]
    kernel = functools.partial(
        multiply_kernel, offsets, halves, first, grid_rows, grid_cols, len(rights)
    )
    return pl.pallas_call(
        kernel,
        out_shape=pltpu.VMEM((GR, KB, 2, BS, BS), jnp.float32),
        in_specs=in_specs,
        out_specs=pl.BlockSpec(memory_space=pltpu.VMEM),
        scratch_shapes=scratch,
        input_output_aliases=aliases,
        compiler_params=pltpu.CompilerParams(vmem_limit_bytes=16 * MIB),
    )(*operands)


def body(
    left_blocks,
    left_rows,
    left_count,
    left_level,
    right_blocks,
    right_cols,
    right_count,
    right_level,
):
    row, col = lax.axis_index("row"), lax.axis_index("col")
    grid_rows, grid_cols = lax.axis_size("row"), lax.axis_size("col")
    start = col + grid_cols - 1
    near = (((start + (row - start) % grid_rows) % grid_cols) // grid_rows).astype(jnp.int32)
    where = jnp.stack([row, col]).astype(jnp.int32)
    own = [pack_left(h, left_blocks, left_rows, left_count, left_level) for h in range(2)]
    right = (right_blocks, right_cols, right_count, right_level)
    held = [pack_right(which.reshape(1), *right) for which in (near, 1 - near)]

    hops = []
    up, down = list(own), list(own)
    for step in range(1, 4):
        for h in range(2):
            up[h] = shifted(up[h], "col", 1)
            down[h] = shifted(down[h], "col", -1)
        hops.append(
            [(up[0], -step, 0), (up[1], -step, 1), (down[0], step, 0), (down[1], step, 1)]
        )
    hops.append([(shifted(up[0], "col", 1), -4, 0), (shifted(down[1], "col", -1), 4, 1)])
    rights = []
    for s in range(2):
        partner = crossed(held[s], "row", 1)
        other = crossed(held[s], "row", 2)
        corner = crossed(other, "row", 1)
        rights += [held[s], partner, other, corner]

    local = own + held
    own_items = [(own[0], 0, 0), (own[1], 0, 1)]
    total = multiply(where, own_items + hops[0], rights[:4], None, local)
    total = multiply(where, hops[1], rights, total, local)
    last_right = fetch(where, 4, rights[4:], local)
    total = multiply(where, hops[2], rights[4:], total, local)
    early = flush(total)
    return finish(hops[3][0][0], hops[3][1][0], last_right, total, early)


def solution(mesh):
    in_specs = (
        P(("kpt", "row"), "col", None, None, None, None),
        P(("kpt", "row"), "col", None),
        P(("kpt", "row"), "col"),
        P(("kpt", "row"), "col", None),
        P("kpt", "row", "col", None, None, None, None),
        P("kpt", "row", "col", None),
        P("kpt", "row", "col"),
        P("kpt", "row", "col", None),
    )
    out_specs = P(("kpt", "row"), "col", None, None, None)

    return jax.shard_map(body, mesh=mesh, in_specs=in_specs, out_specs=out_specs, check_vma=False)
```

time: 118 us -> 111 us (0.941); the launches traced: 117 us -> 109 us
  Pallas kernels: 36.1 us -> 26.1 us
  waiting for transfers between devices: 50 us -> 51.2 us
    pallas_call x5 -> x8, Pallas kernels: 32.1 us -> 24.6 us  [the longest x3 15.6 us: multiply(): pl.pallas_call(kernel, out_shape=pltpu.VMEM((GR, KB, 2, BS, BS), jnp.floa...]
    pallas_call x2, Pallas kernels: 3.95 us -> 1.5 us  [pack_right(): pl.pallas_call(pack_right_kernel, out_shape=pltpu.VMEM((PANEL + META, BS)...]
  transfers between devices with their start and end apart: 20 -> 20, of which waited for: 7 -> 7; matrix products, arithmetic and copies ran while one was open for 0% -> 0% of each run, Pallas kernels for 23% -> 20%
where the time goes in v2:
time: 111 us; the launch traced here: 109 us
  waiting for transfers between devices  51.2 us (46%)
  starting transfers between devices  30.8 us (28%)
  Pallas kernels  26.1 us (24%)
    ppermute x14, waiting for transfers between devices, shifted(): lax.ppermute(value, axis, [(i, (i + steps) % count) for i in range(count)])  40.8 us
    ppermute x14, starting transfers between devices, shifted(): lax.ppermute(value, axis, [(i, (i + steps) % count) for i in range(count)])  17.9 us
    pallas_call x3, Pallas kernels, multiply(): pl.pallas_call(kernel, out_shape=pltpu.VMEM((GR, KB, 2, BS, BS), jnp.floa...  15.6 us
    ppermute x6, starting transfers between devices, crossed(): return lax.ppermute(value, axis, [(i, i ^ bit) for i in range(count)])  12.9 us
    ppermute x6, waiting for transfers between devices, crossed(): return lax.ppermute(value, axis, [(i, i ^ bit) for i in range(count)])  10.4 us
    pallas_call x2, Pallas kernels, pack_left(): pl.pallas_call(functools.partial(pack_left_kernel, half), out_shape=pltpu...  3.45 us
    pallas_call x1, Pallas kernels, finish(): pl.pallas_call(finish_kernel, out_shape=jax.ShapeDtypeStruct(old.shape, o...  2.87 us
  transfers between devices with their start and end apart: 20, of which 7 were waited for; matrix products, arithmetic and copies ran while one was open for 0% of the time, Pallas kernels for 20%

profile of v2, /device:TPU:1, one launch (start us, length us, event | category | flops | bytes accessed | tf_op | source)
XLA Modules:
  0.0 108.6 jit_solution(9538026544637320205)
XLA Ops:
  0.0 2.0 %shard_map.82.refs_1_ = bf16[2064,128]{1,0:T(8,128)(2,1)} custom-call(s32[2,8]{1,0:T(2,128)} %bitcast.31, s32[1,8]{1,0:T(1,128)} %count_hbm.3, s32[2,8]{1,0:T(2,128)} %bitcast.33, bf16[4096,128]{1,0:T(8,128)(2,1)} %bitcast.23), custom_call_target="tpu_custom_call" | custom-call | tf_op jit(solution)/shard_map/pallas_call | solution.py:66
  2.1 0.0 copy-start.2
  2.1 0.0 copy-start.3
  2.1 0.0 copy-start.4
  2.1 2.5 %collective-permute-start = (bf16[2064,128]{1,0:T(8,128)(2,1)}, bf16[2064,128]{1,0:T(8,128)(2,1)}, u32[]{:S(2)}, u32[]{:S(2)}) collective-permute-start(bf16[2064,128]{1,0:T(8,128)(2,1)} %shard_map.82.refs_1_), channel_id=1, source_target_pairs={{0,1},{1,2},{2,3},{3,4},{4,5},{5,6},{6,7},{7,0},{8,9},{9,10},{10,1... | collective-permute-start | bytes 1585160 | tf_op jit(solution)/shard_map/ppermute | solution.py:111
  4.6 1.4 %shard_map.83.refs_2_ = bf16[2064,128]{1,0:T(8,128)(2,1)} custom-call(s32[2,8]{1,0:T(2,128)S(1)} %bitcast.32, s32[1,8]{1,0:T(1,128)S(1)} %copy-done.7, s32[2,8]{1,0:T(2,128)S(1)} %bitcast.34, bf16[4096,128]{1,0:T(8,128)(2,1)S(1)} %bitcast.24), custom_call_target="tpu_custom_call" | custom-call | tf_op jit(solution)/shard_map/pallas_call | solution.py:66
  6.1 1.7 %collective-permute-start.11 = (bf16[2064,128]{1,0:T(8,128)(2,1)}, bf16[2064,128]{1,0:T(8,128)(2,1)}, u32[]{:S(2)}, u32[]{:S(2)}) collective-permute-start(bf16[2064,128]{1,0:T(8,128)(2,1)} %shard_map.83.refs_2_), channel_id=1, source_target_pairs={{0,1},{1,2},{2,3},{3,4},{4,5},{5,6},{6,7},{7,0},{8,9},{9,10},{10,1... | collective-permute-start | bytes 1585160 | tf_op jit(solution)/shard_map/ppermute | solution.py:111
  7.8 2.4 %collective-permute-start.14 = (bf16[2064,128]{1,0:T(8,128)(2,1)}, bf16[2064,128]{1,0:T(8,128)(2,1)}, u32[]{:S(2)}, u32[]{:S(2)}) collective-permute-start(bf16[2064,128]{1,0:T(8,128)(2,1)} %shard_map.82.refs_1_), channel_id=1, source_target_pairs={{0,7},{1,0},{2,1},{3,2},{4,3},{5,4},{6,5},{7,6},{8,15},{9,8},{10,9... | collective-permute-start | bytes 1585160 | tf_op jit(solution)/shard_map/ppermute | solution.py:111
  10.2 0.8 shard_map.86.refs_7_.refs_5_
  11.0 1.3 %collective-permute-start.18 = (bf16[4112,128]{1,0:T(8,128)(2,1)S(1)}, bf16[4112,128]{1,0:T(8,128)(2,1)}, u32[]{:S(2)}, u32[]{:S(2)}) collective-permute-start(bf16[4112,128]{1,0:T(8,128)(2,1)S(1)} %shard_map.86.refs_7_.refs_5_), channel_id=1, source_target_pairs={{0,16},{8,24},{16,0},{24,8},{1,17},{9,25},{17,1},{25,9},{2,18},{10... | collective-permute-start | bytes 3158024 | tf_op jit(solution)/shard_map/ppermute | solution.py:116
  12.3 1.2 %collective-permute-start.17 = (bf16[4112,128]{1,0:T(8,128)(2,1)S(1)}, bf16[4112,128]{1,0:T(8,128)(2,1)}, u32[]{:S(2)}, u32[]{:S(2)}) collective-permute-start(bf16[4112,128]{1,0:T(8,128)(2,1)S(1)} %shard_map.86.refs_7_.refs_5_), channel_id=1, source_target_pairs={{0,8},{8,0},{16,24},{24,16},{1,9},{9,1},{17,25},{25,17},{2,10},{10... | collective-permute-start | bytes 3158024 | tf_op jit(solution)/shard_map/ppermute | solution.py:116
  13.5 0.7 shard_map.84.refs_0_.refs_9_.refs_5_
  14.3 6.3 %collective-permute-done.refs_3_ = bf16[2064,128]{1,0:T(8,128)(2,1)} collective-permute-done((bf16[2064,128]{1,0:T(8,128)(2,1)}, bf16[2064,128]{1,0:T(8,128)(2,1)}, u32[]{:S(2)}, u32[]{:S(2)}) %collective-permute-start) | collective-permute-done | bytes 528416 | tf_op jit(solution)/shard_map/ppermute | solution.py:111
  20.6 1.2 %collective-permute-start.9 = (bf16[4112,128]{1,0:T(8,128)(2,1)S(1)}, bf16[4112,128]{1,0:T(8,128)(2,1)S(1)}, u32[]{:S(2)}, u32[]{:S(2)}) collective-permute-start(bf16[4112,128]{1,0:T(8,128)(2,1)S(1)} %shard_map.84.refs_0_.refs_9_.refs_5_), channel_id=1, source_target_pairs={{0,16},{8,24},{16,0},{24,8},{1,17},{9,25},{17,1},{25,9},{2,18},{10... | collective-permute-start | bytes 3158024 | tf_op jit(solution)/shard_map/ppermute | solution.py:116
  21.8 10.1 %collective-permute-done.11.refs_4_ = bf16[2064,128]{1,0:T(8,128)(2,1)} collective-permute-done((bf16[2064,128]{1,0:T(8,128)(2,1)}, bf16[2064,128]{1,0:T(8,128)(2,1)}, u32[]{:S(2)}, u32[]{:S(2)}) %collective-permute-start.11) | collective-permute-done | bytes 528416 | tf_op jit(solution)/shard_map/ppermute | solution.py:111
  31.9 1.2 %collective-permute-start.4 = (bf16[2064,128]{1,0:T(8,128)(2,1)}, bf16[2064,128]{1,0:T(8,128)(2,1)S(1)}, u32[]{:S(2)}, u32[]{:S(2)}) collective-permute-start(bf16[2064,128]{1,0:T(8,128)(2,1)} %shard_map.83.refs_2_), channel_id=1, source_target_pairs={{0,7},{1,0},{2,1},{3,2},{4,3},{5,4},{6,5},{7,6},{8,15},{9,8},{10,9... | collective-permute-start | bytes 1585160 | tf_op jit(solution)/shard_map/ppermute | solution.py:111
  33.1 0.0 collective-permute-done.14.refs_5_
  33.1 1.8 %collective-permute-start.8 = (bf16[4112,128]{1,0:T(8,128)(2,1)S(1)}, bf16[4112,128]{1,0:T(8,128)(2,1)S(1)}, u32[]{:S(2)}, u32[]{:S(2)}) collective-permute-start(bf16[4112,128]{1,0:T(8,128)(2,1)S(1)} %shard_map.84.refs_0_.refs_9_.refs_5_), channel_id=1, source_target_pairs={{0,8},{8,0},{16,24},{24,16},{1,9},{9,1},{17,25},{25,17},{2,10},{10... | collective-permute-start | bytes 3158024 | tf_op jit(solution)/shard_map/ppermute | solution.py:116
  34.9 9.5 %collective-permute-done.4.refs_6_ = bf16[2064,128]{1,0:T(8,128)(2,1)S(1)} collective-permute-done((bf16[2064,128]{1,0:T(8,128)(2,1)}, bf16[2064,128]{1,0:T(8,128)(2,1)S(1)}, u32[]{:S(2)}, u32[]{:S(2)}) %collective-permute-start.4) | collective-permute-done | bytes 528416 | tf_op jit(solution)/shard_map/ppermute | solution.py:111
  44.5 0.0 collective-permute-start.1
  44.5 0.0 collective-permute-done.18.refs_9_.refs_7_
  44.5 2.7 %collective-permute-start.5 = (bf16[2064,128]{1,0:T(8,128)(2,1)S(1)}, bf16[2064,128]{1,0:T(8,128)(2,1)S(1)}, u32[]{:S(2)}, u32[]{:S(2)}) collective-permute-start(bf16[2064,128]{1,0:T(8,128)(2,1)S(1)} %collective-permute-done.4.refs_6_), channel_id=1, source_target_pairs={{0,7},{1,0},{2,1},{3,2},{4,3},{5,4},{6,5},{7,6},{8,15},{9,8},{10,9... | collective-permute-start | bytes 1585160 | tf_op jit(solution)/shard_map/ppermute | solution.py:111
  47.1 0.0 collective-permute-done.17.refs_8_.refs_6_
  47.1 0.0 collective-permute-start.12
  47.1 10.4 %collective-permute-done.9.refs_2_.refs_11_.refs_7_ = bf16[4112,128]{1,0:T(8,128)(2,1)S(1)} collective-permute-done((bf16[4112,128]{1,0:T(8,128)(2,1)S(1)}, bf16[4112,128]{1,0:T(8,128)(2,1)S(1)}, u32[]{:S(2)}, u32[]{:S(2)}) %collective-permute-start.9) | collective-permute-done | bytes 1052704 | tf_op jit(solution)/shard_map/ppermute | solution.py:116
  57.5 1.8 %collective-permute-start.19 = (bf16[4112,128]{1,0:T(8,128)(2,1)}, bf16[4112,128]{1,0:T(8,128)(2,1)S(1)}, u32[]{:S(2)}, u32[]{:S(2)}) collective-permute-start(bf16[4112,128]{1,0:T(8,128)(2,1)} %collective-permute-done.18.refs_9_.refs_7_), channel_id=1, source_target_pairs={{0,8},{8,0},{16,24},{24,16},{1,9},{9,1},{17,25},{25,17},{2,10},{10... | collective-permute-start | bytes 3158024 | tf_op jit(solution)/shard_map/ppermute | solution.py:116
  59.3 1.4 %collective-permute-start.15 = (bf16[2064,128]{1,0:T(8,128)(2,1)}, bf16[2064,128]{1,0:T(8,128)(2,1)S(1)}, u32[]{:S(2)}, u32[]{:S(2)}) collective-permute-start(bf16[2064,128]{1,0:T(8,128)(2,1)} %collective-permute-done.14.refs_5_), channel_id=1, source_target_pairs={{0,7},{1,0},{2,1},{3,2},{4,3},{5,4},{6,5},{7,6},{8,15},{9,8},{10,9... | collective-permute-start | bytes 1585160 | tf_op jit(solution)/shard_map/ppermute | solution.py:111
  60.7 0.0 collective-permute-start.2
  60.8 0.0 collective-permute-done.5.refs_4_
  60.8 2.6 %collective-permute-start.6 = (bf16[2064,128]{1,0:T(8,128)(2,1)S(1)}, bf16[2064,128]{1,0:T(8,128)(2,1)S(1)}, u32[]{:S(2)}, u32[]{:S(2)}) collective-permute-start(bf16[2064,128]{1,0:T(8,128)(2,1)S(1)} %collective-permute-done.5.refs_4_), channel_id=1, source_target_pairs={{0,7},{1,0},{2,1},{3,2},{4,3},{5,4},{6,5},{7,6},{8,15},{9,8},{10,9... | collective-permute-start | bytes 1585160 | tf_op jit(solution)/shard_map/ppermute | solution.py:111
  63.4 5.2 %collective-permute-done.12.refs_2_ = bf16[2064,128]{1,0:T(8,128)(2,1)S(1)} collective-permute-done((bf16[2064,128]{1,0:T(8,128)(2,1)}, bf16[2064,128]{1,0:T(8,128)(2,1)S(1)}, u32[]{:S(2)}, u32[]{:S(2)}) %collective-permute-start.12) | collective-permute-done | bytes 528416 | tf_op jit(solution)/shard_map/ppermute | solution.py:111
  68.7 5.5 %collective-permute-start.10 = (bf16[4112,128]{1,0:T(8,128)(2,1)S(1)}, bf16[4112,128]{1,0:T(8,128)(2,1)S(1)}, u32[]{:S(2)}, u32[]{:S(2)}) collective-permute-start(bf16[4112,128]{1,0:T(8,128)(2,1)S(1)} %collective-permute-done.9.refs_2_.refs_11_.refs_7_), channel_id=1, source_target_pairs={{0,8},{8,0},{16,24},{24,16},{1,9},{9,1},{17,25},{25,17},{2,10},{10... | collective-permute-start | bytes 3158024 | tf_op jit(solution)/shard_map/ppermute | solution.py:116
  74.2 5.8 %collective-permute-done.2.refs_1_ = bf16[2064,128]{1,0:T(8,128)(2,1)S(1)} collective-permute-done((bf16[2064,128]{1,0:T(8,128)(2,1)S(1)}, bf16[2064,128]{1,0:T(8,128)(2,1)S(1)}, u32[]{:S(2)}, u32[]{:S(2)}) %collective-permute-start.2) | collective-permute-done | bytes 528416 | tf_op jit(solution)/shard_map/ppermute | solution.py:111
  80.0 0.6 collective-permute-start.16
  80.6 3.8 %collective-permute-done.6.refs_4_ = bf16[2064,128]{1,0:T(8,128)(2,1)S(1)} collective-permute-done((bf16[2064,128]{1,0:T(8,128)(2,1)S(1)}, bf16[2064,128]{1,0:T(8,128)(2,1)S(1)}, u32[]{:S(2)}, u32[]{:S(2)}) %collective-permute-start.6) | collective-permute-done | bytes 528416 | tf_op jit(solution)/shard_map/ppermute | solution.py:111
  84.4 0.9 collective-permute-start.3
  85.3 0.0 collective-permute-done.19.refs_10_.refs_8_
  85.3 1.8 %collective-permute-start.7 = (bf16[2064,128]{1,0:T(8,128)(2,1)S(1)}, bf16[2064,128]{1,0:T(8,128)(2,1)S(1)}, u32[]{:S(2)}, u32[]{:S(2)}) collective-permute-start(bf16[2064,128]{1,0:T(8,128)(2,1)S(1)} %collective-permute-done.6.refs_4_), channel_id=1, source_target_pairs={{0,7},{1,0},{2,1},{3,2},{4,3},{5,4},{6,5},{7,6},{8,15},{9,8},{10,9... | collective-permute-start | bytes 1585160 | tf_op jit(solution)/shard_map/ppermute | solution.py:111
  87.1 0.1 pad_add_fusion.where_ref.refs_0_
  87.2 6.9 %shard_map.87.refs_13_ = f32[8,8,2,128,128]{4,3,2,1,0:T(8,128)S(1)} custom-call(s32[2]{0:T(128)S(1)} %pad_add_fusion.where_ref.refs_0_, bf16[2064,128]{1,0:T(8,128)(2,1)} %shard_map.82.refs_1_, bf16[2064,128]{1,0:T(8,128)(2,1)} %shard_map.83.refs_2_, bf16[2064,128]{1,0:T(8,128)(2,1)} %collective-permute-done.refs_3_, ...), custom_call_target="tpu_custom_call" | custom-call | tf_op jit(solution)/shard_map/pallas_call | solution.py:412
  94.1 4.3 %shard_map.88.refs_9_ = f32[8,8,2,128,128]{4,3,2,1,0:T(8,128)S(1)} custom-call(s32[2]{0:T(128)S(1)} %pad_add_fusion.where_ref.refs_0_, bf16[2064,128]{1,0:T(8,128)(2,1)S(1)} %collective-permute-done.1.refs_1_, bf16[2064,128]{1,0:T(8,128)(2,1)S(1)} %collective-permute-done.12.refs_2_, ...), custom_call_target="tpu_custom_call", output_to_operand_aliasing={{}: (13, {})} | custom-call | tf_op jit(solution)/shard_map/pallas_call | solution.py:412
  98.4 0.0 collective-permute-done.13.refs_2_
  98.4 0.0 collective-permute-done.16.refs_3_
  98.4 4.4 %shard_map.89.acc_ref = f32[8,8,2,128,128]{4,3,2,1,0:T(8,128)S(1)} custom-call(s32[2]{0:T(128)S(1)} %pad_add_fusion.where_ref.refs_0_, bf16[2064,128]{1,0:T(8,128)(2,1)S(1)} %collective-permute-done.2.refs_1_, bf16[2064,128]{1,0:T(8,128)(2,1)S(1)} %collective-permute-done.13.refs_2_, ...), custom_call_target="tpu_custom_call", output_to_operand_aliasing={{}: (9, {})} | custom-call | tf_op jit(solution)/shard_map/pallas_call | solution.py:412
  102.8 2.1 %shard_map.90.old_ref = bf16[8,8,2,128,128]{4,3,2,1,0:T(8,128)(2,1)} custom-call(f32[8,8,2,128,128]{4,3,2,1,0:T(8,128)S(1)} %shard_map.89.acc_ref), custom_call_target="tpu_custom_call" | custom-call | tf_op jit(solution)/shard_map/pallas_call | solution.py:280
  104.9 0.7 shard_map.85.right_ref
  105.6 0.0 collective-permute-done.3.up_ref
  105.6 2.9 %shard_map.91 = bf16[8,8,2,128,128]{4,3,2,1,0:T(8,128)(2,1)} custom-call(bf16[2064,128]{1,0:T(8,128)(2,1)S(1)} %collective-permute-done.3.up_ref, bf16[2064,128]{1,0:T(8,128)(2,1)S(1)} %collective-permute-done.7.down_ref, bf16[4112,128]{1,0:T(8,128)(2,1)S(1)} %shard_map.85.right_ref, ...), custom_call_target="tpu_custom_call", output_to_operand_aliasing={{}: (4, {})} | custom-call | tf_op jit(solution)/shard_map/pallas_call | solution.py:363
  (19 shorter events, 0.0 us)
Async XLA Ops:
  0.0 4.6 %copy-start.5 = (s32[1,8,2]{1,2,0:T(2,128)S(1)}, s32[1,8,2]{1,2,0:T(2,128)}, u32[]{:S(2)}) copy-start(s32[1,8,2]{1,2,0:T(2,128)} %param.9) | copy-start | bytes 196
  0.0 4.6 %copy-start.6 = (s32[1,8,2]{1,2,0:T(2,128)S(1)}, s32[1,8,2]{1,2,0:T(2,128)}, u32[]{:S(2)}) copy-start(s32[1,8,2]{1,2,0:T(2,128)} %param.11) | copy-start | bytes 196
  0.0 4.6 %copy-start.1 = (bf16[1,8,2,2,128,128]{5,4,3,2,1,0:T(8,128)(2,1)S(1)}, bf16[1,8,2,2,128,128]{5,4,3,2,1,0:T(8,128)(2,1)}, u32[]{:S(2)}) copy-start(bf16[1,8,2,2,128,128]{5,4,3,2,1,0:T(8,128)(2,1)} %param.8) | copy-start | bytes 3145732
  0.0 4.6 %copy-start.7 = (s32[1,8]{1,0:T(1,128)S(1)}, s32[1,8]{1,0:T(1,128)}, u32[]{:S(2)}) copy-start(s32[1,8]{1,0:T(1,128)} %count_hbm.3) | copy-start | bytes 100
  0.0 10.2 %copy-start = (bf16[2,8,1,2,2,128,128]{6,5,4,3,2,1,0:T(8,128)(2,1)S(1)}, bf16[2,8,1,2,2,128,128]{6,5,4,3,2,1,0:T(8,128)(2,1)}, u32[]{:S(2)}) copy-start(bf16[2,8,1,2,2,128,128]{6,5,4,3,2,1,0:T(8,128)(2,1)} %param.12) | copy-start | bytes 6291460
  2.1 8.2 %copy-start.2 = (s32[2,8,1,2]{1,3,2,0:T(2,128)S(1)}, s32[2,8,1,2]{1,3,2,0:T(2,128)}, u32[]{:S(2)}) copy-start(s32[2,8,1,2]{1,3,2,0:T(2,128)} %param.13) | copy-start | bytes 388
  2.1 8.2 %copy-start.3 = (s32[2,8,1,2]{1,3,2,0:T(2,128)S(1)}, s32[2,8,1,2]{1,3,2,0:T(2,128)}, u32[]{:S(2)}) copy-start(s32[2,8,1,2]{1,3,2,0:T(2,128)} %param.15) | copy-start | bytes 388
  2.1 8.2 %copy-start.4 = (s32[2,8,1]{1,2,0:T(1,128)S(1)}, s32[2,8,1]{1,2,0:T(1,128)}, u32[]{:S(2)}) copy-start(s32[2,8,1]{1,2,0:T(1,128)} %param.14) | copy-start | bytes 196
  2.1 18.5 %collective-permute-start = (bf16[2064,128]{1,0:T(8,128)(2,1)}, bf16[2064,128]{1,0:T(8,128)(2,1)}, u32[]{:S(2)}, u32[]{:S(2)}) collective-permute-start(bf16[2064,128]{1,0:T(8,128)(2,1)} %shard_map.82.refs_1_), channel_id=1, source_target_pairs={{0,1},{1,2},{2,3},{3,4},{4,5},{5,6},{6,7},{7,0},{8,9},{9,10},{10,1... | collective-permute-start | bytes 1585160 | tf_op jit(solution)/shard_map/ppermute | solution.py:111
  6.1 25.8 %collective-permute-start.11 = (bf16[2064,128]{1,0:T(8,128)(2,1)}, bf16[2064,128]{1,0:T(8,128)(2,1)}, u32[]{:S(2)}, u32[]{:S(2)}) collective-permute-start(bf16[2064,128]{1,0:T(8,128)(2,1)} %shard_map.83.refs_2_), channel_id=1, source_target_pairs={{0,1},{1,2},{2,3},{3,4},{4,5},{5,6},{6,7},{7,0},{8,9},{9,10},{10,1... | collective-permute-start | bytes 1585160 | tf_op jit(solution)/shard_map/ppermute | solution.py:111
  7.8 25.3 %collective-permute-start.14 = (bf16[2064,128]{1,0:T(8,128)(2,1)}, bf16[2064,128]{1,0:T(8,128)(2,1)}, u32[]{:S(2)}, u32[]{:S(2)}) collective-permute-start(bf16[2064,128]{1,0:T(8,128)(2,1)} %shard_map.82.refs_1_), channel_id=1, source_target_pairs={{0,7},{1,0},{2,1},{3,2},{4,3},{5,4},{6,5},{7,6},{8,15},{9,8},{10,9... | collective-permute-start | bytes 1585160 | tf_op jit(solution)/shard_map/ppermute | solution.py:111
  11.0 33.5 %collective-permute-start.18 = (bf16[4112,128]{1,0:T(8,128)(2,1)S(1)}, bf16[4112,128]{1,0:T(8,128)(2,1)}, u32[]{:S(2)}, u32[]{:S(2)}) collective-permute-start(bf16[4112,128]{1,0:T(8,128)(2,1)S(1)} %shard_map.86.refs_7_.refs_5_), channel_id=1, source_target_pairs={{0,16},{8,24},{16,0},{24,8},{1,17},{9,25},{17,1},{25,9},{2,18},{10... | collective-permute-start | bytes 3158024 | tf_op jit(solution)/shard_map/ppermute | solution.py:116
  12.3 34.8 %collective-permute-start.17 = (bf16[4112,128]{1,0:T(8,128)(2,1)S(1)}, bf16[4112,128]{1,0:T(8,128)(2,1)}, u32[]{:S(2)}, u32[]{:S(2)}) collective-permute-start(bf16[4112,128]{1,0:T(8,128)(2,1)S(1)} %shard_map.86.refs_7_.refs_5_), channel_id=1, source_target_pairs={{0,8},{8,0},{16,24},{24,16},{1,9},{9,1},{17,25},{25,17},{2,10},{10... | collective-permute-start | bytes 3158024 | tf_op jit(solution)/shard_map/ppermute | solution.py:116
  20.6 36.9 %collective-permute-start.9 = (bf16[4112,128]{1,0:T(8,128)(2,1)S(1)}, bf16[4112,128]{1,0:T(8,128)(2,1)S(1)}, u32[]{:S(2)}, u32[]{:S(2)}) collective-permute-start(bf16[4112,128]{1,0:T(8,128)(2,1)S(1)} %shard_map.84.refs_0_.refs_9_.refs_5_), channel_id=1, source_target_pairs={{0,16},{8,24},{16,0},{24,8},{1,17},{9,25},{17,1},{25,9},{2,18},{10... | collective-permute-start | bytes 3158024 | tf_op jit(solution)/shard_map/ppermute | solution.py:116
  31.9 12.5 %collective-permute-start.4 = (bf16[2064,128]{1,0:T(8,128)(2,1)}, bf16[2064,128]{1,0:T(8,128)(2,1)S(1)}, u32[]{:S(2)}, u32[]{:S(2)}) collective-permute-start(bf16[2064,128]{1,0:T(8,128)(2,1)} %shard_map.83.refs_2_), channel_id=1, source_target_pairs={{0,7},{1,0},{2,1},{3,2},{4,3},{5,4},{6,5},{7,6},{8,15},{9,8},{10,9... | collective-permute-start | bytes 1585160 | tf_op jit(solution)/shard_map/ppermute | solution.py:111
  33.1 26.2 %collective-permute-start.8 = (bf16[4112,128]{1,0:T(8,128)(2,1)S(1)}, bf16[4112,128]{1,0:T(8,128)(2,1)S(1)}, u32[]{:S(2)}, u32[]{:S(2)}) collective-permute-start(bf16[4112,128]{1,0:T(8,128)(2,1)S(1)} %shard_map.84.refs_0_.refs_9_.refs_5_), channel_id=1, source_target_pairs={{0,8},{8,0},{16,24},{24,16},{1,9},{9,1},{17,25},{25,17},{2,10},{10... | collective-permute-start | bytes 3158024 | tf_op jit(solution)/shard_map/ppermute | solution.py:116
  44.5 16.3 %collective-permute-start.1 = (bf16[2064,128]{1,0:T(8,128)(2,1)}, bf16[2064,128]{1,0:T(8,128)(2,1)S(1)}, u32[]{:S(2)}, u32[]{:S(2)}) collective-permute-start(bf16[2064,128]{1,0:T(8,128)(2,1)} %collective-permute-done.refs_3_), channel_id=1, source_target_pairs={{0,1},{1,2},{2,3},{3,4},{4,5},{5,6},{6,7},{7,0},{8,9},{9,10},{10,1... | collective-permute-start | bytes 1585160 | tf_op jit(solution)/shard_map/ppermute | solution.py:111
  44.5 16.3 %collective-permute-start.5 = (bf16[2064,128]{1,0:T(8,128)(2,1)S(1)}, bf16[2064,128]{1,0:T(8,128)(2,1)S(1)}, u32[]{:S(2)}, u32[]{:S(2)}) collective-permute-start(bf16[2064,128]{1,0:T(8,128)(2,1)S(1)} %collective-permute-done.4.refs_6_), channel_id=1, source_target_pairs={{0,7},{1,0},{2,1},{3,2},{4,3},{5,4},{6,5},{7,6},{8,15},{9,8},{10,9... | collective-permute-start | bytes 1585160 | tf_op jit(solution)/shard_map/ppermute | solution.py:111
  47.1 21.5 %collective-permute-start.12 = (bf16[2064,128]{1,0:T(8,128)(2,1)}, bf16[2064,128]{1,0:T(8,128)(2,1)S(1)}, u32[]{:S(2)}, u32[]{:S(2)}) collective-permute-start(bf16[2064,128]{1,0:T(8,128)(2,1)} %collective-permute-done.11.refs_4_), channel_id=1, source_target_pairs={{0,1},{1,2},{2,3},{3,4},{4,5},{5,6},{6,7},{7,0},{8,9},{9,10},{10,1... | collective-permute-start | bytes 1585160 | tf_op jit(solution)/shard_map/ppermute | solution.py:111
  57.5 27.8 %collective-permute-start.19 = (bf16[4112,128]{1,0:T(8,128)(2,1)}, bf16[4112,128]{1,0:T(8,128)(2,1)S(1)}, u32[]{:S(2)}, u32[]{:S(2)}) collective-permute-start(bf16[4112,128]{1,0:T(8,128)(2,1)} %collective-permute-done.18.refs_9_.refs_7_), channel_id=1, source_target_pairs={{0,8},{8,0},{16,24},{24,16},{1,9},{9,1},{17,25},{25,17},{2,10},{10... | collective-permute-start | bytes 3158024 | tf_op jit(solution)/shard_map/ppermute | solution.py:116
  59.3 14.9 %collective-permute-start.15 = (bf16[2064,128]{1,0:T(8,128)(2,1)}, bf16[2064,128]{1,0:T(8,128)(2,1)S(1)}, u32[]{:S(2)}, u32[]{:S(2)}) collective-permute-start(bf16[2064,128]{1,0:T(8,128)(2,1)} %collective-permute-done.14.refs_5_), channel_id=1, source_target_pairs={{0,7},{1,0},{2,1},{3,2},{4,3},{5,4},{6,5},{7,6},{8,15},{9,8},{10,9... | collective-permute-start | bytes 1585160 | tf_op jit(solution)/shard_map/ppermute | solution.py:111
  60.7 19.2 %collective-permute-start.2 = (bf16[2064,128]{1,0:T(8,128)(2,1)S(1)}, bf16[2064,128]{1,0:T(8,128)(2,1)S(1)}, u32[]{:S(2)}, u32[]{:S(2)}) collective-permute-start(bf16[2064,128]{1,0:T(8,128)(2,1)S(1)} %collective-permute-done.1.refs_1_), channel_id=1, source_target_pairs={{0,1},{1,2},{2,3},{3,4},{4,5},{5,6},{6,7},{7,0},{8,9},{9,10},{10,1... | collective-permute-start | bytes 1585160 | tf_op jit(solution)/shard_map/ppermute | solution.py:111
  60.8 23.6 %collective-permute-start.6 = (bf16[2064,128]{1,0:T(8,128)(2,1)S(1)}, bf16[2064,128]{1,0:T(8,128)(2,1)S(1)}, u32[]{:S(2)}, u32[]{:S(2)}) collective-permute-start(bf16[2064,128]{1,0:T(8,128)(2,1)S(1)} %collective-permute-done.5.refs_4_), channel_id=1, source_target_pairs={{0,7},{1,0},{2,1},{3,2},{4,3},{5,4},{6,5},{7,6},{8,15},{9,8},{10,9... | collective-permute-start | bytes 1585160 | tf_op jit(solution)/shard_map/ppermute | solution.py:111
  68.7 25.4 %collective-permute-start.10 = (bf16[4112,128]{1,0:T(8,128)(2,1)S(1)}, bf16[4112,128]{1,0:T(8,128)(2,1)S(1)}, u32[]{:S(2)}, u32[]{:S(2)}) collective-permute-start(bf16[4112,128]{1,0:T(8,128)(2,1)S(1)} %collective-permute-done.9.refs_2_.refs_11_.refs_7_), channel_id=1, source_target_pairs={{0,8},{8,0},{16,24},{24,16},{1,9},{9,1},{17,25},{25,17},{2,10},{10... | collective-permute-start | bytes 3158024 | tf_op jit(solution)/shard_map/ppermute | solution.py:116
  74.2 24.2 %collective-permute-start.13 = (bf16[2064,128]{1,0:T(8,128)(2,1)S(1)}, bf16[2064,128]{1,0:T(8,128)(2,1)S(1)}, u32[]{:S(2)}, u32[]{:S(2)}) collective-permute-start(bf16[2064,128]{1,0:T(8,128)(2,1)S(1)} %collective-permute-done.12.refs_2_), channel_id=1, source_target_pairs={{0,1},{1,2},{2,3},{3,4},{4,5},{5,6},{6,7},{7,0},{8,9},{9,10},{10,1... | collective-permute-start | bytes 1585160 | tf_op jit(solution)/shard_map/ppermute | solution.py:111
  80.0 18.4 %collective-permute-start.16 = (bf16[2064,128]{1,0:T(8,128)(2,1)S(1)}, bf16[2064,128]{1,0:T(8,128)(2,1)S(1)}, u32[]{:S(2)}, u32[]{:S(2)}) collective-permute-start(bf16[2064,128]{1,0:T(8,128)(2,1)S(1)} %collective-permute-done.15.refs_3_), channel_id=1, source_target_pairs={{0,7},{1,0},{2,1},{3,2},{4,3},{5,4},{6,5},{7,6},{8,15},{9,8},{10,9... | collective-permute-start | bytes 1585160 | tf_op jit(solution)/shard_map/ppermute | solution.py:111
  84.4 21.2 %collective-permute-start.3 = (bf16[2064,128]{1,0:T(8,128)(2,1)S(1)}, bf16[2064,128]{1,0:T(8,128)(2,1)S(1)}, u32[]{:S(2)}, u32[]{:S(2)}) collective-permute-start(bf16[2064,128]{1,0:T(8,128)(2,1)S(1)} %collective-permute-done.2.refs_1_), channel_id=1, source_target_pairs={{0,1},{1,2},{2,3},{3,4},{4,5},{5,6},{6,7},{7,0},{8,9},{9,10},{10,1... | collective-permute-start | bytes 1585160 | tf_op jit(solution)/shard_map/ppermute | solution.py:111
  85.3 20.3 %collective-permute-start.7 = (bf16[2064,128]{1,0:T(8,128)(2,1)S(1)}, bf16[2064,128]{1,0:T(8,128)(2,1)S(1)}, u32[]{:S(2)}, u32[]{:S(2)}) collective-permute-start(bf16[2064,128]{1,0:T(8,128)(2,1)S(1)} %collective-permute-done.6.refs_4_), channel_id=1, source_target_pairs={{0,7},{1,0},{2,1},{3,2},{4,3},{5,4},{6,5},{7,6},{8,15},{9,8},{10,9... | collective-permute-start | bytes 1585160 | tf_op jit(solution)/shard_map/ppermute | solution.py:111

commit v3 on v2

--- a/solution.py
+++ b/solution.py
@@ -21,44 +21,33 @@
 PANEL = KB * BLOCK_ROWS
 
 
-def fill_table(table_ref, places, count, level, rows):
-    lane = lax.broadcasted_iota(jnp.int32, (META, BS), 1)
-    sub = lax.broadcasted_iota(jnp.int32, (META, BS), 0)
-    table = jnp.zeros((META, BS), jnp.float32)
-    for k in range(rows):
-        for m in range(2):
-            live = (m < count(k)).astype(jnp.int32)
-            for at, value in ((m, places(k, m)), (2 + m, level(k, m)), (4 + m, live)):
-                table = jnp.where((sub == k) & (lane == at), value.astype(jnp.float32), table)
+def fill_table(table_ref, places, count, level):
+    slot = lax.broadcasted_iota(jnp.int32, places.shape, 0)
+    rows = (places, level, (slot < count).astype(jnp.int32))
+    table = jnp.concatenate([row.astype(jnp.float32) for row in rows], axis=0)
+    table = jnp.pad(table, ((0, META - table.shape[0]), (0, BS - table.shape[1])))
     table_ref[...] = table.astype(jnp.bfloat16)
 
 
 def pack_left_kernel(
     half, rows_hbm, count_hbm, level_hbm, blocks_ref, out_ref, rows_ref, count_ref, level_ref, sem
 ):
+    blocks = pltpu.make_async_copy(
+        blocks_ref.at[pl.ds(half * CHUNK, CHUNK)], out_ref.at[pl.ds(0, CHUNK)], sem.at[3]
+    )
     copies = [
         pltpu.make_async_copy(source, target, sem.at[i])
         for i, (source, target) in enumerate(
-            (
-                (rows_hbm, rows_ref),
-                (count_hbm, count_ref),
-                (level_hbm, level_ref),
-                (blocks_ref.at[pl.ds(half * CHUNK, CHUNK)], out_ref.at[pl.ds(0, CHUNK)]),
-            )
-        )
-    ]
+            ((rows_hbm, rows_ref), (count_hbm, count_ref), (level_hbm, level_ref))
+        )
+    ]
+    blocks.start()
     for copy in copies:
         copy.start()
-    for copy in copies[:3]:
+    for copy in copies:
         copy.wait()
-    fill_table(
-        out_ref.at[pl.ds(CHUNK, META)],
-        lambda k, m: rows_ref[m, half * HALF + k],
-        lambda k: count_ref[0, half * HALF + k],
-        lambda k, m: level_ref[m, half * HALF + k],
-        HALF,
-    )
-    copies[3].wait()
+    fill_table(out_ref.at[pl.ds(CHUNK, META)], rows_ref[...], count_ref[...], level_ref[...])
+    blocks.wait()
 
 
 def pack_left(half, blocks, rows, count, level):
@@ -68,42 +57,51 @@
         out_shape=pltpu.VMEM((CHUNK + META, BS), jnp.bfloat16),
         in_specs=[pl.BlockSpec(memory_space=pltpu.HBM)] * 4,
         out_specs=pl.BlockSpec(memory_space=pltpu.VMEM),
-        scratch_shapes=[pltpu.SMEM(table.shape, jnp.int32) for table in tables]
+        scratch_shapes=[pltpu.VMEM(table.shape, jnp.int32) for table in tables]
         + [pltpu.SemaphoreType.DMA((4,))],
         compiler_params=pltpu.CompilerParams(vmem_limit_bytes=PACK_LIMIT[half] * MIB),
     )(*tables, blocks.reshape(-1, BS))
 
 
-def pack_right_kernel(which_ref, cols_ref, count_ref, level_ref, blocks_ref, out_ref, sem):
+def pack_right_kernel(
+    which_ref, cols_hbm, count_hbm, level_hbm, blocks_ref, out_ref,
+    cols_ref, count_ref, level_ref, sem,
+):
     which = which_ref[0]
-    blocks = pltpu.make_async_copy(blocks_ref.at[which], out_ref.at[pl.ds(0, PANEL)], sem)
+    blocks = pltpu.make_async_copy(
+        blocks_ref.at[which], out_ref.at[pl.ds(0, PANEL)], sem.at[3]
+    )
+    copies = [
+        pltpu.make_async_copy(source.at[which], target, sem.at[i])
+        for i, (source, target) in enumerate(
+            ((cols_hbm, cols_ref), (count_hbm, count_ref), (level_hbm, level_ref))
+        )
+    ]
     blocks.start()
-    fill_table(
-        out_ref.at[pl.ds(PANEL, META)],
-        lambda k, m: cols_ref[which, m, k],
-        lambda k: count_ref[which, 0, k],
-        lambda k, m: level_ref[which, m, k],
-        KB,
-    )
+    for copy in copies:
+        copy.start()
+    for copy in copies:
+        copy.wait()
+    fill_table(out_ref.at[pl.ds(PANEL, META)], cols_ref[...], count_ref[...], level_ref[...])
     blocks.wait()
 
 
 def pack_right(which, blocks, cols, count, level):
-    return pl.pallas_call(
-        pack_right_kernel,
-        out_shape=pltpu.VMEM((PANEL + META, BS), jnp.bfloat16),
-        in_specs=[pl.BlockSpec(memory_space=pltpu.SMEM)] * 4
-        + [pl.BlockSpec(memory_space=pltpu.HBM)],
-        out_specs=pl.BlockSpec(memory_space=pltpu.VMEM),
-        scratch_shapes=[pltpu.SemaphoreType.DMA],
-        compiler_params=pltpu.CompilerParams(vmem_limit_bytes=2 * MIB),
-    )(
-        which,
+    tables = (
         jnp.swapaxes(cols[:, :, 0], 1, 2),
         jnp.swapaxes(count, 1, 2),
         jnp.swapaxes(level[:, :, 0], 1, 2),
-        blocks.reshape(-1, PANEL, BS),
-    )
+    )
+    return pl.pallas_call(
+        pack_right_kernel,
+        out_shape=pltpu.VMEM((PANEL + META, BS), jnp.bfloat16),
+        in_specs=[pl.BlockSpec(memory_space=pltpu.SMEM)]
+        + [pl.BlockSpec(memory_space=pltpu.HBM)] * 4,
+        out_specs=pl.BlockSpec(memory_space=pltpu.VMEM),
+        scratch_shapes=[pltpu.VMEM(table.shape[1:], jnp.int32) for table in tables]
+        + [pltpu.SemaphoreType.DMA((4,))],
+        compiler_params=pltpu.CompilerParams(vmem_limit_bytes=2 * MIB),
+    )(which, *tables, blocks.reshape(-1, PANEL, BS))
 
 
 def shifted(value, axis, steps):
@@ -116,18 +114,18 @@
     return lax.ppermute(value, axis, [(i, i ^ bit) for i in range(count)])
 
 
-def kept_pairs(table_smem, left_at, right_at, k, kr, m):
-    level = table_smem[left_at, k, 2 + m]
-    live = table_smem[left_at, k, 4 + m] > 0
+def kept_pairs(table_smem, left_at, right_at, kb, m):
+    level = table_smem[left_at, 2 + m, kb]
+    live = table_smem[left_at, 4 + m, kb] > 0
     return [
         live
-        & (table_smem[right_at, kr, 4 + q] > 0)
-        & (level + table_smem[right_at, kr, 2 + q] >= LEVEL_CUT)
+        & (table_smem[right_at, 4 + q, kb] > 0)
+        & (level + table_smem[right_at, 2 + q, kb] >= LEVEL_CUT)
         for q in range(2)
     ]
 
 
-def add_products(acc_ref, table_smem, left_at, right_at, k, kr, left_part, right_part, mark):
+def add_products(acc_ref, table_smem, left_at, right_at, kb, left_part, right_part):
     right = jnp.concatenate(
         [
             jnp.concatenate([right_part(0, 0), right_part(1, 0)], axis=1),
@@ -136,8 +134,8 @@
         axis=0,
     )
     for m in range(2):
-        row = table_smem[left_at, k, m]
-        kept = kept_pairs(table_smem, left_at, right_at, k, kr, m)
+        row = table_smem[left_at, m, kb]
+        kept = kept_pairs(table_smem, left_at, right_at, kb, m)
         real, imag = left_part(m, 0), left_part(m, 1)
         left = jnp.concatenate(
             [
@@ -148,13 +146,12 @@
         )
         product = jnp.dot(left, right, preferred_element_type=jnp.float32)
         for q in range(2):
-            col = table_smem[right_at, kr, q]
+            col = table_smem[right_at, q, kb]
             weight = kept[q].astype(jnp.float32)
             for part in range(2):
                 acc_ref[row, col, part] += weight * product[
                     part * BS : (part + 1) * BS, q * BS : (q + 1) * BS
                 ]
-            mark(kept[q], row, col)
 
 
 def tables_to_smem(table_buf, whole_buf, table_smem, sem):
@@ -223,11 +220,9 @@
                 table_smem,
                 2 * i,
                 2 * i + 1,
-                k,
                 (i % 2) * HALF + k,
                 lambda slot, part: left_buf[i, pl.ds(base + (2 * slot + part) * BS, BS), :],
                 lambda slot, part: right_buf[i, pl.ds(base + (2 * slot + part) * BS, BS), :],
-                lambda kept, row, col: None,
             )
             return carry
 
@@ -314,11 +309,11 @@
             list_smem[GR * KB] = count + 1
 
     for h in range(2):
-        for k in range(HALF):
+        for kb in range(h * HALF, (h + 1) * HALF):
             for m in range(2):
-                kept = kept_pairs(table_smem, h, 2, k, h * HALF + k, m)
+                kept = kept_pairs(table_smem, h, 2, kb, m)
                 for q in range(2):
-                    mark(kept[q], table_smem[h, k, m], table_smem[2, h * HALF + k, q])
+                    mark(kept[q], table_smem[h, m, kb], table_smem[2, q, kb])
 
     for h in range(2):
 
@@ -329,13 +324,11 @@
                 table_smem,
                 h,
                 2,
-                k,
                 h * HALF + k,
                 lambda slot, part: lefts[h][pl.ds(base + (2 * slot + part) * BS, BS), :],
                 lambda slot, part: right_ref[
                     pl.ds(h * CHUNK + base + (2 * slot + part) * BS, BS), :
                 ],
-                lambda kept, row, col: None,
             )
             return carry
 

time: 111 us -> 111 us (level)
  the two profiles are of different devices: /device:TPU:1 before, /device:TPU:24 now
where the time goes in v3:
time: 111 us
  waiting for transfers between devices  61.6 us (55%)
  Pallas kernels  24.7 us (22%)
  starting transfers between devices  23.8 us (21%)
    ppermute x14, waiting for transfers between devices, shifted(): lax.ppermute(value, axis, [(i, (i + steps) % count) for i in range(count)])  53.2 us
    ppermute x14, starting transfers between devices, shifted(): lax.ppermute(value, axis, [(i, (i + steps) % count) for i in range(count)])  20.8 us
    pallas_call x3, Pallas kernels, multiply(): pl.pallas_call(kernel, out_shape=pltpu.VMEM((GR, KB, 2, BS, BS), jnp.floa...  15.9 us
    ppermute x6, waiting for transfers between devices, crossed(): return lax.ppermute(value, axis, [(i, i ^ bit) for i in range(count)])  8.34 us
    ppermute x6, starting transfers between devices, crossed(): return lax.ppermute(value, axis, [(i, i ^ bit) for i in range(count)])  3.08 us
    pallas_call x2, Pallas kernels, pack_left(): pl.pallas_call(functools.partial(pack_left_kernel, half), out_shape=pltpu...  2.9 us
    pallas_call x1, Pallas kernels, finish(): pl.pallas_call(finish_kernel, out_shape=jax.ShapeDtypeStruct(old.shape, o...  2.9 us
  transfers between devices with their start and end apart: 20, of which 7 were waited for; matrix products, arithmetic and copies ran while one was open for 0% of the time, Pallas kernels for 18%

profile of v3, /device:TPU:24, one launch (start us, length us, event | category | flops | bytes accessed | tf_op | source)
XLA Modules:
  0.0 110.6 jit_solution(4212378729203123747)
XLA Ops:
  0.0 2.0 %shard_map.82.refs_1_ = bf16[2064,128]{1,0:T(8,128)(2,1)} custom-call(s32[2,8]{1,0:T(2,128)} %bitcast.31, s32[1,8]{1,0:T(1,128)} %count_hbm.3, s32[2,8]{1,0:T(2,128)} %bitcast.33, bf16[4096,128]{1,0:T(8,128)(2,1)} %bitcast.23), custom_call_target="tpu_custom_call" | custom-call | tf_op jit(solution)/shard_map/pallas_call | solution.py:55
  2.1 0.0 copy-start.2
  2.1 0.0 copy-start.3
  2.1 0.0 copy-start.4
  2.1 2.0 %collective-permute-start = (bf16[2064,128]{1,0:T(8,128)(2,1)}, bf16[2064,128]{1,0:T(8,128)(2,1)}, u32[]{:S(2)}, u32[]{:S(2)}) collective-permute-start(bf16[2064,128]{1,0:T(8,128)(2,1)} %shard_map.82.refs_1_), channel_id=1, source_target_pairs={{0,1},{1,2},{2,3},{3,4},{4,5},{5,6},{6,7},{7,0},{8,9},{9,10},{10,1... | collective-permute-start | bytes 1585160 | tf_op jit(solution)/shard_map/ppermute | solution.py:109
  4.1 0.9 shard_map.83.refs_2_
  5.0 2.0 %collective-permute-start.11 = (bf16[2064,128]{1,0:T(8,128)(2,1)}, bf16[2064,128]{1,0:T(8,128)(2,1)}, u32[]{:S(2)}, u32[]{:S(2)}) collective-permute-start(bf16[2064,128]{1,0:T(8,128)(2,1)} %shard_map.83.refs_2_), channel_id=1, source_target_pairs={{0,1},{1,2},{2,3},{3,4},{4,5},{5,6},{6,7},{7,0},{8,9},{9,10},{10,1... | collective-permute-start | bytes 1585160 | tf_op jit(solution)/shard_map/ppermute | solution.py:109
  7.0 2.2 %collective-permute-start.14 = (bf16[2064,128]{1,0:T(8,128)(2,1)}, bf16[2064,128]{1,0:T(8,128)(2,1)}, u32[]{:S(2)}, u32[]{:S(2)}) collective-permute-start(bf16[2064,128]{1,0:T(8,128)(2,1)} %shard_map.82.refs_1_), channel_id=1, source_target_pairs={{0,7},{1,0},{2,1},{3,2},{4,3},{5,4},{6,5},{7,6},{8,15},{9,8},{10,9... | collective-permute-start | bytes 1585160 | tf_op jit(solution)/shard_map/ppermute | solution.py:109
  9.2 0.1 shard_map.86.refs_7_.refs_5_
  9.3 1.6 %collective-permute-start.18 = (bf16[4112,128]{1,0:T(8,128)(2,1)S(1)}, bf16[4112,128]{1,0:T(8,128)(2,1)}, u32[]{:S(2)}, u32[]{:S(2)}) collective-permute-start(bf16[4112,128]{1,0:T(8,128)(2,1)S(1)} %shard_map.86.refs_7_.refs_5_), channel_id=1, source_target_pairs={{0,16},{8,24},{16,0},{24,8},{1,17},{9,25},{17,1},{25,9},{2,18},{10... | collective-permute-start | bytes 3158024 | tf_op jit(solution)/shard_map/ppermute | solution.py:114
  10.9 0.0 collective-permute-start.17
  10.9 0.1 shard_map.84.refs_0_.refs_9_.refs_5_
  11.0 10.2 %collective-permute-done.refs_3_ = bf16[2064,128]{1,0:T(8,128)(2,1)} collective-permute-done((bf16[2064,128]{1,0:T(8,128)(2,1)}, bf16[2064,128]{1,0:T(8,128)(2,1)}, u32[]{:S(2)}, u32[]{:S(2)}) %collective-permute-start) | collective-permute-done | bytes 528416 | tf_op jit(solution)/shard_map/ppermute | solution.py:109
  21.2 1.5 %collective-permute-start.9 = (bf16[4112,128]{1,0:T(8,128)(2,1)S(1)}, bf16[4112,128]{1,0:T(8,128)(2,1)S(1)}, u32[]{:S(2)}, u32[]{:S(2)}) collective-permute-start(bf16[4112,128]{1,0:T(8,128)(2,1)S(1)} %shard_map.84.refs_0_.refs_9_.refs_5_), channel_id=1, source_target_pairs={{0,16},{8,24},{16,0},{24,8},{1,17},{9,25},{17,1},{25,9},{2,18},{10... | collective-permute-start | bytes 3158024 | tf_op jit(solution)/shard_map/ppermute | solution.py:114
  22.7 9.0 %collective-permute-done.11.refs_4_ = bf16[2064,128]{1,0:T(8,128)(2,1)} collective-permute-done((bf16[2064,128]{1,0:T(8,128)(2,1)}, bf16[2064,128]{1,0:T(8,128)(2,1)}, u32[]{:S(2)}, u32[]{:S(2)}) %collective-permute-start.11) | collective-permute-done | bytes 528416 | tf_op jit(solution)/shard_map/ppermute | solution.py:109
  31.7 1.7 %collective-permute-start.4 = (bf16[2064,128]{1,0:T(8,128)(2,1)}, bf16[2064,128]{1,0:T(8,128)(2,1)S(1)}, u32[]{:S(2)}, u32[]{:S(2)}) collective-permute-start(bf16[2064,128]{1,0:T(8,128)(2,1)} %shard_map.83.refs_2_), channel_id=1, source_target_pairs={{0,7},{1,0},{2,1},{3,2},{4,3},{5,4},{6,5},{7,6},{8,15},{9,8},{10,9... | collective-permute-start | bytes 1585160 | tf_op jit(solution)/shard_map/ppermute | solution.py:109
  33.4 0.0 collective-permute-done.14.refs_5_
  33.4 0.0 collective-permute-start.8
  33.4 11.6 %collective-permute-done.4.refs_6_ = bf16[2064,128]{1,0:T(8,128)(2,1)S(1)} collective-permute-done((bf16[2064,128]{1,0:T(8,128)(2,1)}, bf16[2064,128]{1,0:T(8,128)(2,1)S(1)}, u32[]{:S(2)}, u32[]{:S(2)}) %collective-permute-start.4) | collective-permute-done | bytes 528416 | tf_op jit(solution)/shard_map/ppermute | solution.py:109
  45.1 0.0 collective-permute-start.1
  45.1 0.0 collective-permute-done.18.refs_9_.refs_7_
  45.1 3.2 %collective-permute-start.5 = (bf16[2064,128]{1,0:T(8,128)(2,1)S(1)}, bf16[2064,128]{1,0:T(8,128)(2,1)S(1)}, u32[]{:S(2)}, u32[]{:S(2)}) collective-permute-start(bf16[2064,128]{1,0:T(8,128)(2,1)S(1)} %collective-permute-done.4.refs_6_), channel_id=1, source_target_pairs={{0,7},{1,0},{2,1},{3,2},{4,3},{5,4},{6,5},{7,6},{8,15},{9,8},{10,9... | collective-permute-start | bytes 1585160 | tf_op jit(solution)/shard_map/ppermute | solution.py:109
  48.3 0.0 collective-permute-done.17.refs_8_.refs_6_
  48.3 0.0 collective-permute-start.12
  48.3 8.3 %collective-permute-done.9.refs_2_.refs_11_.refs_7_ = bf16[4112,128]{1,0:T(8,128)(2,1)S(1)} collective-permute-done((bf16[4112,128]{1,0:T(8,128)(2,1)S(1)}, bf16[4112,128]{1,0:T(8,128)(2,1)S(1)}, u32[]{:S(2)}, u32[]{:S(2)}) %collective-permute-start.9) | collective-permute-done | bytes 1052704 | tf_op jit(solution)/shard_map/ppermute | solution.py:114
  56.6 0.0 collective-permute-start.19
  56.6 0.0 collective-permute-done.8.refs_1_.refs_10_.refs_6_
  56.6 1.7 %collective-permute-start.15 = (bf16[2064,128]{1,0:T(8,128)(2,1)}, bf16[2064,128]{1,0:T(8,128)(2,1)S(1)}, u32[]{:S(2)}, u32[]{:S(2)}) collective-permute-start(bf16[2064,128]{1,0:T(8,128)(2,1)} %collective-permute-done.14.refs_5_), channel_id=1, source_target_pairs={{0,7},{1,0},{2,1},{3,2},{4,3},{5,4},{6,5},{7,6},{8,15},{9,8},{10,9... | collective-permute-start | bytes 1585160 | tf_op jit(solution)/shard_map/ppermute | solution.py:109
  58.4 3.0 %collective-permute-done.1.refs_1_ = bf16[2064,128]{1,0:T(8,128)(2,1)S(1)} collective-permute-done((bf16[2064,128]{1,0:T(8,128)(2,1)}, bf16[2064,128]{1,0:T(8,128)(2,1)S(1)}, u32[]{:S(2)}, u32[]{:S(2)}) %collective-permute-start.1) | collective-permute-done | bytes 528416 | tf_op jit(solution)/shard_map/ppermute | solution.py:109
  61.4 3.2 %collective-permute-start.6 = (bf16[2064,128]{1,0:T(8,128)(2,1)S(1)}, bf16[2064,128]{1,0:T(8,128)(2,1)S(1)}, u32[]{:S(2)}, u32[]{:S(2)}) collective-permute-start(bf16[2064,128]{1,0:T(8,128)(2,1)S(1)} %collective-permute-done.5.refs_4_), channel_id=1, source_target_pairs={{0,7},{1,0},{2,1},{3,2},{4,3},{5,4},{6,5},{7,6},{8,15},{9,8},{10,9... | collective-permute-start | bytes 1585160 | tf_op jit(solution)/shard_map/ppermute | solution.py:109
  64.6 8.1 %collective-permute-done.12.refs_2_ = bf16[2064,128]{1,0:T(8,128)(2,1)S(1)} collective-permute-done((bf16[2064,128]{1,0:T(8,128)(2,1)}, bf16[2064,128]{1,0:T(8,128)(2,1)S(1)}, u32[]{:S(2)}, u32[]{:S(2)}) %collective-permute-start.12) | collective-permute-done | bytes 528416 | tf_op jit(solution)/shard_map/ppermute | solution.py:109
  72.7 11.3 %collective-permute-done.2.refs_1_ = bf16[2064,128]{1,0:T(8,128)(2,1)S(1)} collective-permute-done((bf16[2064,128]{1,0:T(8,128)(2,1)S(1)}, bf16[2064,128]{1,0:T(8,128)(2,1)S(1)}, u32[]{:S(2)}, u32[]{:S(2)}) %collective-permute-start.2) | collective-permute-done | bytes 528416 | tf_op jit(solution)/shard_map/ppermute | solution.py:109
  84.0 1.5 %collective-permute-start.16 = (bf16[2064,128]{1,0:T(8,128)(2,1)S(1)}, bf16[2064,128]{1,0:T(8,128)(2,1)S(1)}, u32[]{:S(2)}, u32[]{:S(2)}) collective-permute-start(bf16[2064,128]{1,0:T(8,128)(2,1)S(1)} %collective-permute-done.15.refs_3_), channel_id=1, source_target_pairs={{0,7},{1,0},{2,1},{3,2},{4,3},{5,4},{6,5},{7,6},{8,15},{9,8},{10,9... | collective-permute-start | bytes 1585160 | tf_op jit(solution)/shard_map/ppermute | solution.py:109
  85.5 0.0 collective-permute-done.6.refs_4_
  85.5 0.6 collective-permute-start.3
  86.0 0.0 collective-permute-done.19.refs_10_.refs_8_
  86.1 2.7 %collective-permute-start.7 = (bf16[2064,128]{1,0:T(8,128)(2,1)S(1)}, bf16[2064,128]{1,0:T(8,128)(2,1)S(1)}, u32[]{:S(2)}, u32[]{:S(2)}) collective-permute-start(bf16[2064,128]{1,0:T(8,128)(2,1)S(1)} %collective-permute-done.6.refs_4_), channel_id=1, source_target_pairs={{0,7},{1,0},{2,1},{3,2},{4,3},{5,4},{6,5},{7,6},{8,15},{9,8},{10,9... | collective-permute-start | bytes 1585160 | tf_op jit(solution)/shard_map/ppermute | solution.py:109
  88.7 0.1 pad_add_fusion.where_ref.refs_0_
  88.8 6.9 %shard_map.87.refs_13_ = f32[8,8,2,128,128]{4,3,2,1,0:T(8,128)S(1)} custom-call(s32[2]{0:T(128)S(1)} %pad_add_fusion.where_ref.refs_0_, bf16[2064,128]{1,0:T(8,128)(2,1)} %shard_map.82.refs_1_, bf16[2064,128]{1,0:T(8,128)(2,1)} %shard_map.83.refs_2_, bf16[2064,128]{1,0:T(8,128)(2,1)} %collective-permute-done.refs_3_, ...), custom_call_target="tpu_custom_call" | custom-call | tf_op jit(solution)/shard_map/pallas_call | solution.py:405
  95.7 0.0 collective-permute-done.10.refs_3_.refs_12_.refs_8_
  95.7 4.6 %shard_map.88.refs_9_ = f32[8,8,2,128,128]{4,3,2,1,0:T(8,128)S(1)} custom-call(s32[2]{0:T(128)S(1)} %pad_add_fusion.where_ref.refs_0_, bf16[2064,128]{1,0:T(8,128)(2,1)S(1)} %collective-permute-done.1.refs_1_, bf16[2064,128]{1,0:T(8,128)(2,1)S(1)} %collective-permute-done.12.refs_2_, ...), custom_call_target="tpu_custom_call", output_to_operand_aliasing={{}: (13, {})} | custom-call | tf_op jit(solution)/shard_map/pallas_call | solution.py:405
  100.4 0.0 collective-permute-done.16.refs_3_
  100.4 4.4 %shard_map.89.acc_ref = f32[8,8,2,128,128]{4,3,2,1,0:T(8,128)S(1)} custom-call(s32[2]{0:T(128)S(1)} %pad_add_fusion.where_ref.refs_0_, bf16[2064,128]{1,0:T(8,128)(2,1)S(1)} %collective-permute-done.2.refs_1_, bf16[2064,128]{1,0:T(8,128)(2,1)S(1)} %collective-permute-done.13.refs_2_, ...), custom_call_target="tpu_custom_call", output_to_operand_aliasing={{}: (9, {})} | custom-call | tf_op jit(solution)/shard_map/pallas_call | solution.py:405
  104.8 2.1 %shard_map.90.old_ref = bf16[8,8,2,128,128]{4,3,2,1,0:T(8,128)(2,1)} custom-call(f32[8,8,2,128,128]{4,3,2,1,0:T(8,128)S(1)} %shard_map.89.acc_ref), custom_call_target="tpu_custom_call" | custom-call | tf_op jit(solution)/shard_map/pallas_call | solution.py:275
  106.8 0.7 shard_map.85.right_ref
  107.5 0.0 collective-permute-done.3.up_ref
  107.5 0.0 collective-permute-done.7.down_ref
  107.5 2.9 %shard_map.91 = bf16[8,8,2,128,128]{4,3,2,1,0:T(8,128)(2,1)} custom-call(bf16[2064,128]{1,0:T(8,128)(2,1)S(1)} %collective-permute-done.3.up_ref, bf16[2064,128]{1,0:T(8,128)(2,1)S(1)} %collective-permute-done.7.down_ref, bf16[4112,128]{1,0:T(8,128)(2,1)S(1)} %shard_map.85.right_ref, ...), custom_call_target="tpu_custom_call", output_to_operand_aliasing={{}: (4, {})} | custom-call | tf_op jit(solution)/shard_map/pallas_call | solution.py:356
  (19 shorter events, 0.0 us)
Async XLA Ops:
  0.0 4.1 %copy-start.5 = (s32[1,8,2]{1,2,0:T(2,128)S(1)}, s32[1,8,2]{1,2,0:T(2,128)}, u32[]{:S(2)}) copy-start(s32[1,8,2]{1,2,0:T(2,128)} %param.9) | copy-start | bytes 196
  0.0 4.1 %copy-start.6 = (s32[1,8,2]{1,2,0:T(2,128)S(1)}, s32[1,8,2]{1,2,0:T(2,128)}, u32[]{:S(2)}) copy-start(s32[1,8,2]{1,2,0:T(2,128)} %param.11) | copy-start | bytes 196
  0.0 4.1 %copy-start.1 = (bf16[1,8,2,2,128,128]{5,4,3,2,1,0:T(8,128)(2,1)S(1)}, bf16[1,8,2,2,128,128]{5,4,3,2,1,0:T(8,128)(2,1)}, u32[]{:S(2)}) copy-start(bf16[1,8,2,2,128,128]{5,4,3,2,1,0:T(8,128)(2,1)} %param.8) | copy-start | bytes 3145732
  0.0 4.1 %copy-start.7 = (s32[1,8]{1,0:T(1,128)S(1)}, s32[1,8]{1,0:T(1,128)}, u32[]{:S(2)}) copy-start(s32[1,8]{1,0:T(1,128)} %count_hbm.3) | copy-start | bytes 100
  0.0 9.1 %copy-start = (bf16[2,8,1,2,2,128,128]{6,5,4,3,2,1,0:T(8,128)(2,1)S(1)}, bf16[2,8,1,2,2,128,128]{6,5,4,3,2,1,0:T(8,128)(2,1)}, u32[]{:S(2)}) copy-start(bf16[2,8,1,2,2,128,128]{6,5,4,3,2,1,0:T(8,128)(2,1)} %param.12) | copy-start | bytes 6291460
  2.1 7.1 %copy-start.2 = (s32[2,8,1,2]{1,3,2,0:T(2,128)S(1)}, s32[2,8,1,2]{1,3,2,0:T(2,128)}, u32[]{:S(2)}) copy-start(s32[2,8,1,2]{1,3,2,0:T(2,128)} %param.13) | copy-start | bytes 388
  2.1 7.1 %copy-start.3 = (s32[2,8,1,2]{1,3,2,0:T(2,128)S(1)}, s32[2,8,1,2]{1,3,2,0:T(2,128)}, u32[]{:S(2)}) copy-start(s32[2,8,1,2]{1,3,2,0:T(2,128)} %param.15) | copy-start | bytes 388
  2.1 7.1 %copy-start.4 = (s32[2,8,1]{1,2,0:T(1,128)S(1)}, s32[2,8,1]{1,2,0:T(1,128)}, u32[]{:S(2)}) copy-start(s32[2,8,1]{1,2,0:T(1,128)} %param.14) | copy-start | bytes 196
  2.1 19.1 %collective-permute-start = (bf16[2064,128]{1,0:T(8,128)(2,1)}, bf16[2064,128]{1,0:T(8,128)(2,1)}, u32[]{:S(2)}, u32[]{:S(2)}) collective-permute-start(bf16[2064,128]{1,0:T(8,128)(2,1)} %shard_map.82.refs_1_), channel_id=1, source_target_pairs={{0,1},{1,2},{2,3},{3,4},{4,5},{5,6},{6,7},{7,0},{8,9},{9,10},{10,1... | collective-permute-start | bytes 1585160 | tf_op jit(solution)/shard_map/ppermute | solution.py:109
  5.0 26.7 %collective-permute-start.11 = (bf16[2064,128]{1,0:T(8,128)(2,1)}, bf16[2064,128]{1,0:T(8,128)(2,1)}, u32[]{:S(2)}, u32[]{:S(2)}) collective-permute-start(bf16[2064,128]{1,0:T(8,128)(2,1)} %shard_map.83.refs_2_), channel_id=1, source_target_pairs={{0,1},{1,2},{2,3},{3,4},{4,5},{5,6},{6,7},{7,0},{8,9},{9,10},{10,1... | collective-permute-start | bytes 1585160 | tf_op jit(solution)/shard_map/ppermute | solution.py:109
  7.0 26.4 %collective-permute-start.14 = (bf16[2064,128]{1,0:T(8,128)(2,1)}, bf16[2064,128]{1,0:T(8,128)(2,1)}, u32[]{:S(2)}, u32[]{:S(2)}) collective-permute-start(bf16[2064,128]{1,0:T(8,128)(2,1)} %shard_map.82.refs_1_), channel_id=1, source_target_pairs={{0,7},{1,0},{2,1},{3,2},{4,3},{5,4},{6,5},{7,6},{8,15},{9,8},{10,9... | collective-permute-start | bytes 1585160 | tf_op jit(solution)/shard_map/ppermute | solution.py:109
  9.3 35.8 %collective-permute-start.18 = (bf16[4112,128]{1,0:T(8,128)(2,1)S(1)}, bf16[4112,128]{1,0:T(8,128)(2,1)}, u32[]{:S(2)}, u32[]{:S(2)}) collective-permute-start(bf16[4112,128]{1,0:T(8,128)(2,1)S(1)} %shard_map.86.refs_7_.refs_5_), channel_id=1, source_target_pairs={{0,16},{8,24},{16,0},{24,8},{1,17},{9,25},{17,1},{25,9},{2,18},{10... | collective-permute-start | bytes 3158024 | tf_op jit(solution)/shard_map/ppermute | solution.py:114
  10.9 37.4 %collective-permute-start.17 = (bf16[4112,128]{1,0:T(8,128)(2,1)S(1)}, bf16[4112,128]{1,0:T(8,128)(2,1)}, u32[]{:S(2)}, u32[]{:S(2)}) collective-permute-start(bf16[4112,128]{1,0:T(8,128)(2,1)S(1)} %shard_map.86.refs_7_.refs_5_), channel_id=1, source_target_pairs={{0,8},{8,0},{16,24},{24,16},{1,9},{9,1},{17,25},{25,17},{2,10},{10... | collective-permute-start | bytes 3158024 | tf_op jit(solution)/shard_map/ppermute | solution.py:114
  21.2 35.4 %collective-permute-start.9 = (bf16[4112,128]{1,0:T(8,128)(2,1)S(1)}, bf16[4112,128]{1,0:T(8,128)(2,1)S(1)}, u32[]{:S(2)}, u32[]{:S(2)}) collective-permute-start(bf16[4112,128]{1,0:T(8,128)(2,1)S(1)} %shard_map.84.refs_0_.refs_9_.refs_5_), channel_id=1, source_target_pairs={{0,16},{8,24},{16,0},{24,8},{1,17},{9,25},{17,1},{25,9},{2,18},{10... | collective-permute-start | bytes 3158024 | tf_op jit(solution)/shard_map/ppermute | solution.py:114
  31.7 13.4 %collective-permute-start.4 = (bf16[2064,128]{1,0:T(8,128)(2,1)}, bf16[2064,128]{1,0:T(8,128)(2,1)S(1)}, u32[]{:S(2)}, u32[]{:S(2)}) collective-permute-start(bf16[2064,128]{1,0:T(8,128)(2,1)} %shard_map.83.refs_2_), channel_id=1, source_target_pairs={{0,7},{1,0},{2,1},{3,2},{4,3},{5,4},{6,5},{7,6},{8,15},{9,8},{10,9... | collective-permute-start | bytes 1585160 | tf_op jit(solution)/shard_map/ppermute | solution.py:109
  33.4 23.2 %collective-permute-start.8 = (bf16[4112,128]{1,0:T(8,128)(2,1)S(1)}, bf16[4112,128]{1,0:T(8,128)(2,1)S(1)}, u32[]{:S(2)}, u32[]{:S(2)}) collective-permute-start(bf16[4112,128]{1,0:T(8,128)(2,1)S(1)} %shard_map.84.refs_0_.refs_9_.refs_5_), channel_id=1, source_target_pairs={{0,8},{8,0},{16,24},{24,16},{1,9},{9,1},{17,25},{25,17},{2,10},{10... | collective-permute-start | bytes 3158024 | tf_op jit(solution)/shard_map/ppermute | solution.py:114
  45.1 16.3 %collective-permute-start.1 = (bf16[2064,128]{1,0:T(8,128)(2,1)}, bf16[2064,128]{1,0:T(8,128)(2,1)S(1)}, u32[]{:S(2)}, u32[]{:S(2)}) collective-permute-start(bf16[2064,128]{1,0:T(8,128)(2,1)} %collective-permute-done.refs_3_), channel_id=1, source_target_pairs={{0,1},{1,2},{2,3},{3,4},{4,5},{5,6},{6,7},{7,0},{8,9},{9,10},{10,1... | collective-permute-start | bytes 1585160 | tf_op jit(solution)/shard_map/ppermute | solution.py:109
  45.1 16.3 %collective-permute-start.5 = (bf16[2064,128]{1,0:T(8,128)(2,1)S(1)}, bf16[2064,128]{1,0:T(8,128)(2,1)S(1)}, u32[]{:S(2)}, u32[]{:S(2)}) collective-permute-start(bf16[2064,128]{1,0:T(8,128)(2,1)S(1)} %collective-permute-done.4.refs_6_), channel_id=1, source_target_pairs={{0,7},{1,0},{2,1},{3,2},{4,3},{5,4},{6,5},{7,6},{8,15},{9,8},{10,9... | collective-permute-start | bytes 1585160 | tf_op jit(solution)/shard_map/ppermute | solution.py:109
  48.3 24.4 %collective-permute-start.12 = (bf16[2064,128]{1,0:T(8,128)(2,1)}, bf16[2064,128]{1,0:T(8,128)(2,1)S(1)}, u32[]{:S(2)}, u32[]{:S(2)}) collective-permute-start(bf16[2064,128]{1,0:T(8,128)(2,1)} %collective-permute-done.11.refs_4_), channel_id=1, source_target_pairs={{0,1},{1,2},{2,3},{3,4},{4,5},{5,6},{6,7},{7,0},{8,9},{9,10},{10,1... | collective-permute-start | bytes 1585160 | tf_op jit(solution)/shard_map/ppermute | solution.py:109
  56.6 29.4 %collective-permute-start.19 = (bf16[4112,128]{1,0:T(8,128)(2,1)}, bf16[4112,128]{1,0:T(8,128)(2,1)S(1)}, u32[]{:S(2)}, u32[]{:S(2)}) collective-permute-start(bf16[4112,128]{1,0:T(8,128)(2,1)} %collective-permute-done.18.refs_9_.refs_7_), channel_id=1, source_target_pairs={{0,8},{8,0},{16,24},{24,16},{1,9},{9,1},{17,25},{25,17},{2,10},{10... | collective-permute-start | bytes 3158024 | tf_op jit(solution)/shard_map/ppermute | solution.py:114
  56.6 16.0 %collective-permute-start.15 = (bf16[2064,128]{1,0:T(8,128)(2,1)}, bf16[2064,128]{1,0:T(8,128)(2,1)S(1)}, u32[]{:S(2)}, u32[]{:S(2)}) collective-permute-start(bf16[2064,128]{1,0:T(8,128)(2,1)} %collective-permute-done.14.refs_5_), channel_id=1, source_target_pairs={{0,7},{1,0},{2,1},{3,2},{4,3},{5,4},{6,5},{7,6},{8,15},{9,8},{10,9... | collective-permute-start | bytes 1585160 | tf_op jit(solution)/shard_map/ppermute | solution.py:109
  61.4 22.6 %collective-permute-start.2 = (bf16[2064,128]{1,0:T(8,128)(2,1)S(1)}, bf16[2064,128]{1,0:T(8,128)(2,1)S(1)}, u32[]{:S(2)}, u32[]{:S(2)}) collective-permute-start(bf16[2064,128]{1,0:T(8,128)(2,1)S(1)} %collective-permute-done.1.refs_1_), channel_id=1, source_target_pairs={{0,1},{1,2},{2,3},{3,4},{4,5},{5,6},{6,7},{7,0},{8,9},{9,10},{10,1... | collective-permute-start | bytes 1585160 | tf_op jit(solution)/shard_map/ppermute | solution.py:109
  61.4 24.1 %collective-permute-start.6 = (bf16[2064,128]{1,0:T(8,128)(2,1)S(1)}, bf16[2064,128]{1,0:T(8,128)(2,1)S(1)}, u32[]{:S(2)}, u32[]{:S(2)}) collective-permute-start(bf16[2064,128]{1,0:T(8,128)(2,1)S(1)} %collective-permute-done.5.refs_4_), channel_id=1, source_target_pairs={{0,7},{1,0},{2,1},{3,2},{4,3},{5,4},{6,5},{7,6},{8,15},{9,8},{10,9... | collective-permute-start | bytes 1585160 | tf_op jit(solution)/shard_map/ppermute | solution.py:109
  72.7 23.0 %collective-permute-start.10 = (bf16[4112,128]{1,0:T(8,128)(2,1)S(1)}, bf16[4112,128]{1,0:T(8,128)(2,1)S(1)}, u32[]{:S(2)}, u32[]{:S(2)}) collective-permute-start(bf16[4112,128]{1,0:T(8,128)(2,1)S(1)} %collective-permute-done.9.refs_2_.refs_11_.refs_7_), channel_id=1, source_target_pairs={{0,8},{8,0},{16,24},{24,16},{1,9},{9,1},{17,25},{25,17},{2,10},{10... | collective-permute-start | bytes 3158024 | tf_op jit(solution)/shard_map/ppermute | solution.py:114
  72.7 27.7 %collective-permute-start.13 = (bf16[2064,128]{1,0:T(8,128)(2,1)S(1)}, bf16[2064,128]{1,0:T(8,128)(2,1)S(1)}, u32[]{:S(2)}, u32[]{:S(2)}) collective-permute-start(bf16[2064,128]{1,0:T(8,128)(2,1)S(1)} %collective-permute-done.12.refs_2_), channel_id=1, source_target_pairs={{0,1},{1,2},{2,3},{3,4},{4,5},{5,6},{6,7},{7,0},{8,9},{9,10},{10,1... | collective-permute-start | bytes 1585160 | tf_op jit(solution)/shard_map/ppermute | solution.py:109
  84.0 16.4 %collective-permute-start.16 = (bf16[2064,128]{1,0:T(8,128)(2,1)S(1)}, bf16[2064,128]{1,0:T(8,128)(2,1)S(1)}, u32[]{:S(2)}, u32[]{:S(2)}) collective-permute-start(bf16[2064,128]{1,0:T(8,128)(2,1)S(1)} %collective-permute-done.15.refs_3_), channel_id=1, source_target_pairs={{0,7},{1,0},{2,1},{3,2},{4,3},{5,4},{6,5},{7,6},{8,15},{9,8},{10,9... | collective-permute-start | bytes 1585160 | tf_op jit(solution)/shard_map/ppermute | solution.py:109
  85.5 22.0 %collective-permute-start.3 = (bf16[2064,128]{1,0:T(8,128)(2,1)S(1)}, bf16[2064,128]{1,0:T(8,128)(2,1)S(1)}, u32[]{:S(2)}, u32[]{:S(2)}) collective-permute-start(bf16[2064,128]{1,0:T(8,128)(2,1)S(1)} %collective-permute-done.2.refs_1_), channel_id=1, source_target_pairs={{0,1},{1,2},{2,3},{3,4},{4,5},{5,6},{6,7},{7,0},{8,9},{9,10},{10,1... | collective-permute-start | bytes 1585160 | tf_op jit(solution)/shard_map/ppermute | solution.py:109
  86.1 21.5 %collective-permute-start.7 = (bf16[2064,128]{1,0:T(8,128)(2,1)S(1)}, bf16[2064,128]{1,0:T(8,128)(2,1)S(1)}, u32[]{:S(2)}, u32[]{:S(2)}) collective-permute-start(bf16[2064,128]{1,0:T(8,128)(2,1)S(1)} %collective-permute-done.6.refs_4_), channel_id=1, source_target_pairs={{0,7},{1,0},{2,1},{3,2},{4,3},{5,4},{6,5},{7,6},{8,15},{9,8},{10,9... | collective-permute-start | bytes 1585160 | tf_op jit(solution)/shard_map/ppermute | solution.py:109

commit v4 on v3

--- a/solution.py
+++ b/solution.py
@@ -12,6 +12,7 @@
 BS = 128
 LEVEL_CUT = 7
 HALF = 4
+QUARTER = 2
 BLOCK_ROWS = 2 * 2 * BS
 META = 16
 UNROLL = 4
@@ -285,14 +286,64 @@
     )(total)
 
 
+def add_last(acc_ref, table_smem, lefts, right_ref, skipped):
+    for h in range(2):
+
+        def one_kb(k, carry, h=h):
+            kb = h * HALF + skipped + k
+            base = pl.multiple_of(k * BLOCK_ROWS, BLOCK_ROWS)
+            add_products(
+                acc_ref,
+                table_smem,
+                h,
+                2,
+                kb,
+                lambda slot, part: lefts[h][pl.ds(base + (2 * slot + part) * BS, BS), :],
+                lambda slot, part: right_ref[
+                    pl.ds(kb * BLOCK_ROWS + (2 * slot + part) * BS, BS), :
+                ],
+            )
+            return carry
+
+        lax.fori_loop(0, QUARTER, one_kb, 0, unroll=QUARTER)
+
+
+def load_tables(up_ref, down_ref, right_ref, table_buf):
+    table_buf[0] = up_ref[pl.ds(QUARTER * BLOCK_ROWS, META), :]
+    table_buf[1] = down_ref[pl.ds(QUARTER * BLOCK_ROWS, META), :]
+    table_buf[2] = right_ref[pl.ds(PANEL, META), :]
+
+
+def fourth_kernel(
+    up_ref, down_ref, right_ref, total_ref, acc_ref, table_buf, whole_buf, table_smem, smem_sem
+):
+    load_tables(up_ref, down_ref, right_ref, table_buf)
+    tables_to_smem(table_buf, whole_buf, table_smem, smem_sem)
+    add_last(acc_ref, table_smem, (up_ref, down_ref), right_ref, HALF - QUARTER)
+
+
+def fourth(up, down, right, total):
+    return pl.pallas_call(
+        fourth_kernel,
+        out_shape=pltpu.VMEM(total.shape, jnp.float32),
+        in_specs=[pl.BlockSpec(memory_space=pltpu.VMEM)] * 4,
+        out_specs=pl.BlockSpec(memory_space=pltpu.VMEM),
+        input_output_aliases={3: 0},
+        scratch_shapes=[
+            pltpu.VMEM((3, META, BS), jnp.bfloat16),
+            pltpu.VMEM((3, KB, BS), jnp.int32),
+            pltpu.SMEM((3, KB, BS), jnp.int32),
+            pltpu.SemaphoreType.DMA,
+        ],
+        compiler_params=pltpu.CompilerParams(vmem_limit_bytes=5 * MIB),
+    )(up, down, right, total)
+
+
 def finish_kernel(
-    up_ref, down_ref, right_ref, acc_ref, old_ref, out_ref,
+    up_ref, down_ref, early_up_ref, early_down_ref, right_ref, acc_ref, old_ref, out_ref,
     stage_ref, table_buf, whole_buf, table_smem, flag_smem, list_smem, out_sem, smem_sem,
 ):
-    lefts = (up_ref, down_ref)
-    for h in range(2):
-        table_buf[h] = lefts[h][pl.ds(CHUNK, META), :]
-    table_buf[2] = right_ref[pl.ds(PANEL, META), :]
+    load_tables(early_up_ref, early_down_ref, right_ref, table_buf)
     for at in range(GR * KB):
         flag_smem[at] = 0
     list_smem[GR * KB] = 0
@@ -309,30 +360,13 @@
             list_smem[GR * KB] = count + 1
 
     for h in range(2):
-        for kb in range(h * HALF, (h + 1) * HALF):
+        for kb in range(h * HALF, h * HALF + QUARTER):
             for m in range(2):
                 kept = kept_pairs(table_smem, h, 2, kb, m)
                 for q in range(2):
                     mark(kept[q], table_smem[h, m, kb], table_smem[2, q, kb])
 
-    for h in range(2):
-
-        def one_kb(k, carry, h=h):
-            base = pl.multiple_of(k * BLOCK_ROWS, BLOCK_ROWS)
-            add_products(
-                acc_ref,
-                table_smem,
-                h,
-                2,
-                h * HALF + k,
-                lambda slot, part: lefts[h][pl.ds(base + (2 * slot + part) * BS, BS), :],
-                lambda slot, part: right_ref[
-                    pl.ds(h * CHUNK + base + (2 * slot + part) * BS, BS), :
-                ],
-            )
-            return carry
-
-        lax.fori_loop(0, HALF, one_kb, 0, unroll=UNROLL)
+    add_last(acc_ref, table_smem, (up_ref, down_ref), right_ref, 0)
 
     count = list_smem[GR * KB]
 
@@ -351,15 +385,15 @@
     lax.fori_loop(0, count, wait_block, 0)
 
 
-def finish(up, down, right, total, old):
-    most = 2 * HALF * 4
+def finish(late, early, right, total, old):
+    most = 2 * QUARTER * 4
     return pl.pallas_call(
         finish_kernel,
         out_shape=jax.ShapeDtypeStruct(old.shape, old.dtype),
-        in_specs=[pl.BlockSpec(memory_space=pltpu.VMEM)] * 4
+        in_specs=[pl.BlockSpec(memory_space=pltpu.VMEM)] * 6
         + [pl.BlockSpec(memory_space=pltpu.HBM)],
         out_specs=pl.BlockSpec(memory_space=pltpu.HBM),
-        input_output_aliases={4: 0},
+        input_output_aliases={6: 0},
         scratch_shapes=[
             pltpu.VMEM((most, 2, BS, BS), jnp.bfloat16),
             pltpu.VMEM((3, META, BS), jnp.bfloat16),
@@ -371,7 +405,7 @@
             pltpu.SemaphoreType.DMA,
         ],
         compiler_params=pltpu.CompilerParams(vmem_limit_bytes=5 * MIB),
-    )(up, down, right, total, old)
+    )(*late, *early, right, total, old)
 
 
 def multiply(where, items, rights, total, local):
@@ -441,7 +475,16 @@
         hops.append(
             [(up[0], -step, 0), (up[1], -step, 1), (down[0], step, 0), (down[1], step, 1)]
         )
-    hops.append([(shifted(up[0], "col", 1), -4, 0), (shifted(down[1], "col", -1), 4, 1)])
+    cut = QUARTER * BLOCK_ROWS
+
+    def part(value, begin, end):
+        return value[begin:end]
+
+    whole = CHUNK + META
+    soon = (
+        shifted(part(up[0], cut, whole), "col", 1), shifted(part(down[1], cut, whole), "col", -1)
+    )
+    late = (shifted(part(up[0], 0, cut), "col", 1), shifted(part(down[1], 0, cut), "col", -1))
     rights = []
     for s in range(2):
         partner = crossed(held[s], "row", 1)
@@ -455,8 +498,9 @@
     total = multiply(where, hops[1], rights, total, local)
     last_right = fetch(where, 4, rights[4:], local)
     total = multiply(where, hops[2], rights[4:], total, local)
+    total = fourth(*soon, last_right, total)
     early = flush(total)
-    return finish(hops[3][0][0], hops[3][1][0], last_right, total, early)
+    return finish(late, soon, last_right, total, early)
 
 
 def solution(mesh):

time: 111 us -> 115 us (1.036)
  the two profiles are of different devices: /device:TPU:24 before, /device:TPU:28 now
where the time goes in v4:
time: 115 us
  waiting for transfers between devices  58.4 us (51%)
  starting transfers between devices  30.4 us (26%)
  Pallas kernels  25.3 us (22%)
    ppermute x16, waiting for transfers between devices, shifted(): lax.ppermute(value, axis, [(i, (i + steps) % count) for i in range(count)])  54.5 us
    ppermute x16, starting transfers between devices, shifted(): lax.ppermute(value, axis, [(i, (i + steps) % count) for i in range(count)])  27.4 us
    pallas_call x3, Pallas kernels, multiply(): pl.pallas_call(kernel, out_shape=pltpu.VMEM((GR, KB, 2, BS, BS), jnp.floa...  15.9 us
    ppermute x6, waiting for transfers between devices, crossed(): return lax.ppermute(value, axis, [(i, i ^ bit) for i in range(count)])  3.88 us
    ppermute x6, starting transfers between devices, crossed(): return lax.ppermute(value, axis, [(i, i ^ bit) for i in range(count)])  3 us
    pallas_call x2, Pallas kernels, pack_left(): pl.pallas_call(functools.partial(pack_left_kernel, half), out_shape=pltpu...  2.9 us
  transfers between devices with their start and end apart: 22, of which 7 were waited for; matrix products, arithmetic and copies ran while one was open for 0% of the time, Pallas kernels for 18%

profile of v4, /device:TPU:28, one launch (start us, length us, event | category | flops | bytes accessed | tf_op | source)
XLA Modules:
  0.0 114.7 jit_solution(8737537526357824835)
XLA Ops:
  0.0 2.0 %shard_map.82.refs_1_ = bf16[2064,128]{1,0:T(8,128)(2,1)} custom-call(s32[2,8]{1,0:T(2,128)} %bitcast.31, s32[1,8]{1,0:T(1,128)} %count_hbm.3, s32[2,8]{1,0:T(2,128)} %bitcast.33, bf16[4096,128]{1,0:T(8,128)(2,1)} %bitcast.23), custom_call_target="tpu_custom_call" | custom-call | tf_op jit(solution)/shard_map/pallas_call | solution.py:56
  2.1 0.0 copy-start.2
  2.1 0.0 copy-start.3
  2.1 0.0 copy-start.4
  2.1 2.0 %collective-permute-start = (bf16[2064,128]{1,0:T(8,128)(2,1)}, bf16[2064,128]{1,0:T(8,128)(2,1)}, u32[]{:S(2)}, u32[]{:S(2)}) collective-permute-start(bf16[2064,128]{1,0:T(8,128)(2,1)} %shard_map.82.refs_1_), channel_id=1, source_target_pairs={{0,1},{1,2},{2,3},{3,4},{4,5},{5,6},{6,7},{7,0},{8,9},{9,10},{10,1... | collective-permute-start | bytes 1585160 | tf_op jit(solution)/shard_map/ppermute | solution.py:110
  4.1 0.9 shard_map.83.refs_2_
  5.0 2.0 %collective-permute-start.13 = (bf16[2064,128]{1,0:T(8,128)(2,1)}, bf16[2064,128]{1,0:T(8,128)(2,1)}, u32[]{:S(2)}, u32[]{:S(2)}) collective-permute-start(bf16[2064,128]{1,0:T(8,128)(2,1)} %shard_map.83.refs_2_), channel_id=1, source_target_pairs={{0,1},{1,2},{2,3},{3,4},{4,5},{5,6},{6,7},{7,0},{8,9},{9,10},{10,1... | collective-permute-start | bytes 1585160 | tf_op jit(solution)/shard_map/ppermute | solution.py:110
  7.0 0.1 shard_map.86.refs_7_.refs_5_
  7.1 1.3 %collective-permute-start.20 = (bf16[4112,128]{1,0:T(8,128)(2,1)S(1)}, bf16[4112,128]{1,0:T(8,128)(2,1)}, u32[]{:S(2)}, u32[]{:S(2)}) collective-permute-start(bf16[4112,128]{1,0:T(8,128)(2,1)S(1)} %shard_map.86.refs_7_.refs_5_), channel_id=1, source_target_pairs={{0,16},{8,24},{16,0},{24,8},{1,17},{9,25},{17,1},{25,9},{2,18},{10... | collective-permute-start | bytes 3158024 | tf_op jit(solution)/shard_map/ppermute | solution.py:115
  8.4 0.0 collective-permute-start.19
  8.4 2.1 %collective-permute-start.16 = (bf16[2064,128]{1,0:T(8,128)(2,1)}, bf16[2064,128]{1,0:T(8,128)(2,1)}, u32[]{:S(2)}, u32[]{:S(2)}) collective-permute-start(bf16[2064,128]{1,0:T(8,128)(2,1)} %shard_map.82.refs_1_), channel_id=1, source_target_pairs={{0,7},{1,0},{2,1},{3,2},{4,3},{5,4},{6,5},{7,6},{8,15},{9,8},{10,9... | collective-permute-start | bytes 1585160 | tf_op jit(solution)/shard_map/ppermute | solution.py:110
  10.6 0.1 shard_map.84.refs_0_.refs_9_.refs_5_
  10.7 10.5 %collective-permute-done.refs_3_ = bf16[2064,128]{1,0:T(8,128)(2,1)} collective-permute-done((bf16[2064,128]{1,0:T(8,128)(2,1)}, bf16[2064,128]{1,0:T(8,128)(2,1)}, u32[]{:S(2)}, u32[]{:S(2)}) %collective-permute-start) | collective-permute-done | bytes 528416 | tf_op jit(solution)/shard_map/ppermute | solution.py:110
  21.2 1.2 %collective-permute-start.11 = (bf16[4112,128]{1,0:T(8,128)(2,1)S(1)}, bf16[4112,128]{1,0:T(8,128)(2,1)S(1)}, u32[]{:S(2)}, u32[]{:S(2)}) collective-permute-start(bf16[4112,128]{1,0:T(8,128)(2,1)S(1)} %shard_map.84.refs_0_.refs_9_.refs_5_), channel_id=1, source_target_pairs={{0,16},{8,24},{16,0},{24,8},{1,17},{9,25},{17,1},{25,9},{2,18},{10... | collective-permute-start | bytes 3158024 | tf_op jit(solution)/shard_map/ppermute | solution.py:115
  22.4 9.3 %collective-permute-done.13.refs_4_ = bf16[2064,128]{1,0:T(8,128)(2,1)} collective-permute-done((bf16[2064,128]{1,0:T(8,128)(2,1)}, bf16[2064,128]{1,0:T(8,128)(2,1)}, u32[]{:S(2)}, u32[]{:S(2)}) %collective-permute-start.13) | collective-permute-done | bytes 528416 | tf_op jit(solution)/shard_map/ppermute | solution.py:110
  31.7 1.7 %collective-permute-start.4 = (bf16[2064,128]{1,0:T(8,128)(2,1)}, bf16[2064,128]{1,0:T(8,128)(2,1)S(1)}, u32[]{:S(2)}, u32[]{:S(2)}) collective-permute-start(bf16[2064,128]{1,0:T(8,128)(2,1)} %shard_map.83.refs_2_), channel_id=1, source_target_pairs={{0,7},{1,0},{2,1},{3,2},{4,3},{5,4},{6,5},{7,6},{8,15},{9,8},{10,9... | collective-permute-start | bytes 1585160 | tf_op jit(solution)/shard_map/ppermute | solution.py:110
  33.4 0.3 collective-permute-start.1
  33.7 11.4 %collective-permute-done.4.refs_6_ = bf16[2064,128]{1,0:T(8,128)(2,1)S(1)} collective-permute-done((bf16[2064,128]{1,0:T(8,128)(2,1)}, bf16[2064,128]{1,0:T(8,128)(2,1)S(1)}, u32[]{:S(2)}, u32[]{:S(2)}) %collective-permute-start.4) | collective-permute-done | bytes 528416 | tf_op jit(solution)/shard_map/ppermute | solution.py:110
  45.1 0.0 collective-permute-start.14
  45.1 0.0 collective-permute-done.20.refs_9_.refs_7_
  45.1 3.2 %collective-permute-start.17 = (bf16[2064,128]{1,0:T(8,128)(2,1)}, bf16[2064,128]{1,0:T(8,128)(2,1)S(1)}, u32[]{:S(2)}, u32[]{:S(2)}) collective-permute-start(bf16[2064,128]{1,0:T(8,128)(2,1)} %collective-permute-done.16.refs_5_), channel_id=1, source_target_pairs={{0,7},{1,0},{2,1},{3,2},{4,3},{5,4},{6,5},{7,6},{8,15},{9,8},{10,9... | collective-permute-start | bytes 1585160 | tf_op jit(solution)/shard_map/ppermute | solution.py:110
  48.3 0.0 collective-permute-done.19.refs_8_.refs_6_
  48.3 1.5 %collective-permute-start.5 = (bf16[2064,128]{1,0:T(8,128)(2,1)S(1)}, bf16[2064,128]{1,0:T(8,128)(2,1)S(1)}, u32[]{:S(2)}, u32[]{:S(2)}) collective-permute-start(bf16[2064,128]{1,0:T(8,128)(2,1)S(1)} %collective-permute-done.4.refs_6_), channel_id=1, source_target_pairs={{0,7},{1,0},{2,1},{3,2},{4,3},{5,4},{6,5},{7,6},{8,15},{9,8},{10,9... | collective-permute-start | bytes 1585160 | tf_op jit(solution)/shard_map/ppermute | solution.py:110
  49.8 0.0 collective-permute-done.1.refs_1_
  49.8 0.6 collective-permute-start.2
  50.3 3.9 %collective-permute-done.11.refs_2_.refs_11_.refs_7_ = bf16[4112,128]{1,0:T(8,128)(2,1)S(1)} collective-permute-done((bf16[4112,128]{1,0:T(8,128)(2,1)S(1)}, bf16[4112,128]{1,0:T(8,128)(2,1)S(1)}, u32[]{:S(2)}, u32[]{:S(2)}) %collective-permute-start.11) | collective-permute-done | bytes 1052704 | tf_op jit(solution)/shard_map/ppermute | solution.py:115
  54.2 7.2 %collective-permute-done.14.refs_2_ = bf16[2064,128]{1,0:T(8,128)(2,1)S(1)} collective-permute-done((bf16[2064,128]{1,0:T(8,128)(2,1)}, bf16[2064,128]{1,0:T(8,128)(2,1)S(1)}, u32[]{:S(2)}, u32[]{:S(2)}) %collective-permute-start.14) | collective-permute-done | bytes 528416 | tf_op jit(solution)/shard_map/ppermute | solution.py:110
  61.4 0.0 collective-permute-start.21
  61.4 0.0 collective-permute-done.17.refs_3_
  61.4 0.5 collective-permute-start.12
  61.9 7.5 %collective-permute-done.5.refs_4_ = bf16[2064,128]{1,0:T(8,128)(2,1)S(1)} collective-permute-done((bf16[2064,128]{1,0:T(8,128)(2,1)S(1)}, bf16[2064,128]{1,0:T(8,128)(2,1)S(1)}, u32[]{:S(2)}, u32[]{:S(2)}) %collective-permute-start.5) | collective-permute-done | bytes 528416 | tf_op jit(solution)/shard_map/ppermute | solution.py:110
  69.4 3.7 %collective-permute-start.6 = (bf16[2064,128]{1,0:T(8,128)(2,1)S(1)}, bf16[2064,128]{1,0:T(8,128)(2,1)S(1)}, u32[]{:S(2)}, u32[]{:S(2)}) collective-permute-start(bf16[2064,128]{1,0:T(8,128)(2,1)S(1)} %collective-permute-done.5.refs_4_), channel_id=1, source_target_pairs={{0,7},{1,0},{2,1},{3,2},{4,3},{5,4},{6,5},{7,6},{8,15},{9,8},{10,9... | collective-permute-start | bytes 1585160 | tf_op jit(solution)/shard_map/ppermute | solution.py:110
  73.1 8.7 %collective-permute-done.6.refs_4_ = bf16[2064,128]{1,0:T(8,128)(2,1)S(1)} collective-permute-done((bf16[2064,128]{1,0:T(8,128)(2,1)S(1)}, bf16[2064,128]{1,0:T(8,128)(2,1)S(1)}, u32[]{:S(2)}, u32[]{:S(2)}) %collective-permute-start.6) | collective-permute-done | bytes 528416 | tf_op jit(solution)/shard_map/ppermute | solution.py:110
  81.8 3.7 %collective-permute-start.18 = (bf16[2064,128]{1,0:T(8,128)(2,1)S(1)}, bf16[2064,128]{1,0:T(8,128)(2,1)S(1)}, u32[]{:S(2)}, u32[]{:S(2)}) collective-permute-start(bf16[2064,128]{1,0:T(8,128)(2,1)S(1)} %collective-permute-done.17.refs_3_), channel_id=1, source_target_pairs={{0,7},{1,0},{2,1},{3,2},{4,3},{5,4},{6,5},{7,6},{8,15},{9,8},{10,9... | collective-permute-start | bytes 1585160 | tf_op jit(solution)/shard_map/ppermute | solution.py:110
  85.5 0.0 collective-permute-done.10.refs_1_.refs_10_.refs_6_
  85.5 0.1 collective-permute-start.8
  85.6 0.0 collective-permute-done.15.refs_2_
  85.7 3.2 %collective-permute-start.9 = (bf16[1040,128]{1,0:T(8,128)(2,1)S(1)}, bf16[1040,128]{1,0:T(8,128)(2,1)S(1)}, u32[]{:S(2)}, u32[]{:S(2)}) collective-permute-start(bf16[1040,128]{1,0:T(8,128)(2,1)S(1)} %slice.19), channel_id=1, source_target_pairs={{0,7},{1,0},{2,1},{3,2},{4,3},{5,4},{6,5},{7,6},{8,15},{9,8},{10,9... | collective-permute-start | bytes 798728 | tf_op jit(solution)/shard_map/ppermute | solution.py:110
  88.9 0.1 collective-permute-start.3
  89.0 3.2 %collective-permute-start.7 = (bf16[1024,128]{1,0:T(8,128)(2,1)S(1)}, bf16[1024,128]{1,0:T(8,128)(2,1)S(1)}, u32[]{:S(2)}, u32[]{:S(2)}) collective-permute-start(bf16[1024,128]{1,0:T(8,128)(2,1)S(1)} %slice.17), channel_id=1, source_target_pairs={{0,7},{1,0},{2,1},{3,2},{4,3},{5,4},{6,5},{7,6},{8,15},{9,8},{10,9... | collective-permute-start | bytes 786440 | tf_op jit(solution)/shard_map/ppermute | solution.py:110
  92.2 0.1 pad_add_fusion.where_ref.refs_0_
  92.3 6.9 %shard_map.87.refs_13_ = f32[8,8,2,128,128]{4,3,2,1,0:T(8,128)S(1)} custom-call(s32[2]{0:T(128)S(1)} %pad_add_fusion.where_ref.refs_0_, bf16[2064,128]{1,0:T(8,128)(2,1)} %shard_map.82.refs_1_, bf16[2064,128]{1,0:T(8,128)(2,1)} %shard_map.83.refs_2_, bf16[2064,128]{1,0:T(8,128)(2,1)} %collective-permute-done.refs_3_, ...), custom_call_target="tpu_custom_call" | custom-call | tf_op jit(solution)/shard_map/pallas_call | solution.py:439
  99.2 0.7 shard_map.85.right_ref
  99.9 4.6 %shard_map.88.refs_9_ = f32[8,8,2,128,128]{4,3,2,1,0:T(8,128)S(1)} custom-call(s32[2]{0:T(128)S(1)} %pad_add_fusion.where_ref.refs_0_, bf16[2064,128]{1,0:T(8,128)(2,1)S(1)} %collective-permute-done.1.refs_1_, bf16[2064,128]{1,0:T(8,128)(2,1)S(1)} %collective-permute-done.14.refs_2_, ...), custom_call_target="tpu_custom_call", output_to_operand_aliasing={{}: (13, {})} | custom-call | tf_op jit(solution)/shard_map/pallas_call | solution.py:439
  104.6 4.4 %shard_map.89.total_ref = f32[8,8,2,128,128]{4,3,2,1,0:T(8,128)S(1)} custom-call(s32[2]{0:T(128)S(1)} %pad_add_fusion.where_ref.refs_0_, bf16[2064,128]{1,0:T(8,128)(2,1)S(1)} %collective-permute-done.2.refs_1_, bf16[2064,128]{1,0:T(8,128)(2,1)S(1)} %collective-permute-done.15.refs_2_, ...), custom_call_target="tpu_custom_call", output_to_operand_aliasing={{}: (9, {})} | custom-call | tf_op jit(solution)/shard_map/pallas_call | solution.py:439
  109.0 1.3 %shard_map.90.acc_ref = f32[8,8,2,128,128]{4,3,2,1,0:T(8,128)S(1)} custom-call(bf16[1040,128]{1,0:T(8,128)(2,1)S(1)} %collective-permute-done.8.up_ref.early_up_ref, bf16[1040,128]{1,0:T(8,128)(2,1)S(1)} %collective-permute-done.9.down_ref.early_down_ref, bf16[4112,128]{1,0:T(8,128)(2,1)S(1)} %shard_map.85.right_ref, ...), custom_call_target="tpu_custom_call", output_to_operand_aliasing={{}: (3, {})} | custom-call | tf_op jit(solution)/shard_map/pallas_call | solution.py:326
  110.2 2.1 %shard_map.91.old_ref = bf16[8,8,2,128,128]{4,3,2,1,0:T(8,128)(2,1)} custom-call(f32[8,8,2,128,128]{4,3,2,1,0:T(8,128)S(1)} %shard_map.90.acc_ref), custom_call_target="tpu_custom_call" | custom-call | tf_op jit(solution)/shard_map/pallas_call | solution.py:276
  112.3 2.2 %shard_map.92 = bf16[8,8,2,128,128]{4,3,2,1,0:T(8,128)(2,1)} custom-call(bf16[1024,128]{1,0:T(8,128)(2,1)S(1)} %collective-permute-done.3.up_ref, bf16[1024,128]{1,0:T(8,128)(2,1)S(1)} %collective-permute-done.7.down_ref, bf16[1040,128]{1,0:T(8,128)(2,1)S(1)} %collective-permute-done.8.up_ref.early_up_ref, ...), custom_call_target="tpu_custom_call", output_to_operand_aliasing={{}: (6, {})} | custom-call | tf_op jit(solution)/shard_map/pallas_call | solution.py:390
  (28 shorter events, 0.1 us)
Async XLA Ops:
  0.0 4.1 %copy-start.5 = (s32[1,8,2]{1,2,0:T(2,128)S(1)}, s32[1,8,2]{1,2,0:T(2,128)}, u32[]{:S(2)}) copy-start(s32[1,8,2]{1,2,0:T(2,128)} %param.9) | copy-start | bytes 196
  0.0 4.1 %copy-start.6 = (s32[1,8,2]{1,2,0:T(2,128)S(1)}, s32[1,8,2]{1,2,0:T(2,128)}, u32[]{:S(2)}) copy-start(s32[1,8,2]{1,2,0:T(2,128)} %param.11) | copy-start | bytes 196
  0.0 4.1 %copy-start.1 = (bf16[1,8,2,2,128,128]{5,4,3,2,1,0:T(8,128)(2,1)S(1)}, bf16[1,8,2,2,128,128]{5,4,3,2,1,0:T(8,128)(2,1)}, u32[]{:S(2)}) copy-start(bf16[1,8,2,2,128,128]{5,4,3,2,1,0:T(8,128)(2,1)} %param.8) | copy-start | bytes 3145732
  0.0 4.1 %copy-start.7 = (s32[1,8]{1,0:T(1,128)S(1)}, s32[1,8]{1,0:T(1,128)}, u32[]{:S(2)}) copy-start(s32[1,8]{1,0:T(1,128)} %count_hbm.3) | copy-start | bytes 100
  0.0 7.0 %copy-start = (bf16[2,8,1,2,2,128,128]{6,5,4,3,2,1,0:T(8,128)(2,1)S(1)}, bf16[2,8,1,2,2,128,128]{6,5,4,3,2,1,0:T(8,128)(2,1)}, u32[]{:S(2)}) copy-start(bf16[2,8,1,2,2,128,128]{6,5,4,3,2,1,0:T(8,128)(2,1)} %param.12) | copy-start | bytes 6291460
  2.1 4.9 %copy-start.2 = (s32[2,8,1,2]{1,3,2,0:T(2,128)S(1)}, s32[2,8,1,2]{1,3,2,0:T(2,128)}, u32[]{:S(2)}) copy-start(s32[2,8,1,2]{1,3,2,0:T(2,128)} %param.13) | copy-start | bytes 388
  2.1 4.9 %copy-start.3 = (s32[2,8,1,2]{1,3,2,0:T(2,128)S(1)}, s32[2,8,1,2]{1,3,2,0:T(2,128)}, u32[]{:S(2)}) copy-start(s32[2,8,1,2]{1,3,2,0:T(2,128)} %param.15) | copy-start | bytes 388
  2.1 4.9 %copy-start.4 = (s32[2,8,1]{1,2,0:T(1,128)S(1)}, s32[2,8,1]{1,2,0:T(1,128)}, u32[]{:S(2)}) copy-start(s32[2,8,1]{1,2,0:T(1,128)} %param.14) | copy-start | bytes 196
  2.1 19.1 %collective-permute-start = (bf16[2064,128]{1,0:T(8,128)(2,1)}, bf16[2064,128]{1,0:T(8,128)(2,1)}, u32[]{:S(2)}, u32[]{:S(2)}) collective-permute-start(bf16[2064,128]{1,0:T(8,128)(2,1)} %shard_map.82.refs_1_), channel_id=1, source_target_pairs={{0,1},{1,2},{2,3},{3,4},{4,5},{5,6},{6,7},{7,0},{8,9},{9,10},{10,1... | collective-permute-start | bytes 1585160 | tf_op jit(solution)/shard_map/ppermute | solution.py:110
  5.0 26.7 %collective-permute-start.13 = (bf16[2064,128]{1,0:T(8,128)(2,1)}, bf16[2064,128]{1,0:T(8,128)(2,1)}, u32[]{:S(2)}, u32[]{:S(2)}) collective-permute-start(bf16[2064,128]{1,0:T(8,128)(2,1)} %shard_map.83.refs_2_), channel_id=1, source_target_pairs={{0,1},{1,2},{2,3},{3,4},{4,5},{5,6},{6,7},{7,0},{8,9},{9,10},{10,1... | collective-permute-start | bytes 1585160 | tf_op jit(solution)/shard_map/ppermute | solution.py:110
  7.1 37.9 %collective-permute-start.20 = (bf16[4112,128]{1,0:T(8,128)(2,1)S(1)}, bf16[4112,128]{1,0:T(8,128)(2,1)}, u32[]{:S(2)}, u32[]{:S(2)}) collective-permute-start(bf16[4112,128]{1,0:T(8,128)(2,1)S(1)} %shard_map.86.refs_7_.refs_5_), channel_id=1, source_target_pairs={{0,16},{8,24},{16,0},{24,8},{1,17},{9,25},{17,1},{25,9},{2,18},{10... | collective-permute-start | bytes 3158024 | tf_op jit(solution)/shard_map/ppermute | solution.py:115
  8.4 39.9 %collective-permute-start.19 = (bf16[4112,128]{1,0:T(8,128)(2,1)S(1)}, bf16[4112,128]{1,0:T(8,128)(2,1)}, u32[]{:S(2)}, u32[]{:S(2)}) collective-permute-start(bf16[4112,128]{1,0:T(8,128)(2,1)S(1)} %shard_map.86.refs_7_.refs_5_), channel_id=1, source_target_pairs={{0,8},{8,0},{16,24},{24,16},{1,9},{9,1},{17,25},{25,17},{2,10},{10... | collective-permute-start | bytes 3158024 | tf_op jit(solution)/shard_map/ppermute | solution.py:115
  8.4 25.0 %collective-permute-start.16 = (bf16[2064,128]{1,0:T(8,128)(2,1)}, bf16[2064,128]{1,0:T(8,128)(2,1)}, u32[]{:S(2)}, u32[]{:S(2)}) collective-permute-start(bf16[2064,128]{1,0:T(8,128)(2,1)} %shard_map.82.refs_1_), channel_id=1, source_target_pairs={{0,7},{1,0},{2,1},{3,2},{4,3},{5,4},{6,5},{7,6},{8,15},{9,8},{10,9... | collective-permute-start | bytes 1585160 | tf_op jit(solution)/shard_map/ppermute | solution.py:110
  21.2 33.0 %collective-permute-start.11 = (bf16[4112,128]{1,0:T(8,128)(2,1)S(1)}, bf16[4112,128]{1,0:T(8,128)(2,1)S(1)}, u32[]{:S(2)}, u32[]{:S(2)}) collective-permute-start(bf16[4112,128]{1,0:T(8,128)(2,1)S(1)} %shard_map.84.refs_0_.refs_9_.refs_5_), channel_id=1, source_target_pairs={{0,16},{8,24},{16,0},{24,8},{1,17},{9,25},{17,1},{25,9},{2,18},{10... | collective-permute-start | bytes 3158024 | tf_op jit(solution)/shard_map/ppermute | solution.py:115
  31.7 13.4 %collective-permute-start.4 = (bf16[2064,128]{1,0:T(8,128)(2,1)}, bf16[2064,128]{1,0:T(8,128)(2,1)S(1)}, u32[]{:S(2)}, u32[]{:S(2)}) collective-permute-start(bf16[2064,128]{1,0:T(8,128)(2,1)} %shard_map.83.refs_2_), channel_id=1, source_target_pairs={{0,7},{1,0},{2,1},{3,2},{4,3},{5,4},{6,5},{7,6},{8,15},{9,8},{10,9... | collective-permute-start | bytes 1585160 | tf_op jit(solution)/shard_map/ppermute | solution.py:110
  33.4 16.4 %collective-permute-start.1 = (bf16[2064,128]{1,0:T(8,128)(2,1)}, bf16[2064,128]{1,0:T(8,128)(2,1)S(1)}, u32[]{:S(2)}, u32[]{:S(2)}) collective-permute-start(bf16[2064,128]{1,0:T(8,128)(2,1)} %collective-permute-done.refs_3_), channel_id=1, source_target_pairs={{0,1},{1,2},{2,3},{3,4},{4,5},{5,6},{6,7},{7,0},{8,9},{9,10},{10,1... | collective-permute-start | bytes 1585160 | tf_op jit(solution)/shard_map/ppermute | solution.py:110
  45.1 16.3 %collective-permute-start.14 = (bf16[2064,128]{1,0:T(8,128)(2,1)}, bf16[2064,128]{1,0:T(8,128)(2,1)S(1)}, u32[]{:S(2)}, u32[]{:S(2)}) collective-permute-start(bf16[2064,128]{1,0:T(8,128)(2,1)} %collective-permute-done.13.refs_4_), channel_id=1, source_target_pairs={{0,1},{1,2},{2,3},{3,4},{4,5},{5,6},{6,7},{7,0},{8,9},{9,10},{10,1... | collective-permute-start | bytes 1585160 | tf_op jit(solution)/shard_map/ppermute | solution.py:110
  45.1 16.3 %collective-permute-start.17 = (bf16[2064,128]{1,0:T(8,128)(2,1)}, bf16[2064,128]{1,0:T(8,128)(2,1)S(1)}, u32[]{:S(2)}, u32[]{:S(2)}) collective-permute-start(bf16[2064,128]{1,0:T(8,128)(2,1)} %collective-permute-done.16.refs_5_), channel_id=1, source_target_pairs={{0,7},{1,0},{2,1},{3,2},{4,3},{5,4},{6,5},{7,6},{8,15},{9,8},{10,9... | collective-permute-start | bytes 1585160 | tf_op jit(solution)/shard_map/ppermute | solution.py:110
  48.3 21.1 %collective-permute-start.5 = (bf16[2064,128]{1,0:T(8,128)(2,1)S(1)}, bf16[2064,128]{1,0:T(8,128)(2,1)S(1)}, u32[]{:S(2)}, u32[]{:S(2)}) collective-permute-start(bf16[2064,128]{1,0:T(8,128)(2,1)S(1)} %collective-permute-done.4.refs_6_), channel_id=1, source_target_pairs={{0,7},{1,0},{2,1},{3,2},{4,3},{5,4},{6,5},{7,6},{8,15},{9,8},{10,9... | collective-permute-start | bytes 1585160 | tf_op jit(solution)/shard_map/ppermute | solution.py:110
  49.8 23.3 %collective-permute-start.2 = (bf16[2064,128]{1,0:T(8,128)(2,1)S(1)}, bf16[2064,128]{1,0:T(8,128)(2,1)S(1)}, u32[]{:S(2)}, u32[]{:S(2)}) collective-permute-start(bf16[2064,128]{1,0:T(8,128)(2,1)S(1)} %collective-permute-done.1.refs_1_), channel_id=1, source_target_pairs={{0,1},{1,2},{2,3},{3,4},{4,5},{5,6},{6,7},{7,0},{8,9},{9,10},{10,1... | collective-permute-start | bytes 1585160 | tf_op jit(solution)/shard_map/ppermute | solution.py:110
  54.2 31.3 %collective-permute-start.10 = (bf16[4112,128]{1,0:T(8,128)(2,1)S(1)}, bf16[4112,128]{1,0:T(8,128)(2,1)S(1)}, u32[]{:S(2)}, u32[]{:S(2)}) collective-permute-start(bf16[4112,128]{1,0:T(8,128)(2,1)S(1)} %shard_map.84.refs_0_.refs_9_.refs_5_), channel_id=1, source_target_pairs={{0,8},{8,0},{16,24},{24,16},{1,9},{9,1},{17,25},{25,17},{2,10},{10... | collective-permute-start | bytes 3158024 | tf_op jit(solution)/shard_map/ppermute | solution.py:115
  61.4 27.5 %collective-permute-start.21 = (bf16[4112,128]{1,0:T(8,128)(2,1)}, bf16[4112,128]{1,0:T(8,128)(2,1)S(1)}, u32[]{:S(2)}, u32[]{:S(2)}) collective-permute-start(bf16[4112,128]{1,0:T(8,128)(2,1)} %collective-permute-done.20.refs_9_.refs_7_), channel_id=1, source_target_pairs={{0,8},{8,0},{16,24},{24,16},{1,9},{9,1},{17,25},{25,17},{2,10},{10... | collective-permute-start | bytes 3158024 | tf_op jit(solution)/shard_map/ppermute | solution.py:115
  61.4 27.6 %collective-permute-start.12 = (bf16[4112,128]{1,0:T(8,128)(2,1)S(1)}, bf16[4112,128]{1,0:T(8,128)(2,1)S(1)}, u32[]{:S(2)}, u32[]{:S(2)}) collective-permute-start(bf16[4112,128]{1,0:T(8,128)(2,1)S(1)} %collective-permute-done.11.refs_2_.refs_11_.refs_7_), channel_id=1, source_target_pairs={{0,8},{8,0},{16,24},{24,16},{1,9},{9,1},{17,25},{25,17},{2,10},{10... | collective-permute-start | bytes 3158024 | tf_op jit(solution)/shard_map/ppermute | solution.py:115
  69.4 12.4 %collective-permute-start.6 = (bf16[2064,128]{1,0:T(8,128)(2,1)S(1)}, bf16[2064,128]{1,0:T(8,128)(2,1)S(1)}, u32[]{:S(2)}, u32[]{:S(2)}) collective-permute-start(bf16[2064,128]{1,0:T(8,128)(2,1)S(1)} %collective-permute-done.5.refs_4_), channel_id=1, source_target_pairs={{0,7},{1,0},{2,1},{3,2},{4,3},{5,4},{6,5},{7,6},{8,15},{9,8},{10,9... | collective-permute-start | bytes 1585160 | tf_op jit(solution)/shard_map/ppermute | solution.py:110
  73.1 12.5 %collective-permute-start.15 = (bf16[2064,128]{1,0:T(8,128)(2,1)S(1)}, bf16[2064,128]{1,0:T(8,128)(2,1)S(1)}, u32[]{:S(2)}, u32[]{:S(2)}) collective-permute-start(bf16[2064,128]{1,0:T(8,128)(2,1)S(1)} %collective-permute-done.14.refs_2_), channel_id=1, source_target_pairs={{0,1},{1,2},{2,3},{3,4},{4,5},{5,6},{6,7},{7,0},{8,9},{9,10},{10,1... | collective-permute-start | bytes 1585160 | tf_op jit(solution)/shard_map/ppermute | solution.py:110
  81.8 22.8 %collective-permute-start.18 = (bf16[2064,128]{1,0:T(8,128)(2,1)S(1)}, bf16[2064,128]{1,0:T(8,128)(2,1)S(1)}, u32[]{:S(2)}, u32[]{:S(2)}) collective-permute-start(bf16[2064,128]{1,0:T(8,128)(2,1)S(1)} %collective-permute-done.17.refs_3_), channel_id=1, source_target_pairs={{0,7},{1,0},{2,1},{3,2},{4,3},{5,4},{6,5},{7,6},{8,15},{9,8},{10,9... | collective-permute-start | bytes 1585160 | tf_op jit(solution)/shard_map/ppermute | solution.py:110
  85.5 23.4 %collective-permute-start.8 = (bf16[1040,128]{1,0:T(8,128)(2,1)S(1)}, bf16[1040,128]{1,0:T(8,128)(2,1)S(1)}, u32[]{:S(2)}, u32[]{:S(2)}) collective-permute-start(bf16[1040,128]{1,0:T(8,128)(2,1)S(1)} %slice.18), channel_id=1, source_target_pairs={{0,1},{1,2},{2,3},{3,4},{4,5},{5,6},{6,7},{7,0},{8,9},{9,10},{10,1... | collective-permute-start | bytes 798728 | tf_op jit(solution)/shard_map/ppermute | solution.py:110
  85.7 23.3 %collective-permute-start.9 = (bf16[1040,128]{1,0:T(8,128)(2,1)S(1)}, bf16[1040,128]{1,0:T(8,128)(2,1)S(1)}, u32[]{:S(2)}, u32[]{:S(2)}) collective-permute-start(bf16[1040,128]{1,0:T(8,128)(2,1)S(1)} %slice.19), channel_id=1, source_target_pairs={{0,7},{1,0},{2,1},{3,2},{4,3},{5,4},{6,5},{7,6},{8,15},{9,8},{10,9... | collective-permute-start | bytes 798728 | tf_op jit(solution)/shard_map/ppermute | solution.py:110
  88.9 23.4 %collective-permute-start.3 = (bf16[1024,128]{1,0:T(8,128)(2,1)S(1)}, bf16[1024,128]{1,0:T(8,128)(2,1)S(1)}, u32[]{:S(2)}, u32[]{:S(2)}) collective-permute-start(bf16[1024,128]{1,0:T(8,128)(2,1)S(1)} %slice.16), channel_id=1, source_target_pairs={{0,1},{1,2},{2,3},{3,4},{4,5},{5,6},{6,7},{7,0},{8,9},{9,10},{10,1... | collective-permute-start | bytes 786440 | tf_op jit(solution)/shard_map/ppermute | solution.py:110
  89.0 23.3 %collective-permute-start.7 = (bf16[1024,128]{1,0:T(8,128)(2,1)S(1)}, bf16[1024,128]{1,0:T(8,128)(2,1)S(1)}, u32[]{:S(2)}, u32[]{:S(2)}) collective-permute-start(bf16[1024,128]{1,0:T(8,128)(2,1)S(1)} %slice.17), channel_id=1, source_target_pairs={{0,7},{1,0},{2,1},{3,2},{4,3},{5,4},{6,5},{7,6},{8,15},{9,8},{10,9... | collective-permute-start | bytes 786440 | tf_op jit(solution)/shard_map/ppermute | solution.py:110
